TPU v7x, 32 devices: a whole 2x2x4 slice. The times are simulated.
32 devices in a mesh: groups: 2 (over y), seq: 4 (over z), head: 2 (over x), loader: 2 (over core).
Axes of the slice: x: 2, y: 2, z: 4, core: 2. Of those that a mesh axis runs over, the one named last changes fastest.
Arguments:
- queries: bfloat16 [20480, 512], P(('groups', 'seq', 'loader'), 'head'), parts along dimension 0, may hold values from -6 to 6
- key_rows: bfloat16 [20480, 512], P(('groups', 'seq', 'loader'), 'head'), parts along dimension 0, may hold values from -6 to 6
- values: bfloat16 [20480, 512], P(('groups', 'seq', 'loader'), 'head'), parts along dimension 0, may hold values from -6 to 6
- cotangent: bfloat16 [20480, 512], P(('groups', 'seq', 'loader'), 'head'), parts along dimension 0, may hold values from -6 to 6
- out_gain: float32 [512], P('head'), may hold values from 0.1 to 1.9
- counts: int32 [16], P(('groups', 'seq', 'loader')), parts along dimension 0, may hold values from 1 to 5, as said below
Outputs:
- grad_query: bfloat16 [20480, 512], P(('groups', 'seq', 'loader'), 'head'), parts along dimension 0
- grad_key: bfloat16 [20480, 512], P(('groups', 'seq', 'loader'), 'head'), parts along dimension 0
- grad_value: bfloat16 [20480, 512], P(('groups', 'seq', 'loader'), 'head'), parts along dimension 0
There are 2 independent parts, one for each index of `groups`. A program takes and returns all parts, laid end to end along the dimension named above; an argument that names none is the same for every part. Nothing has to cross between parts.
Inputs may be any that keep to these rules, and one draw needn't show every extreme that they name: `counts`: for each seq index the buffers of its two loader indices hold 6 live blocks together.
All inputs are finite; a program needn't handle non-finite values.
Results may differ from a plain program's by a relative error of at most 0.0059.
Values may be sent and summed in bfloat16 or wider, within the bound.
No kernel may reach another device: no remote copies, remote signals or barrier semaphores. Data moves between devices by JAX's collectives and lax.ppermute only.
A program may use at most 64 MiB of HBM per device.

v0:
```python
import jax
import jax.numpy as jnp
from jax import lax
from jax.sharding import PartitionSpec as P

DH = 128
SPAN = 256


epsilon = 1e-06


def prefix_2(part, axis, combine, identity, reverse):
    count = lax.axis_size(axis)
    place = lax.axis_index(axis)
    ahead = count - 1 - place if reverse else place
    gathered = lax.all_gather(part, axis)
    state = jnp.zeros_like(part) + jnp.asarray(identity, part.dtype)

    def one(hop, state):
        source = count - 1 - hop if reverse else hop
        return combine(state, lax.dynamic_index_in_dim(gathered, source, 0, False))

    return lax.fori_loop(0, ahead, one, state)


def add_states(earlier, later):
    return earlier + later


def forward_chain(device_total):
    zero_state = jnp.zeros_like(device_total)
    return prefix_2(device_total, ("seq", "loader"), add_states, zero_state, False)


def backward_chain(device_total):
    zero_state = jnp.zeros_like(device_total)
    return prefix_2(device_total, ("seq", "loader"), add_states, zero_state, True)


def attention_core(queries, key_rows, values, cotangent, gain_rows):
    length = queries.shape[1]
    row_ids = lax.broadcasted_iota(jnp.int32, (length, length), 0)
    col_ids = lax.broadcasted_iota(jnp.int32, (length, length), 1)
    visible = (row_ids >= col_ids)[None, None]
    states = jnp.einsum("bchd,bche->bhde", key_rows, values, preferred_element_type=jnp.float32)
    incoming = forward_chain(jnp.sum(states, axis=0))
    zero_state = jnp.zeros((1,) + states.shape[1:], jnp.float32)
    running = jnp.concatenate([zero_state, jnp.cumsum(states[:-1], axis=0)], axis=0)
    prefix = (incoming[None] + running).astype(jnp.bfloat16)
    scores = jnp.einsum("bchd,bshd->bhcs", queries, key_rows, preferred_element_type=jnp.float32)
    scored = jnp.where(visible, scores, jnp.zeros((), jnp.float32)).astype(jnp.bfloat16)
    raw_out = jnp.einsum("bchd,bhde->bche", queries, prefix, preferred_element_type=jnp.float32)
    raw_out = raw_out + jnp.einsum(
        "bhcs,bshe->bche", scored, values, preferred_element_type=jnp.float32
    )
    inverse_rms = lax.rsqrt(jnp.mean(raw_out * raw_out, axis=-1, keepdims=True) + epsilon)
    weighted = gain_rows * cotangent.astype(jnp.float32)
    grad_raw = inverse_rms * weighted - raw_out * inverse_rms**3 * jnp.mean(
        weighted * raw_out, axis=-1, keepdims=True
    )
    grad_raw = grad_raw.astype(jnp.bfloat16)
    back_states = jnp.einsum(
        "bchd,bche->bhde", queries, grad_raw, preferred_element_type=jnp.float32
    )
    outgoing = backward_chain(jnp.sum(back_states, axis=0))
    later_sum = jnp.flip(jnp.cumsum(jnp.flip(back_states[1:], 0), axis=0), 0)
    later_sum = jnp.concatenate([later_sum, zero_state], axis=0)
    suffix = (outgoing[None] + later_sum).astype(jnp.bfloat16)
    pulled = jnp.einsum("bche,bshe->bhcs", grad_raw, values, preferred_element_type=jnp.float32)
    pull_scores = jnp.where(visible, pulled, jnp.zeros((), jnp.float32)).astype(jnp.bfloat16)
    grad_query = jnp.einsum("bche,bhde->bchd", grad_raw, prefix, preferred_element_type=jnp.float32)
    grad_query = grad_query + jnp.einsum(
        "bhcs,bshd->bchd", pull_scores, key_rows, preferred_element_type=jnp.float32
    )
    grad_key = jnp.einsum("bshe,bhde->bshd", values, suffix, preferred_element_type=jnp.float32)
    grad_key = grad_key + jnp.einsum(
        "bhcs,bchd->bshd", pull_scores, queries, preferred_element_type=jnp.float32
    )
    grad_value = jnp.einsum("bshd,bhde->bshe", key_rows, suffix, preferred_element_type=jnp.float32)
    grad_value = grad_value + jnp.einsum(
        "bhcs,bche->bshe", scored, grad_raw, preferred_element_type=jnp.float32
    )
    return (
        grad_query.astype(jnp.bfloat16),
        grad_key.astype(jnp.bfloat16),
        grad_value.astype(jnp.bfloat16),
    )


def shards(queries, key_rows, values, cotangent, out_gain, counts):
    blocks = queries.shape[0] // SPAN
    head_count = out_gain.shape[0] // DH
    own_count = counts[0]
    gain_rows = out_gain.reshape(head_count, DH)
    own_blocks = jnp.arange(blocks, dtype=jnp.int32)
    live_mask = (own_blocks < own_count)[:, None, None, None]

    def shaped(array):
        blocked = array.reshape(blocks, SPAN, head_count, DH)
        return jnp.where(live_mask, blocked, jnp.zeros((), jnp.bfloat16))

    grad_query, grad_key, grad_value = attention_core(
        shaped(queries), shaped(key_rows), shaped(values), shaped(cotangent), gain_rows
    )
    return (
        grad_query.reshape(queries.shape),
        grad_key.reshape(queries.shape),
        grad_value.reshape(queries.shape),
    )


def solution(mesh):
    return jax.shard_map(
        shards,
        mesh=mesh,
        in_specs=(
            P(("groups", "seq", "loader"), "head"),
            P(("groups", "seq", "loader"), "head"),
            P(("groups", "seq", "loader"), "head"),
            P(("groups", "seq", "loader"), "head"),
            P("head"),
            P(("groups", "seq", "loader")),
        ),
        out_specs=(
            P(("groups", "seq", "loader"), "head"),
            P(("groups", "seq", "loader"), "head"),
            P(("groups", "seq", "loader"), "head"),
        ),
        check_vma=False,
    )
```

profile of v0, /device:TPU:0, one launch (start us, length us, event | category | flops | bytes accessed | tf_op | source)
XLA Modules:
  0.0 97.2 jit_solution(4006877925537953717)
XLA Ops:
  7.9 1.9 %reshape.59 = bf16[5,256,2,128]{3,2,1,0:T(2,128)(2,1)S(1)} reshape(bf16[1280,256]{1,0:T(8,128)(2,1)} %param.11) | data formatting | bytes 1310720 | tf_op jit(solution)/shard_map/reshape | solution.py:100
  9.8 1.0 %copy.40 = bf16[5,256,2,128]{1,3,2,0:T(8,128)(2,1)S(1)} copy(bf16[5,256,2,128]{3,2,1,0:T(2,128)(2,1)S(1)} %reshape.59) | data formatting | bytes 1310720 | tf_op jit(solution)/shard_map/reshape | solution.py:100
  11.0 1.0 %copy.41 = bf16[5,256,2,128]{1,3,2,0:T(8,128)(2,1)S(1)} copy(bf16[5,256,2,128]{3,2,1,0:T(2,128)(2,1)S(1)} %reshape.60) | data formatting | bytes 1310720 | tf_op jit(solution)/shard_map/reshape | solution.py:100
  12.0 1.9 %fusion.19 = (f32[2,128,128]{2,1,0:T(8,128)}, f32[5,2,128,128]{3,2,1,0:T(8,128)}) fusion(bf16[5,256,2,128]{1,3,2,0:T(8,128)(2,1)S(1)} %copy.41, pred[5]{0:T(512)(128)(4,1)S(1)} %iota_compare_fusion.1, bf16[5,256,2,128]{1,3,2,0:T(8,128)(2,1)S(1)} %copy.40), kind=kOutput, calls=%fused_computation.45 | convolution fusion | flops 84672512 | bytes 2097157 | tf_op jit(solution)/shard_map/bchd,bche->bhde/dot_general | solution.py:46
  14.2 1.0 %copy.43 = bf16[5,256,2,128]{1,3,2,0:T(8,128)(2,1)S(1)} copy(bf16[5,256,2,128]{3,2,1,0:T(2,128)(2,1)S(1)} %reshape.61) | data formatting | bytes 1310720 | tf_op jit(solution)/shard_map/reshape | solution.py:100
  15.4 1.0 %copy.48 = bf16[5,256,2,128]{1,3,2,0:T(8,128)(2,1)S(1)} copy(bf16[5,256,2,128]{3,2,1,0:T(2,128)(2,1)S(1)} %reshape.62) | data formatting | bytes 1310720 | tf_op jit(solution)/shard_map/reshape | solution.py:100
  16.4 1.1 %fusion.7 = f32[4,2,128,128]{3,2,1,0:T(8,128)S(1)} fusion(f32[5,2,128,128]{3,2,1,0:T(8,128)} %get-tuple-element.105), kind=kOutput, calls=%fused_computation.28 | output fusion | flops 393216 | bytes 1048576 | tf_op jit(solution)/shard_map/jit(cumsum)/reduce_window_sum | solution.py:49
  17.5 1.7 %select_convert_fusion.1 = bf16[5,2,256,256]{3,2,1,0:T(8,128)(2,1)} fusion(pred[256,256]{1,0:T(8,128)(4,1)S(1)} %iota_compare_fusion, bf16[5,256,2,128]{1,3,2,0:T(8,128)(2,1)S(1)} %copy.40, pred[5]{0:T(512)(128)(4,1)S(1)} %iota_compare_fusion.1, bf16[5,256,2,128]{1,3,2,0:T(8,128)(2,1)S(1)} %copy.43), kind=kOutput, calls=%fused_computation.3 | convolution fusion | flops 169738240 | bytes 2686981 | tf_op jit(solution)/shard_map/bchd,bshd->bhcs/dot_general | solution.py:51
  19.2 19.7 %all-gather.5.cloned.1.call-done = f32[16,128,128]{2,1,0:T(8,128)} async-done(((f32[2,128,128]{2,1,0:T(8,128)}), f32[16,128,128]{2,1,0:T(8,128)}) %all-gather.5.cloned.1.call-update) | async-done | bytes 1048592 | tf_op jit(solution)/shard_map/all_gather | solution.py:17
  41.4 1.0 %fusion.20 = (f32[2,128,128]{2,1,0:T(8,128)}, f32[5,2,128,128]{3,2,1,0:T(8,128)S(1)}) fusion(bf16[5,256,2,128]{1,3,2,0:T(8,128)(2,1)S(1)} %subtract_convert_fusion, bf16[5,256,2,128]{1,3,2,0:T(8,128)(2,1)S(1)} %copy.43, pred[5]{0:T(512)(128)(4,1)S(1)} %iota_compare_fusion.1), kind=kOutput, calls=%fused_computation.46 | convolution fusion | flops 84344832 | bytes 2097157 | tf_op jit(solution)/shard_map/bchd,bche->bhde/dot_general | solution.py:63
  43.3 1.9 %rev.7 = f32[4,2,128,128]{3,2,1,0:T(8,128)} reverse(f32[4,2,128,128]{3,2,1,0:T(8,128)} %slice.9), dimensions={0} | reverse | bytes 1048576 | tf_op jit(solution)/shard_map/jit(_flip)/rev | solution.py:67
  45.2 1.9 %fusion.21 = f32[4,2,128,128]{3,2,1,0:T(8,128)} fusion(f32[4,2,128,128]{3,2,1,0:T(8,128)} %rev.7), kind=kOutput, calls=%fused_computation.47 | output fusion | flops 393216 | bytes 1048576 | tf_op jit(solution)/shard_map/jit(cumsum)/reduce_window_sum | solution.py:67
  47.1 1.9 %rev.8 = f32[4,2,128,128]{3,2,1,0:T(8,128)} reverse(f32[4,2,128,128]{3,2,1,0:T(8,128)} %fusion.21), dimensions={0} | reverse | bytes 1048576 | tf_op jit(solution)/shard_map/jit(_flip)/rev | solution.py:67
  49.9 1.1 %copy-done = bf16[5,2,256,256]{3,2,1,0:T(8,128)(2,1)} copy-done((bf16[5,2,256,256]{3,2,1,0:T(8,128)(2,1)}, bf16[5,2,256,256]{3,2,1,0:T(8,128)(2,1)S(1)}, u32[]{:S(2)}) %copy-start) | copy-done | bytes 1310744
  51.0 1.4 %fusion.6 = bf16[5,256,2,128]{1,3,2,0:T(8,128)(2,1)} fusion(f32[5,2,128,256]{3,2,1,0:T(8,128)S(1)} %fusion.9, bf16[5,2,256,256]{3,2,1,0:T(8,128)(2,1)S(1)} %select_convert_fusion, bf16[5,256,2,128]{1,3,2,0:T(8,128)(2,1)S(1)} %copy.40, pred[5]{0:T(512)(128)(4,1)S(1)} %iota_compare_fusion.1), kind=kOutput, calls=%fused_computation.18 | convolution fusion | flops 168755200 | bytes 3932165 | tf_op jit(solution)/shard_map/bhcs,bshd->bchd/dot_general | solution.py:73
  52.4 2.4 %copy.52 = bf16[5,256,2,128]{3,2,1,0:T(2,128)(2,1)S(1)} copy(bf16[5,256,2,128]{1,3,2,0:T(8,128)(2,1)} %fusion.6) | data formatting | bytes 1310720 | tf_op jit(solution)/shard_map/convert_element_type | solution.py:85
  54.8 0.9 copy.79
  55.7 15.0 %all-gather.7.cloned.1.call-done = f32[16,128,128]{2,1,0:T(8,128)} async-done(((f32[2,128,128]{2,1,0:T(8,128)}), f32[16,128,128]{2,1,0:T(8,128)}) %all-gather.7.cloned.1.call-update) | async-done | bytes 1048592 | tf_op jit(solution)/shard_map/all_gather | solution.py:17
  70.8 6.8 %while.23 = (s32[]{:T(128)}, f32[2,128,128]{2,1,0:T(8,128)S(1)}, s32[]{:T(128)}, f32[8,2,128,128]{3,2,1,0:T(8,128)}, s32[]{:T(128)}, /*index=5*/s32[]{:T(128)}, s32[]{:T(128)}, s32[]{:T(128)}) while((s32[]{:T(128)}, f32[2,128,128]{2,1,0:T(8,128)S(1)}, s32[]{:T(128)}, f32[8,2,128,128]{3,2,1,0:T(8,128)}, s32[]{:T(128)}, /*index=5*/s32[]{:T(128)}, ...), condition=%wide.region_8.9_spmd, body=%wide.region_7.8_spmd.sunk | while | flops 32774 | bytes 393351 | solution.py:24
  70.8 0.9 bitcast_add_fusion.5
  71.8 0.9 bitcast_add_fusion.5
  72.7 0.9 bitcast_add_fusion.5
  73.7 0.9 bitcast_add_fusion.5
  74.7 0.9 bitcast_add_fusion.5
  75.6 0.9 bitcast_add_fusion.5
  76.6 0.9 bitcast_add_fusion.5
  78.0 1.4 %fusion.12 = f32[5,2,128,256]{3,2,1,0:T(8,128)} fusion(f32[4,2,128,128]{3,2,1,0:T(8,128)S(1)} %copy-done.7, f32[2,128,128]{2,1,0:T(8,128)S(1)} %get-tuple-element.83, bf16[5,256,2,128]{1,3,2,0:T(8,128)(2,1)S(1)} %copy.41, pred[5]{0:T(512)(128)(4,1)S(1)} %iota_compare_fusion.1), kind=kOutput, calls=%fused_computation.34 | convolution fusion | flops 84541440 | bytes 2621445 | tf_op jit(solution)/shard_map/bshe,bhde->bshd/dot_general | solution.py:76
  79.4 1.2 %fusion.4 = bf16[5,256,2,128]{1,3,2,0:T(8,128)(2,1)} fusion(f32[5,2,128,256]{3,2,1,0:T(8,128)S(1)} %fusion.11, bf16[5,256,2,128]{1,3,2,0:T(8,128)(2,1)S(1)} %subtract_convert_fusion, bf16[5,2,256,256]{3,2,1,0:T(8,128)(2,1)S(1)} %copy-done.4), kind=kOutput, calls=%fused_computation.16 | convolution fusion | flops 168427520 | bytes 3932160 | tf_op jit(solution)/shard_map/bhcs,bche->bshe/dot_general | solution.py:81
  80.6 3.1 %copy.58 = bf16[5,256,2,128]{3,2,1,0:T(2,128)(2,1)} copy(bf16[5,256,2,128]{1,3,2,0:T(8,128)(2,1)} %fusion.4) | data formatting | bytes 1310720 | tf_op jit(solution)/shard_map/convert_element_type | solution.py:87
  83.7 2.0 %copy.77 = bf16[160,8,2,128]{3,1,2,0:T(8,128)(2,1)} copy(bf16[160,8,2,128]{3,2,1,0:T(2,128)(2,1)} %bitcast.46) | data formatting | bytes 1310720
  85.7 1.2 %fusion.5 = bf16[5,256,2,128]{1,3,2,0:T(8,128)(2,1)} fusion(f32[5,2,128,256]{3,2,1,0:T(8,128)S(1)} %copy-done.2, bf16[5,2,256,256]{3,2,1,0:T(8,128)(2,1)S(1)} %copy-done.1, bf16[5,256,2,128]{1,3,2,0:T(8,128)(2,1)S(1)} %copy.43, pred[5]{0:T(512)(128)(4,1)S(1)} %iota_compare_fusion.1), kind=kOutput, calls=%fused_computation.17 | convolution fusion | flops 168755200 | bytes 3932165 | tf_op jit(solution)/shard_map/bhcs,bchd->bshd/dot_general | solution.py:77
  87.0 2.4 %copy.55 = bf16[5,256,2,128]{3,2,1,0:T(2,128)(2,1)S(1)} copy(bf16[5,256,2,128]{1,3,2,0:T(8,128)(2,1)} %fusion.5) | data formatting | bytes 1310720 | tf_op jit(solution)/shard_map/convert_element_type | solution.py:86
  (44 shorter events, 6.2 us)
Async XLA Ops:
  7.2 31.7 %all-gather.5.cloned.1.call-start = ((), (), s32[]{:S(2)}) async-start(), calls=%async_computation | async-start | bytes 1179648 | tf_op jit(solution)/shard_map/all_gather | solution.py:17
  7.9 3.0 %copy-start.8 = (bf16[1280,256]{1,0:T(8,128)(2,1)S(1)}, bf16[1280,256]{1,0:T(8,128)(2,1)}, u32[]{:S(2)}) copy-start(bf16[1280,256]{1,0:T(8,128)(2,1)} %param.12) | copy-start | bytes 1966084
  12.0 2.0 %copy-start.9 = (bf16[1280,256]{1,0:T(8,128)(2,1)S(1)}, bf16[1280,256]{1,0:T(8,128)(2,1)}, u32[]{:S(2)}) copy-start(bf16[1280,256]{1,0:T(8,128)(2,1)} %param.10) | copy-start | bytes 1966084
  14.0 56.8 %all-gather.7.cloned.1.call-start = ((), (), s32[]{:S(2)}) async-start(), calls=%async_computation.1 | async-start | bytes 1179648 | tf_op jit(solution)/shard_map/all_gather | solution.py:17
  14.0 1.2 %copy-start.10 = (bf16[1280,256]{1,0:T(8,128)(2,1)S(1)}, bf16[1280,256]{1,0:T(8,128)(2,1)}, u32[]{:S(2)}) copy-start(bf16[1280,256]{1,0:T(8,128)(2,1)} %param.13) | copy-start | bytes 1966084
  17.5 21.4 %copy-start.5 = (f32[4,2,128,128]{3,2,1,0:T(8,128)}, f32[4,2,128,128]{3,2,1,0:T(8,128)S(1)}, u32[]{:S(2)}) copy-start(f32[4,2,128,128]{3,2,1,0:T(8,128)S(1)} %fusion.7) | copy-start | bytes 1572868
  38.9 1.3 %copy-start.3 = (bf16[5,2,256,256]{3,2,1,0:T(8,128)(2,1)S(1)}, bf16[5,2,256,256]{3,2,1,0:T(8,128)(2,1)}, u32[]{:S(2)}) copy-start(bf16[5,2,256,256]{3,2,1,0:T(8,128)(2,1)} %select_convert_fusion.1) | copy-start | bytes 3932164
  39.0 1.3 %copy-start.11 = (f32[256]{0:T(256)S(1)}, f32[256]{0:T(256)}, u32[]{:S(2)}) copy-start(f32[256]{0:T(256)} %param.14) | copy-start | bytes 3076
  45.2 3.8 %copy-start.6 = (f32[4,2,128,128]{3,2,1,0:T(8,128)S(1)}, f32[4,2,128,128]{3,2,1,0:T(8,128)}, u32[]{:S(2)}) copy-start(f32[4,2,128,128]{3,2,1,0:T(8,128)} %copy-done.5) | copy-start | bytes 1572868
  49.9 1.1 %copy-start = (bf16[5,2,256,256]{3,2,1,0:T(8,128)(2,1)}, bf16[5,2,256,256]{3,2,1,0:T(8,128)(2,1)S(1)}, u32[]{:S(2)}) copy-start(bf16[5,2,256,256]{3,2,1,0:T(8,128)(2,1)S(1)} %select_convert_fusion) | copy-start | bytes 3932164
  55.7 21.8 %copy-start.7 = (f32[4,2,128,128]{3,2,1,0:T(8,128)S(1)}, f32[4,2,128,128]{3,2,1,0:T(8,128)}, u32[]{:S(2)}) copy-start(f32[4,2,128,128]{3,2,1,0:T(8,128)} %rev.8) | copy-start | bytes 1572868
  77.9 1.5 %copy-start.4 = (bf16[5,2,256,256]{3,2,1,0:T(8,128)(2,1)S(1)}, bf16[5,2,256,256]{3,2,1,0:T(8,128)(2,1)}, u32[]{:S(2)}) copy-start(bf16[5,2,256,256]{3,2,1,0:T(8,128)(2,1)} %select_convert_fusion.1) | copy-start | bytes 3932164
  80.6 5.1 %copy-start.1 = (bf16[5,2,256,256]{3,2,1,0:T(8,128)(2,1)S(1)}, bf16[5,2,256,256]{3,2,1,0:T(8,128)(2,1)}, u32[]{:S(2)}) copy-start(bf16[5,2,256,256]{3,2,1,0:T(8,128)(2,1)} %copy-done) | copy-start | bytes 3932164
  80.6 5.1 %copy-start.2 = (f32[5,2,128,256]{3,2,1,0:T(8,128)S(1)}, f32[5,2,128,256]{3,2,1,0:T(8,128)}, u32[]{:S(2)}) copy-start(f32[5,2,128,256]{3,2,1,0:T(8,128)} %fusion.12) | copy-start | bytes 3932164
Sparse Core Ops, SparseCore 0:
  14.1 24.7 all-gather.4
  42.6 28.1 all-gather.6
where the time goes:
time: 97.8 us; the launch traced here: 97.2 us
  waiting for transfers between devices  34.7 us (35%)
  local copies, waits for them, and re-layouts  24.8 us (25%)
  between operations  15 us (15%)
  matrix products  12.4 us (13%)
  other arithmetic  10 us (10%)
    all_gather x2, waiting for transfers between devices, prefix_2(): gathered = lax.all_gather(part, axis)  34.7 us
    add x7, other arithmetic, add_states(): return earlier + later  6.56 us
    reshape x8, local copies, waits for them, and re-layouts, shaped(): blocked = array.reshape(blocks, SPAN, head_count, DH)  6.38 us
    unnamed x27, local copies, waits for them, and re-layouts  5.87 us
    rev x2, local copies, waits for them, and re-layouts, attention_core(): later_sum = jnp.flip(jnp.cumsum(jnp.flip(back_states[1:], 0), axis=0), 0)  3.74 us
    convert_element_type x1, local copies, waits for them, and re-layouts, attention_core(): grad_value.astype(jnp.bfloat16)  3.1 us
    convert_element_type x1, local copies, waits for them, and re-layouts, attention_core(): grad_query.astype(jnp.bfloat16)  2.44 us
    convert_element_type x1, local copies, waits for them, and re-layouts, attention_core(): grad_key.astype(jnp.bfloat16)  2.44 us
  transfers between devices with their start and end apart: 2, of which 2 were waited for; matrix products, arithmetic and copies ran while one was open for 18% of the time, Pallas kernels for 0%

commit v1 on v0

v1 whole, which is shorter than its diff:
```python
import functools

import jax
import jax.numpy as jnp
from jax import lax
from jax.experimental import pallas as pl
from jax.experimental.pallas import tpu as pltpu
from jax.sharding import PartitionSpec as P

DH = 128
SPAN = 256
EPSILON = 1e-06
F32 = jnp.float32
BF16 = jnp.bfloat16
VMEM = pl.BlockSpec(memory_space=pltpu.VMEM)
SMEM = pl.BlockSpec(memory_space=pltpu.SMEM)


def nn(a, b):
    return lax.dot_general(a, b, (((1,), (0,)), ((), ())), preferred_element_type=F32)


def nt(a, b):
    return lax.dot_general(a, b, (((1,), (1,)), ((), ())), preferred_element_type=F32)


def tn(a, b):
    return lax.dot_general(a, b, (((0,), (0,)), ((), ())), preferred_element_type=F32)


def tiles(rows, width):
    for b in range(rows // SPAN):
        for h in range(width // DH):
            yield b, h, slice(b * SPAN, (b + 1) * SPAN), slice(h * DH, (h + 1) * DH)


def state_kernel(count_ref, k_ref, v_ref, run_ref, total_ref):
    running = {}
    for b, h, r, c in tiles(*k_ref.shape):
        state = tn(k_ref[r, c], v_ref[r, c])
        state = jnp.where(b < count_ref[0], state, jnp.zeros_like(state))
        if b == 0:
            run_ref[b, h] = jnp.zeros_like(state)
            running[h] = state
        else:
            run_ref[b, h] = running[h]
            running[h] = running[h] + state
    for h, state in running.items():
        total_ref[h] = state.astype(total_ref.dtype)


def score_kernel(q_ref, k_ref, v_ref, part_ref, turned_ref):
    t = lax.broadcasted_iota(jnp.int32, (SPAN, SPAN), 0)
    s = lax.broadcasted_iota(jnp.int32, (SPAN, SPAN), 1)
    for b, h, r, c in tiles(*q_ref.shape):
        q, k = q_ref[r, c], k_ref[r, c]
        scored = jnp.where(t >= s, nt(q, k), 0.0).astype(BF16)
        part_ref[r, c] = nn(scored, v_ref[r, c])
        turned_ref[b, h] = jnp.where(t <= s, nt(k, q), 0.0).astype(BF16)


def norm_kernel(count_ref, q_ref, cot_ref, gain_ref, part_ref, run_ref, near_ref, far_ref,
                grad_ref, prefix_ref, back_ref, total_ref):
    running = {}
    for b, h, r, c in reversed(list(tiles(*q_ref.shape))):
        prefix = (run_ref[b, h] + near_ref[h] + far_ref[h]).astype(BF16)
        prefix_ref[b, h] = prefix
        q = q_ref[r, c]
        raw = part_ref[r, c] + nn(q, prefix)
        inverse = lax.rsqrt(jnp.mean(raw * raw, axis=-1, keepdims=True) + EPSILON)
        gain = gain_ref[:, c]
        gain = jnp.where(b < count_ref[0], gain, jnp.zeros_like(gain))
        weighted = gain * cot_ref[r, c].astype(F32)
        pulled = jnp.mean(weighted * raw, axis=-1, keepdims=True)
        grad = (inverse * weighted - raw * (inverse * inverse * inverse * pulled)).astype(BF16)
        grad_ref[r, c] = grad
        state = tn(q, grad)
        back_ref[b, h] = running.get(h, jnp.zeros_like(state))
        running[h] = running[h] + state if h in running else state
    for h, state in running.items():
        total_ref[h] = state.astype(total_ref.dtype)


def pull_kernel(q_ref, k_ref, v_ref, grad_ref, turned_ref, prefix_ref, gq_ref, gk_ref, gv_ref):
    t = lax.broadcasted_iota(jnp.int32, (SPAN, SPAN), 0)
    s = lax.broadcasted_iota(jnp.int32, (SPAN, SPAN), 1)
    for b, h, r, c in tiles(*q_ref.shape):
        v, grad = v_ref[r, c], grad_ref[r, c]
        pull = jnp.where(t >= s, nt(grad, v), 0.0).astype(BF16)
        gq_ref[r, c] = (nn(pull, k_ref[r, c]) + nt(grad, prefix_ref[b, h])).astype(BF16)
        turned = jnp.where(t <= s, nt(v, grad), 0.0).astype(BF16)
        gk_ref[r, c] = nn(turned, q_ref[r, c])
        gv_ref[r, c] = nn(turned_ref[b, h], grad)


def final_kernel(count_ref, k_ref, v_ref, gk_part_ref, gv_part_ref, back_ref, near_ref, far_ref,
                 gk_ref, gv_ref):
    for b, h, r, c in tiles(*k_ref.shape):
        suffix = back_ref[b, h] + near_ref[h] + far_ref[h]
        suffix = jnp.where(b < count_ref[0], suffix, jnp.zeros_like(suffix)).astype(BF16)
        gk_ref[r, c] = (gk_part_ref[r, c] + nt(v_ref[r, c], suffix)).astype(BF16)
        gv_ref[r, c] = (gv_part_ref[r, c] + nn(k_ref[r, c], suffix)).astype(BF16)


def call(kernel, out_shape, flops, *args):
    specs = [SMEM if a.dtype == jnp.int32 else VMEM for a in args]
    size = sum(a.size * a.dtype.itemsize for a in args)
    size += sum(a.size * a.dtype.itemsize for a in out_shape)
    return pl.pallas_call(
        kernel,
        out_shape=out_shape,
        in_specs=specs,
        out_specs=[VMEM] * len(out_shape),
        cost_estimate=pl.CostEstimate(flops=flops, bytes_accessed=size, transcendentals=0),
        compiler_params=pltpu.CompilerParams(vmem_limit_bytes=32 * 2**20),
    )(*args)


def radices(count):
    found = []
    for radix in (4, 2):
        while count % radix == 0:
            found.append(radix)
            count //= radix
    return found + [count] if count > 1 else found


def chip_sums(total, reverse):
    count, place = lax.axis_size("seq"), lax.axis_index("seq")
    outside = jnp.zeros(total.shape, F32)
    group, stride = total, 1
    chain = radices(count)
    for at, radix in enumerate(chain):
        digit = place // stride % radix
        whole = group.astype(F32)
        for step in range(1, radix):
            def partner(d, step=step):
                return d ^ step if radix in (2, 4) else (d + step) % radix
            pairs = [(s, s + (partner(s // stride % radix) - s // stride % radix) * stride)
                     for s in range(count)]
            came = lax.ppermute(group, "seq", pairs).astype(F32)
            source = digit ^ step if radix in (2, 4) else (digit + radix - step) % radix
            use = source > digit if reverse else source < digit
            outside = outside + jnp.where(use, came, 0.0)
            whole = whole + came
        if at + 1 < len(chain):
            group = whole.astype(total.dtype)
        stride *= radix
    return outside


def outside_sum(total, reverse):
    near = chip_sums(total, reverse)
    core = lax.axis_index("loader")
    mine = core == (1 if reverse else 0)
    sent = near + jnp.where(mine, total.astype(F32), 0.0)
    far = lax.ppermute(sent, "loader", [(0, 1), (1, 0)])
    return near, far


def shards(queries, key_rows, values, cotangent, out_gain, counts):
    rows, width = queries.shape
    blocks, heads = rows // SPAN, width // DH
    unit = 2 * rows * width * DH
    like = jax.ShapeDtypeStruct
    states = like((blocks, heads, DH, DH), F32)
    total = like((heads, DH, DH), BF16)
    plane = like((rows, width), F32)
    half = like((rows, width), BF16)
    square = like((blocks, heads, SPAN, SPAN), BF16)
    gain_row = out_gain.reshape(1, width)

    run, own = call(state_kernel, [states, total], unit, counts, key_rows, values)
    near, far = outside_sum(own, False)
    part, turned = call(score_kernel, [plane, square], 6 * unit, queries, key_rows, values)
    grad, prefix, back, own_back = call(
        norm_kernel, [half, like(states.shape, BF16), states, total], 2 * unit,
        counts, queries, cotangent, gain_row, part, run, near, far)
    near, far = outside_sum(own_back, True)
    gq, gk_part, gv_part = call(
        pull_kernel, [half, plane, plane], 11 * unit,
        queries, key_rows, values, grad, turned, prefix)
    gk, gv = call(final_kernel, [half, half], 2 * unit,
                  counts, key_rows, values, gk_part, gv_part, back, near, far)
    return gq, gk, gv


def solution(mesh):
    rows = P(("groups", "seq", "loader"), "head")
    return jax.shard_map(
        shards,
        mesh=mesh,
        in_specs=(rows, rows, rows, rows, P("head"), P(("groups", "seq", "loader"))),
        out_specs=(rows, rows, rows),
        check_vma=False,
    )
```

time: 97.8 us -> 39.2 us (0.40)
  waiting for transfers between devices: 34.7 us -> 9.83 us
  local copies, waits for them, and re-layouts: 24.8 us -> 8.56 us
  between operations: 15 us -> 1.42 us
  matrix products: 12.4 us -> 0 us
  starting transfers between devices: 0.08 us -> 10.3 us
  other arithmetic: 10 us -> 0.1 us
  Pallas kernels: 0 us -> 8.7 us
    all_gather x2 -> x0, waiting for transfers between devices: 34.7 us -> none  [prefix_2(): gathered = lax.all_gather(part, axis)]
    dot_general x12 -> x0, matrix products: 12.4 us -> none  [the longest x1 1.92 us: attention_core(): jnp.einsum('bchd,bche->bhde', key_rows, values, preferred_element_type=jn...]
    ppermute x0 -> x8, starting transfers between devices: none -> 10.3 us  [the longest x6 10 us: chip_sums(): came = lax.ppermute(group, 'seq', pairs).astype(F32)]
    ppermute x0 -> x8, waiting for transfers between devices: none -> 9.83 us  [the longest x6 9.82 us: chip_sums(): came = lax.ppermute(group, 'seq', pairs).astype(F32)]
    pallas_call x0 -> x5, Pallas kernels: none -> 8.7 us  [call(): pl.pallas_call(kernel, out_shape=out_shape, in_specs=specs, out_specs=[VM...]
    convert_element_type x3 -> x0, local copies, waits for them, and re-layouts: 7.97 us -> none  [the longest x1 3.1 us: attention_core(): grad_value.astype(jnp.bfloat16)]
    add x7 -> x2, other arithmetic: 6.56 us -> 0.1 us  [outside_sum(): sent = near + jnp.where(mine, total.astype(F32), 0.0)]
    reshape x8 -> x0, local copies, waits for them, and re-layouts: 6.38 us -> none  [shaped(): blocked = array.reshape(blocks, SPAN, head_count, DH)]
  transfers between devices with their start and end apart: 2 -> 8, of which waited for: 2 -> 4; matrix products, arithmetic and copies ran while one was open for 18% -> 0% of each run, Pallas kernels for 0% -> 14%
where the time goes in v1:
time: 39.2 us; the launch traced here: 38.9 us
  starting transfers between devices  10.3 us (26%)
  waiting for transfers between devices  9.83 us (25%)
  Pallas kernels  8.7 us (22%)
  local copies, waits for them, and re-layouts  8.56 us (22%)
  between operations  1.42 us (4%)
    ppermute x6, starting transfers between devices, chip_sums(): came = lax.ppermute(group, 'seq', pairs).astype(F32)  10 us
    ppermute x6, waiting for transfers between devices, chip_sums(): came = lax.ppermute(group, 'seq', pairs).astype(F32)  9.82 us
    pallas_call x5, Pallas kernels, call(): pl.pallas_call(kernel, out_shape=out_shape, in_specs=specs, out_specs=[VM...  8.7 us
    unnamed x32, local copies, waits for them, and re-layouts  8.56 us
  transfers between devices with their start and end apart: 8, of which 4 were waited for; matrix products, arithmetic and copies ran while one was open for 0% of the time, Pallas kernels for 14%

profile of v1, /device:TPU:0, one launch (start us, length us, event | category | flops | bytes accessed | tf_op | source)
XLA Modules:
  0.0 38.9 jit_solution(18383038752820046515)
XLA Ops:
  1.3 1.1 %copy-done = bf16[1280,256]{1,0:T(8,128)(2,1)S(1)} copy-done((bf16[1280,256]{1,0:T(8,128)(2,1)S(1)}, bf16[1280,256]{1,0:T(8,128)(2,1)}, u32[]{:S(2)}) %copy-start) | copy-done | bytes 655384
  2.4 1.1 %copy-done.2 = bf16[1280,256]{1,0:T(8,128)(2,1)S(1)} copy-done((bf16[1280,256]{1,0:T(8,128)(2,1)S(1)}, bf16[1280,256]{1,0:T(8,128)(2,1)}, u32[]{:S(2)}) %copy-start.2) | copy-done | bytes 655384
  3.5 0.4 shard_map.86
  3.9 0.0 copy-start.9
  3.9 0.8 %copy-done.9 = f32[5,2,128,128]{3,2,1,0:T(8,128)} copy-done((f32[5,2,128,128]{3,2,1,0:T(8,128)}, f32[5,2,128,128]{3,2,1,0:T(8,128)S(1)}, u32[]{:S(2)}) %copy-start.9) | copy-done | bytes 655384
  4.7 5.0 %collective-permute-start.2 = (bf16[2,128,128]{2,1,0:T(8,128)(2,1)S(1)}, bf16[2,128,128]{2,1,0:T(8,128)(2,1)S(1)}, u32[]{:S(2)}, u32[]{:S(2)}) collective-permute-start(bf16[2,128,128]{2,1,0:T(8,128)(2,1)S(1)} %get-tuple-element.18), channel_id=1, source_target_pairs={{0,12},{4,8},{8,4},{12,0},{1,13},{5,9},{9,5},{13,1},{2,14},{6,10},... | collective-permute-start | bytes 196616 | tf_op jit(solution)/shard_map/ppermute | solution.py:141
  9.7 0.6 %collective-permute-start = (bf16[2,128,128]{2,1,0:T(8,128)(2,1)S(1)}, bf16[2,128,128]{2,1,0:T(8,128)(2,1)S(1)}, u32[]{:S(2)}, u32[]{:S(2)}) collective-permute-start(bf16[2,128,128]{2,1,0:T(8,128)(2,1)S(1)} %get-tuple-element.18), channel_id=1, source_target_pairs={{0,4},{4,0},{8,12},{12,8},{1,5},{5,1},{9,13},{13,9},{2,6},{6,2},{1... | collective-permute-start | bytes 196616 | tf_op jit(solution)/shard_map/ppermute | solution.py:141
  10.3 2.0 %collective-permute-done.2 = bf16[2,128,128]{2,1,0:T(8,128)(2,1)S(1)} collective-permute-done((bf16[2,128,128]{2,1,0:T(8,128)(2,1)S(1)}, bf16[2,128,128]{2,1,0:T(8,128)(2,1)S(1)}, u32[]{:S(2)}, u32[]{:S(2)}) %collective-permute-start.2) | collective-permute-done | bytes 65568 | tf_op jit(solution)/shard_map/ppermute | solution.py:141
  12.3 3.0 %collective-permute-done.1 = bf16[2,128,128]{2,1,0:T(8,128)(2,1)S(1)} collective-permute-done((bf16[2,128,128]{2,1,0:T(8,128)(2,1)S(1)}, bf16[2,128,128]{2,1,0:T(8,128)(2,1)S(1)}, u32[]{:S(2)}, u32[]{:S(2)}) %collective-permute-start.1) | collective-permute-done | bytes 65568 | tf_op jit(solution)/shard_map/ppermute | solution.py:141
  15.3 0.1 select_add_fusion.2
  15.4 0.1 collective-permute-start.3
  15.5 0.0 copy-start.4
  15.5 1.1 %copy-done.4 = bf16[1280,256]{1,0:T(8,128)(2,1)S(1)} copy-done((bf16[1280,256]{1,0:T(8,128)(2,1)S(1)}, bf16[1280,256]{1,0:T(8,128)(2,1)}, u32[]{:S(2)}) %copy-start.4) | copy-done | bytes 655384
  16.6 2.0 %shard_map.85 = (f32[1280,256]{1,0:T(8,128)S(1)}, bf16[5,2,256,256]{3,2,1,0:T(8,128)(2,1)S(1)}) custom-call(bf16[1280,256]{1,0:T(8,128)(2,1)S(1)} %copy-done.4, bf16[1280,256]{1,0:T(8,128)(2,1)S(1)} %copy-done.1, bf16[1280,256]{1,0:T(8,128)(2,1)S(1)} %copy-done.3), custom_call_target="tpu_custom_call" | custom-call | flops 503316480 | bytes 4587520 | tf_op jit(solution)/shard_map/pallas_call | solution.py:109
  18.6 0.0 collective-permute-done.3.far_ref
  18.6 0.0 copy-start.5
  18.6 1.3 %shard_map.87 = (bf16[1280,256]{1,0:T(8,128)(2,1)S(1)}, bf16[5,2,128,128]{3,2,1,0:T(8,128)(2,1)S(1)}, f32[5,2,128,128]{3,2,1,0:T(8,128)S(1)}, bf16[2,128,128]{2,1,0:T(8,128)(2,1)S(1)}) custom-call(s32[1]{0:T(128)S(6)} %copy.9.count_ref, bf16[1280,256]{1,0:T(8,128)(2,1)S(1)} %copy-done.4, bf16[1280,256]{1,0:T(8,128)(2,1)S(1)} %copy-done.8, ...), custom_call_target="tpu_custom_call" | custom-call | flops 167772160 | bytes 5243908 | tf_op jit(solution)/shard_map/pallas_call | solution.py:109
  19.9 0.0 copy-start.6
  19.9 0.8 %copy-done.6 = f32[5,2,128,128]{3,2,1,0:T(8,128)} copy-done((f32[5,2,128,128]{3,2,1,0:T(8,128)}, f32[5,2,128,128]{3,2,1,0:T(8,128)S(1)}, u32[]{:S(2)}) %copy-start.6) | copy-done | bytes 655384
  20.8 0.8 %copy-done.11 = bf16[1280,256]{1,0:T(8,128)(2,1)} copy-done((bf16[1280,256]{1,0:T(8,128)(2,1)}, bf16[1280,256]{1,0:T(8,128)(2,1)S(1)}, u32[]{:S(2)}) %copy-start.11) | copy-done | bytes 655384
  21.6 0.7 %copy-done.13 = bf16[5,2,128,128]{3,2,1,0:T(8,128)(2,1)} copy-done((bf16[5,2,128,128]{3,2,1,0:T(8,128)(2,1)}, bf16[5,2,128,128]{3,2,1,0:T(8,128)(2,1)S(1)}, u32[]{:S(2)}) %copy-start.13) | copy-done | bytes 327704
  22.3 2.6 %collective-permute-start.6 = (bf16[2,128,128]{2,1,0:T(8,128)(2,1)S(1)}, bf16[2,128,128]{2,1,0:T(8,128)(2,1)S(1)}, u32[]{:S(2)}, u32[]{:S(2)}) collective-permute-start(bf16[2,128,128]{2,1,0:T(8,128)(2,1)S(1)} %get-tuple-element.26), channel_id=1, source_target_pairs={{0,12},{4,8},{8,4},{12,0},{1,13},{5,9},{9,5},{13,1},{2,14},{6,10},... | collective-permute-start | bytes 196616 | tf_op jit(solution)/shard_map/ppermute | solution.py:141
  25.0 1.7 %collective-permute-start.4 = (bf16[2,128,128]{2,1,0:T(8,128)(2,1)S(1)}, bf16[2,128,128]{2,1,0:T(8,128)(2,1)S(1)}, u32[]{:S(2)}, u32[]{:S(2)}) collective-permute-start(bf16[2,128,128]{2,1,0:T(8,128)(2,1)S(1)} %get-tuple-element.26), channel_id=1, source_target_pairs={{0,4},{4,0},{8,12},{12,8},{1,5},{5,1},{9,13},{13,9},{2,6},{6,2},{1... | collective-permute-start | bytes 196616 | tf_op jit(solution)/shard_map/ppermute | solution.py:141
  26.7 2.4 %collective-permute-done.6 = bf16[2,128,128]{2,1,0:T(8,128)(2,1)S(1)} collective-permute-done((bf16[2,128,128]{2,1,0:T(8,128)(2,1)S(1)}, bf16[2,128,128]{2,1,0:T(8,128)(2,1)S(1)}, u32[]{:S(2)}, u32[]{:S(2)}) %collective-permute-start.6) | collective-permute-done | bytes 65568 | tf_op jit(solution)/shard_map/ppermute | solution.py:141
  29.1 2.4 %collective-permute-done.5 = bf16[2,128,128]{2,1,0:T(8,128)(2,1)S(1)} collective-permute-done((bf16[2,128,128]{2,1,0:T(8,128)(2,1)S(1)}, bf16[2,128,128]{2,1,0:T(8,128)(2,1)S(1)}, u32[]{:S(2)}, u32[]{:S(2)}) %collective-permute-start.5) | collective-permute-done | bytes 65568 | tf_op jit(solution)/shard_map/ppermute | solution.py:141
  31.5 0.1 select_add_fusion
  31.6 0.2 collective-permute-start.7
  31.7 1.1 %copy-done.12 = bf16[1280,256]{1,0:T(8,128)(2,1)S(1)} copy-done((bf16[1280,256]{1,0:T(8,128)(2,1)S(1)}, bf16[1280,256]{1,0:T(8,128)(2,1)}, u32[]{:S(2)}) %copy-start.12) | copy-done | bytes 655384
  32.8 1.0 %copy-done.14 = bf16[5,2,128,128]{3,2,1,0:T(8,128)(2,1)S(1)} copy-done((bf16[5,2,128,128]{3,2,1,0:T(8,128)(2,1)S(1)}, bf16[5,2,128,128]{3,2,1,0:T(8,128)(2,1)}, u32[]{:S(2)}) %copy-start.14) | copy-done | bytes 327704
  33.8 3.5 %shard_map.88 = (bf16[1280,256]{1,0:T(8,128)(2,1)}, f32[1280,256]{1,0:T(8,128)S(1)}, f32[1280,256]{1,0:T(8,128)S(1)}) custom-call(bf16[1280,256]{1,0:T(8,128)(2,1)S(1)} %copy-done.5, bf16[1280,256]{1,0:T(8,128)(2,1)S(1)} %copy-done.1, bf16[1280,256]{1,0:T(8,128)(2,1)S(1)} %copy-done.3, bf16[1280,256]{1,0:T(8,128)(2,1)S(1)} %copy-done.12, ...), custom_call_target="tpu_custom_call" | custom-call | flops 922746880 | bytes 7536640 | tf_op jit(solution)/shard_map/pallas_call | solution.py:109
  37.3 0.0 collective-permute-done.7.far_ref
  37.3 1.5 %shard_map.89 = (bf16[1280,256]{1,0:T(8,128)(2,1)}, bf16[1280,256]{1,0:T(8,128)(2,1)}) custom-call(s32[1]{0:T(128)S(6)} %copy.9.count_ref, bf16[1280,256]{1,0:T(8,128)(2,1)S(1)} %copy-done.1, bf16[1280,256]{1,0:T(8,128)(2,1)S(1)} %copy-done.3, f32[1280,256]{1,0:T(8,128)S(1)} %get-tuple-element.23.gk_part_ref, f32[1280,256]{1,0:T(8,128)S(1)} %get-tuple-element.24.gv_part_ref, ...), custom_call_target="tpu_custom_call" | custom-call | flops 167772160 | bytes 6160388 | tf_op jit(solution)/shard_map/pallas_call | solution.py:109
  (23 shorter events, 0.0 us)
Async XLA Ops:
  1.3 1.1 %copy-start = (bf16[1280,256]{1,0:T(8,128)(2,1)S(1)}, bf16[1280,256]{1,0:T(8,128)(2,1)}, u32[]{:S(2)}) copy-start(bf16[1280,256]{1,0:T(8,128)(2,1)} %k_ref.7) | copy-start | bytes 1966084
  2.4 1.1 %copy-start.2 = (bf16[1280,256]{1,0:T(8,128)(2,1)S(1)}, bf16[1280,256]{1,0:T(8,128)(2,1)}, u32[]{:S(2)}) copy-start(bf16[1280,256]{1,0:T(8,128)(2,1)} %v_ref.7) | copy-start | bytes 1966084
  3.5 12.0 %copy-start.1 = (bf16[1280,256]{1,0:T(8,128)(2,1)S(1)}, bf16[1280,256]{1,0:T(8,128)(2,1)}, u32[]{:S(2)}) copy-start(bf16[1280,256]{1,0:T(8,128)(2,1)} %k_ref.7) | copy-start | bytes 1966084
  3.5 12.0 %copy-start.3 = (bf16[1280,256]{1,0:T(8,128)(2,1)S(1)}, bf16[1280,256]{1,0:T(8,128)(2,1)}, u32[]{:S(2)}) copy-start(bf16[1280,256]{1,0:T(8,128)(2,1)} %v_ref.7) | copy-start | bytes 1966084
  3.9 0.8 %copy-start.9 = (f32[5,2,128,128]{3,2,1,0:T(8,128)}, f32[5,2,128,128]{3,2,1,0:T(8,128)S(1)}, u32[]{:S(2)}) copy-start(f32[5,2,128,128]{3,2,1,0:T(8,128)S(1)} %get-tuple-element.17.run_ref) | copy-start | bytes 1966084
  4.7 13.9 %copy-start.15 = (f32[256]{0:T(256)S(1)}, f32[256]{0:T(256)}, u32[]{:S(2)}) copy-start(f32[256]{0:T(256)} %param.10) | copy-start | bytes 3076
  4.7 7.6 %collective-permute-start.2 = (bf16[2,128,128]{2,1,0:T(8,128)(2,1)S(1)}, bf16[2,128,128]{2,1,0:T(8,128)(2,1)S(1)}, u32[]{:S(2)}, u32[]{:S(2)}) collective-permute-start(bf16[2,128,128]{2,1,0:T(8,128)(2,1)S(1)} %get-tuple-element.18), channel_id=1, source_target_pairs={{0,12},{4,8},{8,4},{12,0},{1,13},{5,9},{9,5},{13,1},{2,14},{6,10},... | collective-permute-start | bytes 196616 | tf_op jit(solution)/shard_map/ppermute | solution.py:141
  9.7 5.6 %collective-permute-start.1 = (bf16[2,128,128]{2,1,0:T(8,128)(2,1)S(1)}, bf16[2,128,128]{2,1,0:T(8,128)(2,1)S(1)}, u32[]{:S(2)}, u32[]{:S(2)}) collective-permute-start(bf16[2,128,128]{2,1,0:T(8,128)(2,1)S(1)} %get-tuple-element.18), channel_id=1, source_target_pairs={{0,8},{4,12},{8,0},{12,4},{1,9},{5,13},{9,1},{13,5},{2,10},{6,14},... | collective-permute-start | bytes 196616 | tf_op jit(solution)/shard_map/ppermute | solution.py:141
  9.7 5.6 %collective-permute-start = (bf16[2,128,128]{2,1,0:T(8,128)(2,1)S(1)}, bf16[2,128,128]{2,1,0:T(8,128)(2,1)S(1)}, u32[]{:S(2)}, u32[]{:S(2)}) collective-permute-start(bf16[2,128,128]{2,1,0:T(8,128)(2,1)S(1)} %get-tuple-element.18), channel_id=1, source_target_pairs={{0,4},{4,0},{8,12},{12,8},{1,5},{5,1},{9,13},{13,9},{2,6},{6,2},{1... | collective-permute-start | bytes 196616 | tf_op jit(solution)/shard_map/ppermute | solution.py:141
  15.4 3.2 %collective-permute-start.3 = (f32[2,128,128]{2,1,0:T(8,128)S(1)}, f32[2,128,128]{2,1,0:T(8,128)S(1)}, u32[]{:S(2)}, u32[]{:S(2)}) collective-permute-start(f32[2,128,128]{2,1,0:T(8,128)S(1)} %get-tuple-element.31), channel_id=1, source_target_pairs={{0,1},{1,0},{2,3},{3,2},{4,5},{5,4},{6,7},{7,6},{8,9},{9,8},{10,11... | collective-permute-start | bytes 393224 | tf_op jit(solution)/shard_map/ppermute | solution.py:157
  15.5 1.1 %copy-start.4 = (bf16[1280,256]{1,0:T(8,128)(2,1)S(1)}, bf16[1280,256]{1,0:T(8,128)(2,1)}, u32[]{:S(2)}) copy-start(bf16[1280,256]{1,0:T(8,128)(2,1)} %q_ref.5) | copy-start | bytes 1966084
  16.6 2.0 %copy-start.8 = (bf16[1280,256]{1,0:T(8,128)(2,1)S(1)}, bf16[1280,256]{1,0:T(8,128)(2,1)}, u32[]{:S(2)}) copy-start(bf16[1280,256]{1,0:T(8,128)(2,1)} %cot_ref.1) | copy-start | bytes 1966084
  16.6 2.0 %copy-start.10 = (f32[5,2,128,128]{3,2,1,0:T(8,128)S(1)}, f32[5,2,128,128]{3,2,1,0:T(8,128)}, u32[]{:S(2)}) copy-start(f32[5,2,128,128]{3,2,1,0:T(8,128)} %copy-done.9) | copy-start | bytes 1966084
  18.6 13.1 %copy-start.5 = (bf16[1280,256]{1,0:T(8,128)(2,1)S(1)}, bf16[1280,256]{1,0:T(8,128)(2,1)}, u32[]{:S(2)}) copy-start(bf16[1280,256]{1,0:T(8,128)(2,1)} %q_ref.5) | copy-start | bytes 1966084
  19.9 0.8 %copy-start.6 = (f32[5,2,128,128]{3,2,1,0:T(8,128)}, f32[5,2,128,128]{3,2,1,0:T(8,128)S(1)}, u32[]{:S(2)}) copy-start(f32[5,2,128,128]{3,2,1,0:T(8,128)S(1)} %get-tuple-element.25.back_ref) | copy-start | bytes 1966084
  20.8 0.8 %copy-start.11 = (bf16[1280,256]{1,0:T(8,128)(2,1)}, bf16[1280,256]{1,0:T(8,128)(2,1)S(1)}, u32[]{:S(2)}) copy-start(bf16[1280,256]{1,0:T(8,128)(2,1)S(1)} %get-tuple-element.19.grad_ref) | copy-start | bytes 1966084
  21.6 0.7 %copy-start.13 = (bf16[5,2,128,128]{3,2,1,0:T(8,128)(2,1)}, bf16[5,2,128,128]{3,2,1,0:T(8,128)(2,1)S(1)}, u32[]{:S(2)}) copy-start(bf16[5,2,128,128]{3,2,1,0:T(8,128)(2,1)S(1)} %get-tuple-element.21.prefix_ref) | copy-start | bytes 983044
  22.3 6.8 %collective-permute-start.6 = (bf16[2,128,128]{2,1,0:T(8,128)(2,1)S(1)}, bf16[2,128,128]{2,1,0:T(8,128)(2,1)S(1)}, u32[]{:S(2)}, u32[]{:S(2)}) collective-permute-start(bf16[2,128,128]{2,1,0:T(8,128)(2,1)S(1)} %get-tuple-element.26), channel_id=1, source_target_pairs={{0,12},{4,8},{8,4},{12,0},{1,13},{5,9},{9,5},{13,1},{2,14},{6,10},... | collective-permute-start | bytes 196616 | tf_op jit(solution)/shard_map/ppermute | solution.py:141
  25.0 6.5 %collective-permute-start.5 = (bf16[2,128,128]{2,1,0:T(8,128)(2,1)S(1)}, bf16[2,128,128]{2,1,0:T(8,128)(2,1)S(1)}, u32[]{:S(2)}, u32[]{:S(2)}) collective-permute-start(bf16[2,128,128]{2,1,0:T(8,128)(2,1)S(1)} %get-tuple-element.26), channel_id=1, source_target_pairs={{0,8},{4,12},{8,0},{12,4},{1,9},{5,13},{9,1},{13,5},{2,10},{6,14},... | collective-permute-start | bytes 196616 | tf_op jit(solution)/shard_map/ppermute | solution.py:141
  25.0 6.5 %collective-permute-start.4 = (bf16[2,128,128]{2,1,0:T(8,128)(2,1)S(1)}, bf16[2,128,128]{2,1,0:T(8,128)(2,1)S(1)}, u32[]{:S(2)}, u32[]{:S(2)}) collective-permute-start(bf16[2,128,128]{2,1,0:T(8,128)(2,1)S(1)} %get-tuple-element.26), channel_id=1, source_target_pairs={{0,4},{4,0},{8,12},{12,8},{1,5},{5,1},{9,13},{13,9},{2,6},{6,2},{1... | collective-permute-start | bytes 196616 | tf_op jit(solution)/shard_map/ppermute | solution.py:141
  31.6 5.8 %collective-permute-start.7 = (f32[2,128,128]{2,1,0:T(8,128)S(1)}, f32[2,128,128]{2,1,0:T(8,128)S(1)}, u32[]{:S(2)}, u32[]{:S(2)}) collective-permute-start(f32[2,128,128]{2,1,0:T(8,128)S(1)} %get-tuple-element.29), channel_id=1, source_target_pairs={{0,1},{1,0},{2,3},{3,2},{4,5},{5,4},{6,7},{7,6},{8,9},{9,8},{10,11... | collective-permute-start | bytes 393224 | tf_op jit(solution)/shard_map/ppermute | solution.py:157
  31.7 1.1 %copy-start.12 = (bf16[1280,256]{1,0:T(8,128)(2,1)S(1)}, bf16[1280,256]{1,0:T(8,128)(2,1)}, u32[]{:S(2)}) copy-start(bf16[1280,256]{1,0:T(8,128)(2,1)} %copy-done.11) | copy-start | bytes 1966084
  32.8 1.0 %copy-start.14 = (bf16[5,2,128,128]{3,2,1,0:T(8,128)(2,1)S(1)}, bf16[5,2,128,128]{3,2,1,0:T(8,128)(2,1)}, u32[]{:S(2)}) copy-start(bf16[5,2,128,128]{3,2,1,0:T(8,128)(2,1)} %copy-done.13) | copy-start | bytes 983044
  33.8 3.5 %copy-start.7 = (f32[5,2,128,128]{3,2,1,0:T(8,128)S(1)}, f32[5,2,128,128]{3,2,1,0:T(8,128)}, u32[]{:S(2)}) copy-start(f32[5,2,128,128]{3,2,1,0:T(8,128)} %copy-done.6) | copy-start | bytes 1966084

commit v2 on v1

v2 whole, which is shorter than its diff:
```python
import functools
import math

import jax
import jax.numpy as jnp
from jax import lax
from jax.experimental import pallas as pl
from jax.experimental.pallas import tpu as pltpu
from jax.sharding import PartitionSpec as P

DH = 128
SPAN = 256
EPSILON = 1e-06
F32 = jnp.float32
BF16 = jnp.bfloat16
VMEM = pl.BlockSpec(memory_space=pltpu.VMEM)
SMEM = pl.BlockSpec(memory_space=pltpu.SMEM)
HBM = pl.BlockSpec(memory_space=pltpu.HBM)


def nn(a, b):
    return lax.dot_general(a, b, (((1,), (0,)), ((), ())), preferred_element_type=F32)


def nt(a, b):
    return lax.dot_general(a, b, (((1,), (1,)), ((), ())), preferred_element_type=F32)


def tn(a, b):
    return lax.dot_general(a, b, (((0,), (0,)), ((), ())), preferred_element_type=F32)


def tiles(rows, width):
    for b in range(rows // SPAN):
        for h in range(width // DH):
            yield b, h, slice(b * SPAN, (b + 1) * SPAN), slice(h * DH, (h + 1) * DH)


def fetch(pairs, sems):
    copies = []
    for b in range(pairs[0][0].shape[0] // SPAN):
        r = pl.ds(b * SPAN, SPAN)
        copies.append([pltpu.make_async_copy(source.at[r], target.at[r], sems.at[b, at])
                       for at, (source, target) in enumerate(pairs)])
        for copy in copies[-1]:
            copy.start()
    return copies


def wait(copies):
    for copy in copies:
        copy.wait()


def state_of(count_ref, b, k, v):
    state = tn(k, v)
    return jnp.where(b < count_ref[0], state, jnp.zeros_like(state))


def state_kernel(count_ref, k_hbm, v_hbm, total_ref, k_ref, v_ref, sems):
    copies = fetch(((k_hbm, k_ref), (v_hbm, v_ref)), sems)
    running = {}
    for b, h, r, c in tiles(*k_ref.shape):
        if h == 0:
            wait(copies[b])
        state = state_of(count_ref, b, k_ref[r, c], v_ref[r, c])
        running[h] = running[h] + state if b else state
    for h, state in running.items():
        total_ref[h] = state.astype(total_ref.dtype)


def score_kernel(count_ref, q_hbm, cot_hbm, k_ref, v_ref,
                 part_ref, turned_ref, run_ref, q_ref, cot_ref, sems):
    copies = fetch(((q_hbm, q_ref), (cot_hbm, cot_ref)), sems)
    running = {}
    t = lax.broadcasted_iota(jnp.int32, (SPAN, SPAN), 0)
    s = lax.broadcasted_iota(jnp.int32, (SPAN, SPAN), 1)
    for b, h, r, c in tiles(*q_ref.shape):
        if h == 0:
            wait(copies[b])
        q, k, v = q_ref[r, c], k_ref[r, c], v_ref[r, c]
        state = state_of(count_ref, b, k, v)
        run_ref[b, h] = running[h] if b else jnp.zeros_like(state)
        running[h] = running[h] + state if b else state
        scored = jnp.where(t >= s, nt(q, k), 0.0).astype(BF16)
        part_ref[r, c] = nn(scored, v)
        turned_ref[b, h] = jnp.where(t <= s, nt(k, q), 0.0).astype(BF16)


def norm_kernel(count_ref, q_ref, cot_ref, gain_ref, part_ref, run_ref, near_ref, far_ref,
                grad_ref, prefix_ref, back_ref, total_ref):
    running = {}
    for b, h, r, c in reversed(list(tiles(*q_ref.shape))):
        prefix = (run_ref[b, h] + near_ref[h] + far_ref[h]).astype(BF16)
        prefix_ref[b, h] = prefix
        q = q_ref[r, c]
        raw = part_ref[r, c] + nn(q, prefix)
        inverse = lax.rsqrt(jnp.mean(raw * raw, axis=-1, keepdims=True) + EPSILON)
        gain = gain_ref[:, c]
        gain = jnp.where(b < count_ref[0], gain, jnp.zeros_like(gain))
        weighted = gain * cot_ref[r, c].astype(F32)
        pulled = jnp.mean(weighted * raw, axis=-1, keepdims=True)
        grad = (inverse * weighted - raw * (inverse * inverse * inverse * pulled)).astype(BF16)
        grad_ref[r, c] = grad
        state = tn(q, grad)
        back_ref[b, h] = running.get(h, jnp.zeros_like(state))
        running[h] = running[h] + state if h in running else state
    for h, state in running.items():
        total_ref[h] = state.astype(total_ref.dtype)


def pull_kernel(q_ref, k_ref, v_ref, grad_ref, turned_ref, prefix_ref,
                gq_hbm, gk_ref, gv_ref, gq_ref, sems):
    t = lax.broadcasted_iota(jnp.int32, (SPAN, SPAN), 0)
    s = lax.broadcasted_iota(jnp.int32, (SPAN, SPAN), 1)
    heads = q_ref.shape[1] // DH
    copies = []
    for b, h, r, c in tiles(*q_ref.shape):
        v, grad = v_ref[r, c], grad_ref[r, c]
        pull = jnp.where(t >= s, nt(grad, v), 0.0).astype(BF16)
        gq_ref[r, c] = (nn(pull, k_ref[r, c]) + nt(grad, prefix_ref[b, h])).astype(BF16)
        if h == heads - 1:
            copies.append(pltpu.make_async_copy(gq_ref.at[r], gq_hbm.at[r], sems.at[b]))
            copies[-1].start()
        turned = jnp.where(t <= s, nt(v, grad), 0.0).astype(BF16)
        gk_ref[r, c] = nn(turned, q_ref[r, c])
        gv_ref[r, c] = nn(turned_ref[b, h], grad)
    wait(copies)


def final_kernel(count_ref, k_ref, v_ref, gk_part_ref, gv_part_ref, back_ref, near_ref, far_ref,
                 gk_hbm, gv_hbm, gk_ref, gv_ref, sems):
    heads = k_ref.shape[1] // DH
    copies = []
    for b, h, r, c in tiles(*k_ref.shape):
        suffix = back_ref[b, h] + near_ref[h] + far_ref[h]
        suffix = jnp.where(b < count_ref[0], suffix, jnp.zeros_like(suffix)).astype(BF16)
        gk_ref[r, c] = (gk_part_ref[r, c] + nt(v_ref[r, c], suffix)).astype(BF16)
        gv_ref[r, c] = (gv_part_ref[r, c] + nn(k_ref[r, c], suffix)).astype(BF16)
        if h == heads - 1:
            for at, (source, target) in enumerate(((gk_ref, gk_hbm), (gv_ref, gv_hbm))):
                copies.append(pltpu.make_async_copy(source.at[r], target.at[r], sems.at[b, at]))
                copies[-1].start()
    wait(copies)


def place(array, space):
    return array if space is SMEM else pltpu.with_memory_space_constraint(array, space.memory_space)


def call(kernel, ins, outs, flops, scratch=()):
    size = sum(a.size * a.dtype.itemsize for a, _ in ins)
    size += sum(math.prod(shape) * jnp.dtype(kind).itemsize for (shape, kind), _ in outs)
    return pl.pallas_call(
        kernel,
        out_shape=[pltpu.VMEM(*a) if space is VMEM else pltpu.HBM(*a) for a, space in outs],
        in_specs=[space for _, space in ins],
        out_specs=[space for _, space in outs],
        scratch_shapes=scratch,
        cost_estimate=pl.CostEstimate(flops=flops, bytes_accessed=size, transcendentals=0),
        compiler_params=pltpu.CompilerParams(vmem_limit_bytes=16 * 2**20),
    )(*[place(a, space) for a, space in ins])


def radices(count):
    found = []
    for radix in (4, 2):
        while count % radix == 0:
            found.append(radix)
            count //= radix
    return found + [count] if count > 1 else found


def partner(digit, step, radix):
    return digit ^ step if radix in (2, 4) else (digit + step) % radix


def combine_kernel(steps, radix, stride, reverse, last, *refs):
    own_ref, group_ref, outside_ref = refs[:3]
    came = refs[3:3 + len(steps)]
    near_ref, sent_ref = refs[3 + len(steps):]
    digit = lax.rem(lax.div(lax.axis_index("seq"), stride), radix)
    near = outside_ref[...]
    whole = group_ref[...].astype(F32)
    for step, piece_ref in zip(steps, came):
        back = step if radix in (2, 4) else radix - step
        source = partner(digit, back, radix)
        use = source > digit if reverse else source < digit
        piece = piece_ref[...].astype(F32)
        near = near + jnp.where(use, piece, 0.0)
        whole = whole + piece
    near_ref[...] = near
    if last:
        mine = lax.axis_index("loader") == (1 if reverse else 0)
        sent_ref[...] = near + jnp.where(mine, own_ref[...].astype(F32), 0.0)
    else:
        sent_ref[...] = whole.astype(sent_ref.dtype)


def outside_sum(total, reverse, cover):
    count = lax.axis_size("seq")
    outside = jnp.zeros(total.shape, F32)
    group, stride = total, 1
    chain = radices(count)
    for at, radix in enumerate(chain):
        steps = list(range(radix - 1, 0, -1))
        came = []
        for step in steps:
            pairs = [(s, s + (partner(s // stride % radix, step, radix) - s // stride % radix) * stride)
                     for s in range(count)]
            came.append(lax.ppermute(group, "seq", pairs))
        if at == 0:
            came, cover = lax.optimization_barrier((came, cover))
        last = at + 1 == len(chain)
        kernel = functools.partial(combine_kernel, steps, radix, stride, reverse, last)
        sum_like = (total.shape, F32), VMEM
        outside, group = call(
            kernel, [(a, VMEM) for a in (total, group, outside, *came)],
            [sum_like, sum_like if last else ((total.shape, total.dtype), VMEM)], total.size)
        stride *= radix
    far = lax.ppermute(group, "loader", [(0, 1), (1, 0)])
    return outside, far, cover


def shards(queries, key_rows, values, cotangent, out_gain, counts):
    rows, width = queries.shape
    blocks, heads = rows // SPAN, width // DH
    unit = 2 * rows * width * DH
    states = ((blocks, heads, DH, DH), F32), VMEM
    prefixes = ((blocks, heads, DH, DH), BF16), VMEM
    total = ((heads, DH, DH), BF16), VMEM
    plane = ((rows, width), F32), VMEM
    half = ((rows, width), BF16), VMEM
    result = ((rows, width), BF16), HBM
    square = ((blocks, heads, SPAN, SPAN), BF16), VMEM
    staged = pltpu.VMEM((rows, width), BF16)
    pair_sems = pltpu.SemaphoreType.DMA((blocks, 2))

    def vmem(*arrays):
        return [(a, VMEM) for a in arrays]

    count = [(counts, SMEM)]
    own, k, v = call(
        state_kernel, count + [(key_rows, HBM), (values, HBM)], [total, half, half], unit, [pair_sems])
    cover = call(
        score_kernel, count + [(queries, HBM), (cotangent, HBM)] + vmem(k, v),
        [plane, square, states, half, half], 7 * unit, [pair_sems])
    near, far, (part, turned, run, q, cot) = outside_sum(own, False, cover)
    grad, prefix, back, own_back = call(
        norm_kernel, count + vmem(q, cot, out_gain.reshape(1, width), part, run, near, far),
        [half, prefixes, states, total], 2 * unit)
    cover = call(
        pull_kernel, vmem(q, k, v, grad, turned, prefix), [result, plane, plane], 11 * unit,
        [staged, pltpu.SemaphoreType.DMA((blocks,))])
    near, far, (gq, gk_part, gv_part) = outside_sum(own_back, True, cover)
    gk, gv = call(
        final_kernel, count + vmem(k, v, gk_part, gv_part, back, near, far), [result, result], 2 * unit,
        [staged, staged, pair_sems])
    return gq, gk, gv


def solution(mesh):
    rows = P(("groups", "seq", "loader"), "head")
    return jax.shard_map(
        shards,
        mesh=mesh,
        in_specs=(rows, rows, rows, rows, P("head"), P(("groups", "seq", "loader"))),
        out_specs=(rows, rows, rows),
        check_vma=False,
    )
```

time: 39.2 us -> 29 us (0.74)
  local copies, waits for them, and re-layouts: 8.56 us -> 0.01 us
  waiting for transfers between devices: 9.83 us -> 4.74 us
  Pallas kernels: 8.7 us -> 12.4 us
    unnamed x32 -> x2, local copies, waits for them, and re-layouts: 8.56 us -> 0.01 us
    ppermute x8, waiting for transfers between devices: 9.83 us -> 4.74 us  [the longest x2 2.65 us: outside_sum(): far = lax.ppermute(group, 'loader', [(0, 1), (1, 0)])]
    pallas_call x5 -> x7, Pallas kernels: 8.7 us -> 12.4 us  [call(): pl.pallas_call(kernel, out_shape=[pltpu.VMEM(*a) if space is VMEM else pl...]
  transfers between devices with their start and end apart: 8 -> 8, of which waited for: 4 -> 4; matrix products, arithmetic and copies ran while one was open for 0% -> 0% of each run, Pallas kernels for 14% -> 26%
where the time goes in v2:
time: 29 us; the launch traced here: 28.9 us
  Pallas kernels  12.4 us (43%)
  starting transfers between devices  10.4 us (36%)
  waiting for transfers between devices  4.74 us (16%)
  between operations  1.36 us (5%)
    pallas_call x7, Pallas kernels, call(): pl.pallas_call(kernel, out_shape=[pltpu.VMEM(*a) if space is VMEM else pl...  12.4 us
    ppermute x6, starting transfers between devices, outside_sum(): came.append(lax.ppermute(group, 'seq', pairs))  10.2 us
    ppermute x2, waiting for transfers between devices, outside_sum(): far = lax.ppermute(group, 'loader', [(0, 1), (1, 0)])  2.65 us
    ppermute x6, waiting for transfers between devices, outside_sum(): came.append(lax.ppermute(group, 'seq', pairs))  2.09 us
  transfers between devices with their start and end apart: 8, of which 4 were waited for; matrix products, arithmetic and copies ran while one was open for 0% of the time, Pallas kernels for 26%

profile of v2, /device:TPU:0, one launch (start us, length us, event | category | flops | bytes accessed | tf_op | source)
XLA Modules:
  0.0 28.9 jit_solution(2485082367549035989)
XLA Ops:
  1.3 2.2 %shard_map.85 = (bf16[2,128,128]{2,1,0:T(8,128)(2,1)S(1)}, bf16[1280,256]{1,0:T(8,128)(2,1)S(1)}, bf16[1280,256]{1,0:T(8,128)(2,1)S(1)}) custom-call(s32[1]{0:T(128)S(6)} %copy.9.count_ref, bf16[1280,256]{1,0:T(8,128)(2,1)} %k_hbm.1, bf16[1280,256]{1,0:T(8,128)(2,1)} %v_hbm.1), custom_call_target="tpu_custom_call" | custom-call | flops 83886080 | bytes 2686980 | tf_op jit(solution)/shard_map/pallas_call | solution.py:154
  3.5 5.1 %collective-permute-start = (bf16[2,128,128]{2,1,0:T(8,128)(2,1)S(1)}, bf16[2,128,128]{2,1,0:T(8,128)(2,1)S(1)}, u32[]{:S(2)}, u32[]{:S(2)}) collective-permute-start(bf16[2,128,128]{2,1,0:T(8,128)(2,1)S(1)} %get-tuple-element.38.refs_0_.refs_1_), channel_id=1, source_target_pairs={{0,12},{4,8},{8,4},{12,0},{1,13},{5,9},{9,5},{13,1},{2,14},{6,10},... | collective-permute-start | bytes 196616 | tf_op jit(solution)/shard_map/ppermute | solution.py:211
  8.6 0.0 collective-permute-start.1
  8.6 0.6 %collective-permute-start.2 = (bf16[2,128,128]{2,1,0:T(8,128)(2,1)S(1)}, bf16[2,128,128]{2,1,0:T(8,128)(2,1)S(1)}, u32[]{:S(2)}, u32[]{:S(2)}) collective-permute-start(bf16[2,128,128]{2,1,0:T(8,128)(2,1)S(1)} %get-tuple-element.38.refs_0_.refs_1_), channel_id=1, source_target_pairs={{0,4},{4,0},{8,12},{12,8},{1,5},{5,1},{9,13},{13,9},{2,6},{6,2},{1... | collective-permute-start | bytes 196616 | tf_op jit(solution)/shard_map/ppermute | solution.py:211
  9.2 0.0 copy-start
  9.2 4.1 %shard_map.86 = (f32[1280,256]{1,0:T(8,128)S(1)}, bf16[5,2,256,256]{3,2,1,0:T(8,128)(2,1)S(1)}, f32[5,2,128,128]{3,2,1,0:T(8,128)S(1)}, bf16[1280,256]{1,0:T(8,128)(2,1)S(1)}, bf16[1280,256]{1,0:T(8,128)(2,1)S(1)}) custom-call(s32[1]{0:T(128)S(6)} %copy.9.count_ref, bf16[1280,256]{1,0:T(8,128)(2,1)} %q_hbm.1, bf16[1280,256]{1,0:T(8,128)(2,1)} %cot_hbm.1, ...), custom_call_target="tpu_custom_call" | custom-call | flops 587202560 | bytes 7208964 | tf_op jit(solution)/shard_map/pallas_call | solution.py:154
  13.3 0.0 collective-permute-done.refs_3_
  13.4 0.9 %collective-permute-done.1.refs_4_ = bf16[2,128,128]{2,1,0:T(8,128)(2,1)S(1)} collective-permute-done((bf16[2,128,128]{2,1,0:T(8,128)(2,1)S(1)}, bf16[2,128,128]{2,1,0:T(8,128)(2,1)S(1)}, u32[]{:S(2)}, u32[]{:S(2)}) %collective-permute-start.1) | collective-permute-done | bytes 65568 | tf_op jit(solution)/shard_map/ppermute | solution.py:211
  14.2 0.0 collective-permute-done.2.refs_5_
  14.2 0.1 shard_map.87
  14.3 0.1 collective-permute-start.3
  14.4 1.3 %collective-permute-done.3.far_ref = f32[2,128,128]{2,1,0:T(8,128)S(1)} collective-permute-done((f32[2,128,128]{2,1,0:T(8,128)S(1)}, f32[2,128,128]{2,1,0:T(8,128)S(1)}, u32[]{:S(2)}, u32[]{:S(2)}) %collective-permute-start.3) | collective-permute-done | bytes 131104 | tf_op jit(solution)/shard_map/ppermute | solution.py:221
  15.7 0.0 copy-done
  15.7 1.3 %shard_map.88 = (bf16[1280,256]{1,0:T(8,128)(2,1)S(1)}, bf16[5,2,128,128]{3,2,1,0:T(8,128)(2,1)S(1)}, f32[5,2,128,128]{3,2,1,0:T(8,128)S(1)}, bf16[2,128,128]{2,1,0:T(8,128)(2,1)S(1)}) custom-call(s32[1]{0:T(128)S(6)} %copy.9.count_ref, bf16[1280,256]{1,0:T(8,128)(2,1)S(1)} %get-tuple-element.46.q_ref, bf16[1280,256]{1,0:T(8,128)(2,1)S(1)} %get-tuple-element.47.cot_ref, ...), custom_call_target="tpu_custom_call" | custom-call | flops 167772160 | bytes 5243908 | tf_op jit(solution)/shard_map/pallas_call | solution.py:154
  17.0 3.0 %collective-permute-start.4 = (bf16[2,128,128]{2,1,0:T(8,128)(2,1)S(1)}, bf16[2,128,128]{2,1,0:T(8,128)(2,1)S(1)}, u32[]{:S(2)}, u32[]{:S(2)}) collective-permute-start(bf16[2,128,128]{2,1,0:T(8,128)(2,1)S(1)} %get-tuple-element.55.refs_0_.refs_1_), channel_id=1, source_target_pairs={{0,12},{4,8},{8,4},{12,0},{1,13},{5,9},{9,5},{13,1},{2,14},{6,10},... | collective-permute-start | bytes 196616 | tf_op jit(solution)/shard_map/ppermute | solution.py:211
  20.0 0.0 collective-permute-start.5
  20.0 1.5 %collective-permute-start.6 = (bf16[2,128,128]{2,1,0:T(8,128)(2,1)S(1)}, bf16[2,128,128]{2,1,0:T(8,128)(2,1)S(1)}, u32[]{:S(2)}, u32[]{:S(2)}) collective-permute-start(bf16[2,128,128]{2,1,0:T(8,128)(2,1)S(1)} %get-tuple-element.55.refs_0_.refs_1_), channel_id=1, source_target_pairs={{0,4},{4,0},{8,12},{12,8},{1,5},{5,1},{9,13},{13,9},{2,6},{6,2},{1... | collective-permute-start | bytes 196616 | tf_op jit(solution)/shard_map/ppermute | solution.py:211
  21.4 3.4 %shard_map.89 = (bf16[1280,256]{1,0:T(8,128)(2,1)}, f32[1280,256]{1,0:T(8,128)S(1)}, f32[1280,256]{1,0:T(8,128)S(1)}) custom-call(bf16[1280,256]{1,0:T(8,128)(2,1)S(1)} %get-tuple-element.46.q_ref, bf16[1280,256]{1,0:T(8,128)(2,1)S(1)} %get-tuple-element.39.k_ref, bf16[1280,256]{1,0:T(8,128)(2,1)S(1)} %get-tuple-element.40.v_ref, ...), custom_call_target="tpu_custom_call" | custom-call | flops 922746880 | bytes 7536640 | tf_op jit(solution)/shard_map/pallas_call | solution.py:154
  24.8 0.0 collective-permute-done.4.refs_3_
  24.8 1.2 %collective-permute-done.5.refs_4_ = bf16[2,128,128]{2,1,0:T(8,128)(2,1)S(1)} collective-permute-done((bf16[2,128,128]{2,1,0:T(8,128)(2,1)S(1)}, bf16[2,128,128]{2,1,0:T(8,128)(2,1)S(1)}, u32[]{:S(2)}, u32[]{:S(2)}) %collective-permute-start.5) | collective-permute-done | bytes 65568 | tf_op jit(solution)/shard_map/ppermute | solution.py:211
  26.0 0.0 collective-permute-done.6.refs_5_
  26.0 0.1 shard_map.90
  26.1 0.1 collective-permute-start.7
  26.2 1.3 %collective-permute-done.7.far_ref = f32[2,128,128]{2,1,0:T(8,128)S(1)} collective-permute-done((f32[2,128,128]{2,1,0:T(8,128)S(1)}, f32[2,128,128]{2,1,0:T(8,128)S(1)}, u32[]{:S(2)}, u32[]{:S(2)}) %collective-permute-start.7) | collective-permute-done | bytes 131104 | tf_op jit(solution)/shard_map/ppermute | solution.py:221
  27.5 1.3 %shard_map.91 = (bf16[1280,256]{1,0:T(8,128)(2,1)}, bf16[1280,256]{1,0:T(8,128)(2,1)}) custom-call(s32[1]{0:T(128)S(6)} %copy.9.count_ref, bf16[1280,256]{1,0:T(8,128)(2,1)S(1)} %get-tuple-element.39.k_ref, bf16[1280,256]{1,0:T(8,128)(2,1)S(1)} %get-tuple-element.40.v_ref, f32[1280,256]{1,0:T(8,128)S(1)} %get-tuple-element.63.gk_part_ref, ...), custom_call_target="tpu_custom_call" | custom-call | flops 167772160 | bytes 6160388 | tf_op jit(solution)/shard_map/pallas_call | solution.py:154
  (1 shorter events, 0.0 us)
Async XLA Ops:
  3.5 9.9 %collective-permute-start = (bf16[2,128,128]{2,1,0:T(8,128)(2,1)S(1)}, bf16[2,128,128]{2,1,0:T(8,128)(2,1)S(1)}, u32[]{:S(2)}, u32[]{:S(2)}) collective-permute-start(bf16[2,128,128]{2,1,0:T(8,128)(2,1)S(1)} %get-tuple-element.38.refs_0_.refs_1_), channel_id=1, source_target_pairs={{0,12},{4,8},{8,4},{12,0},{1,13},{5,9},{9,5},{13,1},{2,14},{6,10},... | collective-permute-start | bytes 196616 | tf_op jit(solution)/shard_map/ppermute | solution.py:211
  8.6 5.6 %collective-permute-start.1 = (bf16[2,128,128]{2,1,0:T(8,128)(2,1)S(1)}, bf16[2,128,128]{2,1,0:T(8,128)(2,1)S(1)}, u32[]{:S(2)}, u32[]{:S(2)}) collective-permute-start(bf16[2,128,128]{2,1,0:T(8,128)(2,1)S(1)} %get-tuple-element.38.refs_0_.refs_1_), channel_id=1, source_target_pairs={{0,8},{4,12},{8,0},{12,4},{1,9},{5,13},{9,1},{13,5},{2,10},{6,14},... | collective-permute-start | bytes 196616 | tf_op jit(solution)/shard_map/ppermute | solution.py:211
  8.6 5.6 %collective-permute-start.2 = (bf16[2,128,128]{2,1,0:T(8,128)(2,1)S(1)}, bf16[2,128,128]{2,1,0:T(8,128)(2,1)S(1)}, u32[]{:S(2)}, u32[]{:S(2)}) collective-permute-start(bf16[2,128,128]{2,1,0:T(8,128)(2,1)S(1)} %get-tuple-element.38.refs_0_.refs_1_), channel_id=1, source_target_pairs={{0,4},{4,0},{8,12},{12,8},{1,5},{5,1},{9,13},{13,9},{2,6},{6,2},{1... | collective-permute-start | bytes 196616 | tf_op jit(solution)/shard_map/ppermute | solution.py:211
  9.2 6.5 %copy-start = (f32[256]{0:T(256)S(1)}, f32[256]{0:T(256)}, u32[]{:S(2)}) copy-start(f32[256]{0:T(256)} %param.10) | copy-start | bytes 3076
  14.3 1.4 %collective-permute-start.3 = (f32[2,128,128]{2,1,0:T(8,128)S(1)}, f32[2,128,128]{2,1,0:T(8,128)S(1)}, u32[]{:S(2)}, u32[]{:S(2)}) collective-permute-start(f32[2,128,128]{2,1,0:T(8,128)S(1)} %get-tuple-element.54), channel_id=1, source_target_pairs={{0,1},{1,0},{2,3},{3,2},{4,5},{5,4},{6,7},{7,6},{8,9},{9,8},{10,11... | collective-permute-start | bytes 393224 | tf_op jit(solution)/shard_map/ppermute | solution.py:221
  17.0 7.8 %collective-permute-start.4 = (bf16[2,128,128]{2,1,0:T(8,128)(2,1)S(1)}, bf16[2,128,128]{2,1,0:T(8,128)(2,1)S(1)}, u32[]{:S(2)}, u32[]{:S(2)}) collective-permute-start(bf16[2,128,128]{2,1,0:T(8,128)(2,1)S(1)} %get-tuple-element.55.refs_0_.refs_1_), channel_id=1, source_target_pairs={{0,12},{4,8},{8,4},{12,0},{1,13},{5,9},{9,5},{13,1},{2,14},{6,10},... | collective-permute-start | bytes 196616 | tf_op jit(solution)/shard_map/ppermute | solution.py:211
  20.0 6.1 %collective-permute-start.5 = (bf16[2,128,128]{2,1,0:T(8,128)(2,1)S(1)}, bf16[2,128,128]{2,1,0:T(8,128)(2,1)S(1)}, u32[]{:S(2)}, u32[]{:S(2)}) collective-permute-start(bf16[2,128,128]{2,1,0:T(8,128)(2,1)S(1)} %get-tuple-element.55.refs_0_.refs_1_), channel_id=1, source_target_pairs={{0,8},{4,12},{8,0},{12,4},{1,9},{5,13},{9,1},{13,5},{2,10},{6,14},... | collective-permute-start | bytes 196616 | tf_op jit(solution)/shard_map/ppermute | solution.py:211
  20.0 6.1 %collective-permute-start.6 = (bf16[2,128,128]{2,1,0:T(8,128)(2,1)S(1)}, bf16[2,128,128]{2,1,0:T(8,128)(2,1)S(1)}, u32[]{:S(2)}, u32[]{:S(2)}) collective-permute-start(bf16[2,128,128]{2,1,0:T(8,128)(2,1)S(1)} %get-tuple-element.55.refs_0_.refs_1_), channel_id=1, source_target_pairs={{0,4},{4,0},{8,12},{12,8},{1,5},{5,1},{9,13},{13,9},{2,6},{6,2},{1... | collective-permute-start | bytes 196616 | tf_op jit(solution)/shard_map/ppermute | solution.py:211
  26.1 1.4 %collective-permute-start.7 = (f32[2,128,128]{2,1,0:T(8,128)S(1)}, f32[2,128,128]{2,1,0:T(8,128)S(1)}, u32[]{:S(2)}, u32[]{:S(2)}) collective-permute-start(f32[2,128,128]{2,1,0:T(8,128)S(1)} %get-tuple-element.70), channel_id=1, source_target_pairs={{0,1},{1,0},{2,3},{3,2},{4,5},{5,4},{6,7},{7,6},{8,9},{9,8},{10,11... | collective-permute-start | bytes 393224 | tf_op jit(solution)/shard_map/ppermute | solution.py:221

commit v3 on v2

v3 whole, which is shorter than its diff:
```python
import functools
import math

import jax
import jax.numpy as jnp
from jax import lax
from jax.experimental import pallas as pl
from jax.experimental.pallas import tpu as pltpu
from jax.sharding import PartitionSpec as P

DH = 128
SPAN = 256
EPSILON = 1e-06
F32 = jnp.float32
BF16 = jnp.bfloat16
VMEM = pl.BlockSpec(memory_space=pltpu.VMEM)
SMEM = pl.BlockSpec(memory_space=pltpu.SMEM)
HBM = pl.BlockSpec(memory_space=pltpu.HBM)


def nn(a, b):
    return lax.dot_general(a, b, (((1,), (0,)), ((), ())), preferred_element_type=F32)


def nt(a, b):
    return lax.dot_general(a, b, (((1,), (1,)), ((), ())), preferred_element_type=F32)


def tn(a, b):
    return lax.dot_general(a, b, (((0,), (0,)), ((), ())), preferred_element_type=F32)


def tiles(rows, width):
    for b in range(rows // SPAN):
        for h in range(width // DH):
            yield b, h, slice(b * SPAN, (b + 1) * SPAN), slice(h * DH, (h + 1) * DH)


def fetch(pairs, sems):
    copies = [pltpu.make_async_copy(source, target, sems.at[at]) for at, (source, target) in enumerate(pairs)]
    for copy in copies:
        copy.start()
    return copies


def wait(copies):
    for copy in copies:
        copy.wait()


def state_of(count_ref, b, k, v):
    state = tn(k, v)
    return jnp.where(b < count_ref[0], state, jnp.zeros_like(state))


def halves(total, h, keep_ref, give_ref):
    first = lax.axis_index("loader") == 0
    low, high = total[:DH // 2], total[DH // 2:]
    keep_ref[h] = jnp.where(first, low, high)
    give_ref[h] = jnp.where(first, high, low).astype(give_ref.dtype)


def state_kernel(count_ref, k_hbm, v_hbm, q_hbm, keep_ref, give_ref, k_ref, v_ref, q_ref, sems):
    copies = fetch(((k_hbm, k_ref), (v_hbm, v_ref), (q_hbm, q_ref)), sems)
    wait(copies[:2])
    running = {}
    for b, h, r, c in tiles(*k_ref.shape):
        state = state_of(count_ref, b, k_ref[r, c], v_ref[r, c])
        running[h] = running[h] + state if b else state
    for h, state in running.items():
        halves(state, h, keep_ref, give_ref)
    wait(copies[2:])


def score_kernel(count_ref, cot_hbm, q_ref, k_ref, v_ref, part_ref, turned_ref, run_ref, cot_ref, sems):
    copies = fetch(((cot_hbm, cot_ref),), sems)
    running = {}
    t = lax.broadcasted_iota(jnp.int32, (SPAN, SPAN), 0)
    s = lax.broadcasted_iota(jnp.int32, (SPAN, SPAN), 1)
    for b, h, r, c in tiles(*q_ref.shape):
        q, k, v = q_ref[r, c], k_ref[r, c], v_ref[r, c]
        state = state_of(count_ref, b, k, v)
        run_ref[b, h] = running[h] if b else jnp.zeros_like(state)
        running[h] = running[h] + state if b else state
        scored = jnp.where(t >= s, nt(q, k), 0.0).astype(BF16)
        part_ref[r, c] = nn(scored, v)
        turned_ref[b, h] = jnp.where(t <= s, nt(k, q), 0.0).astype(BF16)
    wait(copies)


def joined(near_ref, far_ref):
    first = lax.axis_index("loader") == 0
    sums = []
    for h in range(near_ref.shape[0]):
        near, far = near_ref[h], far_ref[h]
        sums.append(jnp.concatenate([jnp.where(first, near, far), jnp.where(first, far, near)], axis=0))
    return sums


def norm_kernel(count_ref, q_ref, cot_ref, gain_ref, part_ref, run_ref, near_ref, far_ref,
                grad_ref, prefix_ref, back_ref, keep_ref, give_ref):
    running = {}
    outside = joined(near_ref, far_ref)
    for b, h, r, c in reversed(list(tiles(*q_ref.shape))):
        prefix = (run_ref[b, h] + outside[h]).astype(BF16)
        prefix_ref[b, h] = prefix
        q = q_ref[r, c]
        raw = part_ref[r, c] + nn(q, prefix)
        inverse = lax.rsqrt(jnp.mean(raw * raw, axis=-1, keepdims=True) + EPSILON)
        gain = gain_ref[:, c]
        gain = jnp.where(b < count_ref[0], gain, jnp.zeros_like(gain))
        weighted = gain * cot_ref[r, c].astype(F32)
        pulled = jnp.mean(weighted * raw, axis=-1, keepdims=True)
        grad = (inverse * weighted - raw * (inverse * inverse * inverse * pulled)).astype(BF16)
        grad_ref[r, c] = grad
        state = tn(q, grad)
        back_ref[b, h] = running.get(h, jnp.zeros_like(state))
        running[h] = running[h] + state if h in running else state
    for h, state in running.items():
        halves(state, h, keep_ref, give_ref)


def value_kernel(grad_ref, turned_ref, gv_ref):
    for b, h, r, c in tiles(*grad_ref.shape):
        gv_ref[r, c] = nn(turned_ref[b, h], grad_ref[r, c])


def pull_kernel(q_ref, k_ref, v_ref, grad_ref, prefix_ref, gq_hbm, gk_ref, gq_ref, sems):
    t = lax.broadcasted_iota(jnp.int32, (SPAN, SPAN), 0)
    s = lax.broadcasted_iota(jnp.int32, (SPAN, SPAN), 1)
    for b, h, r, c in tiles(*q_ref.shape):
        v, grad = v_ref[r, c], grad_ref[r, c]
        pull = jnp.where(t >= s, nt(grad, v), 0.0).astype(BF16)
        gq_ref[r, c] = (nn(pull, k_ref[r, c]) + nt(grad, prefix_ref[b, h])).astype(BF16)
    copies = fetch(((gq_ref, gq_hbm),), sems)
    for b, h, r, c in tiles(*q_ref.shape):
        v, grad = v_ref[r, c], grad_ref[r, c]
        turned = jnp.where(t <= s, nt(v, grad), 0.0).astype(BF16)
        gk_ref[r, c] = nn(turned, q_ref[r, c])
    wait(copies)


def final_kernel(count_ref, k_ref, v_ref, gk_part_ref, gv_part_ref, back_ref, near_ref, far_ref,
                 gk_hbm, gv_hbm, gk_ref, gv_ref, sems):
    heads = k_ref.shape[1] // DH
    outside = joined(near_ref, far_ref)
    copies = []
    for b, h, r, c in tiles(*k_ref.shape):
        suffix = back_ref[b, h] + outside[h]
        suffix = jnp.where(b < count_ref[0], suffix, jnp.zeros_like(suffix)).astype(BF16)
        gk_ref[r, c] = (gk_part_ref[r, c] + nt(v_ref[r, c], suffix)).astype(BF16)
        gv_ref[r, c] = (gv_part_ref[r, c] + nn(k_ref[r, c], suffix)).astype(BF16)
        if h == heads - 1:
            for at, (source, target) in enumerate(((gk_ref, gk_hbm), (gv_ref, gv_hbm))):
                copies.append(pltpu.make_async_copy(source.at[r], target.at[r], sems.at[b, at]))
                copies[-1].start()
    wait(copies)


def place(array, space):
    return array if space is SMEM else pltpu.with_memory_space_constraint(array, space.memory_space)


def call(kernel, ins, outs, flops, scratch=()):
    size = sum(a.size * a.dtype.itemsize for a, _ in ins)
    size += sum(math.prod(shape) * jnp.dtype(kind).itemsize for (shape, kind), _ in outs)
    return pl.pallas_call(
        kernel,
        out_shape=[pltpu.VMEM(*a) if space is VMEM else pltpu.HBM(*a) for a, space in outs],
        in_specs=[space for _, space in ins],
        out_specs=[space for _, space in outs],
        scratch_shapes=scratch,
        cost_estimate=pl.CostEstimate(flops=flops, bytes_accessed=size, transcendentals=0),
        compiler_params=pltpu.CompilerParams(vmem_limit_bytes=16 * 2**20),
    )(*[place(a, space) for a, space in ins])


def radices(count):
    found = []
    for radix in (4, 2):
        while count % radix == 0:
            found.append(radix)
            count //= radix
    return found + [count] if count > 1 else found


def partner(digit, step, radix):
    return digit ^ step if radix in (2, 4) else (digit + step) % radix


def pair_kernel(keep_ref, came_ref, group_ref):
    group_ref[...] = (keep_ref[...] + came_ref[...].astype(F32)).astype(group_ref.dtype)


def combine_kernel(steps, radix, stride, reverse, first, last, *refs):
    refs = list(refs)
    sent_ref, near_ref = refs.pop(), refs.pop()
    keep_ref, beside_ref, group_ref = refs[:3]
    came = refs[3:3 + len(steps)]
    digit = lax.rem(lax.div(lax.axis_index("seq"), stride), radix)
    near = jnp.zeros(near_ref.shape, F32) if first else refs[-1][...]
    whole = group_ref[...].astype(F32)
    for step, piece_ref in zip(steps, came):
        source = partner(digit, step if radix in (2, 4) else radix - step, radix)
        use = source > digit if reverse else source < digit
        piece = piece_ref[...].astype(F32)
        near = near + jnp.where(use, piece, 0.0)
        whole = whole + piece
    if last:
        ahead = lax.axis_index("loader") == (1 if reverse else 0)
        sent_ref[...] = near + jnp.where(ahead, keep_ref[...], 0.0)
        near_ref[...] = near + jnp.where(ahead, 0.0, beside_ref[...].astype(F32))
    else:
        near_ref[...] = near
        sent_ref[...] = whole.astype(sent_ref.dtype)


def order(radix, reverse):
    if radix == 4:
        return [1, 3, 2] if reverse else [1, 3, 2]
    return list(range(radix - 1, 0, -1))


def outside_sum(keep, give, reverse, core_cover, chip_cover):
    swap = [(0, 1), (1, 0)]
    beside, core_cover = lax.optimization_barrier((lax.ppermute(give, "loader", swap), core_cover))
    like = (keep.shape, F32), VMEM
    small = (keep.shape, give.dtype), VMEM
    group, = call(pair_kernel, [(keep, VMEM), (beside, VMEM)], [small], keep.size)
    count, stride, outside = lax.axis_size("seq"), 1, []
    chain = radices(count)
    for at, radix in enumerate(chain):
        steps = order(radix, reverse)
        came = []
        for step in steps:
            pairs = [(s, s + (partner(s // stride % radix, step, radix) - s // stride % radix) * stride)
                     for s in range(count)]
            came.append(lax.ppermute(group, "seq", pairs))
        if at == 0:
            came, chip_cover = lax.optimization_barrier((came, chip_cover))
        last = at + 1 == len(chain)
        kernel = functools.partial(combine_kernel, steps, radix, stride, reverse, at == 0, last)
        near, group = call(
            kernel, [(a, VMEM) for a in (keep, beside, group, *came, *outside)],
            [like, like if last else small], keep.size)
        outside = [near]
        stride *= radix
    far = lax.ppermute(group, "loader", swap)
    return near, far, core_cover, chip_cover


def shards(queries, key_rows, values, cotangent, out_gain, counts):
    rows, width = queries.shape
    blocks, heads = rows // SPAN, width // DH
    unit = 2 * rows * width * DH
    states = ((blocks, heads, DH, DH), F32), VMEM
    prefixes = ((blocks, heads, DH, DH), BF16), VMEM
    keep = ((heads, DH // 2, DH), F32), VMEM
    give = ((heads, DH // 2, DH), BF16), VMEM
    plane = ((rows, width), F32), VMEM
    half = ((rows, width), BF16), VMEM
    result = ((rows, width), BF16), HBM
    square = ((blocks, heads, SPAN, SPAN), BF16), VMEM
    staged = pltpu.VMEM((rows, width), BF16)
    pair_sems = pltpu.SemaphoreType.DMA((blocks, 2))

    def vmem(*arrays):
        return [(a, VMEM) for a in arrays]

    count = [(counts, SMEM)]
    kept, given, k, v, q = call(
        state_kernel, count + [(key_rows, HBM), (values, HBM), (queries, HBM)],
        [keep, give, half, half, half], unit, [pltpu.SemaphoreType.DMA((3,))])
    cover = call(
        score_kernel, count + [(cotangent, HBM)] + vmem(q, k, v),
        [plane, square, states, half], 7 * unit, [pltpu.SemaphoreType.DMA((1,))])
    near, far, _, (part, turned, run, cot) = outside_sum(kept, given, False, [], cover)
    grad, prefix, back, kept, given = call(
        norm_kernel, count + vmem(q, cot, out_gain.reshape(1, width), part, run, near, far),
        [half, prefixes, states, keep, give], 2 * unit)
    core_cover = call(value_kernel, vmem(grad, turned), [plane], 2 * unit)
    cover = call(
        pull_kernel, vmem(q, k, v, grad, prefix), [result, plane], 9 * unit,
        [staged, pltpu.SemaphoreType.DMA((1,))])
    near, far, (gv_part,), (gq, gk_part) = outside_sum(kept, given, True, core_cover, cover)
    gk, gv = call(
        final_kernel, count + vmem(k, v, gk_part, gv_part, back, near, far), [result, result], 2 * unit,
        [staged, staged, pair_sems])
    return gq, gk, gv


def solution(mesh):
    rows = P(("groups", "seq", "loader"), "head")
    return jax.shard_map(
        shards,
        mesh=mesh,
        in_specs=(rows, rows, rows, rows, P("head"), P(("groups", "seq", "loader"))),
        out_specs=(rows, rows, rows),
        check_vma=False,
    )
```

time: 29 us -> 27.9 us (0.962)
  Pallas kernels: 12.4 us -> 9.35 us
  waiting for transfers between devices: 4.74 us -> 6.99 us
  starting transfers between devices: 10.4 us -> 10 us
    pallas_call x7 -> x10, Pallas kernels: 12.4 us -> 9.35 us  [call(): pl.pallas_call(kernel, out_shape=[pltpu.VMEM(*a) if space is VMEM else pl...]
    ppermute x2 -> x4, waiting for transfers between devices: 2.65 us -> 3.9 us  [the longest x2 2.48 us: outside_sum(): far = lax.ppermute(group, 'loader', swap)]
    ppermute x6, starting transfers between devices: 10.2 us -> 9.13 us  [outside_sum(): came.append(lax.ppermute(group, 'seq', pairs))]
    ppermute x6, waiting for transfers between devices: 2.09 us -> 3.09 us  [outside_sum(): came.append(lax.ppermute(group, 'seq', pairs))]
    ppermute x2 -> x4, starting transfers between devices: 0.17 us -> 0.88 us  [the longest x2 0.74 us: outside_sum(): lax.ppermute(give, 'loader', swap)]
  transfers between devices with their start and end apart: 8 -> 10, of which waited for: 4 -> 6; matrix products, arithmetic and copies ran while one was open for 0% -> 0% of each run, Pallas kernels for 26% -> 18%
where the time goes in v3:
time: 27.9 us; the launch traced here: 27.7 us
  starting transfers between devices  10 us (36%)
  Pallas kernels  9.35 us (34%)
  waiting for transfers between devices  6.99 us (25%)
  between operations  1.38 us (5%)
    pallas_call x10, Pallas kernels, call(): pl.pallas_call(kernel, out_shape=[pltpu.VMEM(*a) if space is VMEM else pl...  9.35 us
    ppermute x6, starting transfers between devices, outside_sum(): came.append(lax.ppermute(group, 'seq', pairs))  9.13 us
    ppermute x6, waiting for transfers between devices, outside_sum(): came.append(lax.ppermute(group, 'seq', pairs))  3.09 us
    ppermute x2, waiting for transfers between devices, outside_sum(): far = lax.ppermute(group, 'loader', swap)  2.48 us
    ppermute x2, waiting for transfers between devices, outside_sum(): lax.ppermute(give, 'loader', swap)  1.42 us
    ppermute x2, starting transfers between devices, outside_sum(): lax.ppermute(give, 'loader', swap)  0.74 us
  transfers between devices with their start and end apart: 10, of which 6 were waited for; matrix products, arithmetic and copies ran while one was open for 0% of the time, Pallas kernels for 18%

profile of v3, /device:TPU:0, one launch (start us, length us, event | category | flops | bytes accessed | tf_op | source)
XLA Modules:
  0.0 27.7 jit_solution(846001288728880855)
XLA Ops:
  1.3 1.7 %shard_map.85 = (f32[2,64,128]{2,1,0:T(8,128)S(1)}, bf16[2,64,128]{2,1,0:T(8,128)(2,1)S(1)}, bf16[1280,256]{1,0:T(8,128)(2,1)S(1)}, bf16[1280,256]{1,0:T(8,128)(2,1)S(1)}, bf16[1280,256]{1,0:T(8,128)(2,1)S(1)}) custom-call(s32[1]{0:T(128)S(6)} %copy.9.count_ref, bf16[1280,256]{1,0:T(8,128)(2,1)} %k_hbm.1, bf16[1280,256]{1,0:T(8,128)(2,1)} %v_hbm.1, ...), custom_call_target="tpu_custom_call" | custom-call | flops 83886080 | bytes 4030468 | tf_op jit(solution)/shard_map/pallas_call | solution.py:167
  3.0 0.5 %collective-permute-start = (bf16[2,64,128]{2,1,0:T(8,128)(2,1)S(1)}, bf16[2,64,128]{2,1,0:T(8,128)(2,1)S(1)}, u32[]{:S(2)}, u32[]{:S(2)}) collective-permute-start(bf16[2,64,128]{2,1,0:T(8,128)(2,1)S(1)} %get-tuple-element.41), channel_id=1, source_target_pairs={{0,1},{1,0},{2,3},{3,2},{4,5},{5,4},{6,7},{7,6},{8,9},{9,8},{10,11... | collective-permute-start | bytes 98312 | tf_op jit(solution)/shard_map/ppermute | solution.py:226
  3.5 0.9 %collective-permute-done.came_ref.refs_1_ = bf16[2,64,128]{2,1,0:T(8,128)(2,1)S(1)} collective-permute-done((bf16[2,64,128]{2,1,0:T(8,128)(2,1)S(1)}, bf16[2,64,128]{2,1,0:T(8,128)(2,1)S(1)}, u32[]{:S(2)}, u32[]{:S(2)}) %collective-permute-start) | collective-permute-done | bytes 32800 | tf_op jit(solution)/shard_map/ppermute | solution.py:226
  4.4 4.0 %collective-permute-start.3 = (bf16[2,64,128]{2,1,0:T(8,128)(2,1)S(1)}, bf16[2,64,128]{2,1,0:T(8,128)(2,1)S(1)}, u32[]{:S(2)}, u32[]{:S(2)}) collective-permute-start(bf16[2,64,128]{2,1,0:T(8,128)(2,1)S(1)} %shard_map.86.refs_2_), channel_id=1, source_target_pairs={{0,8},{4,12},{8,0},{12,4},{1,9},{5,13},{9,1},{13,5},{2,10},{6,14},... | collective-permute-start | bytes 98312 | tf_op jit(solution)/shard_map/ppermute | solution.py:238
  8.4 1.3 %collective-permute-start.2 = (bf16[2,64,128]{2,1,0:T(8,128)(2,1)S(1)}, bf16[2,64,128]{2,1,0:T(8,128)(2,1)S(1)}, u32[]{:S(2)}, u32[]{:S(2)}) collective-permute-start(bf16[2,64,128]{2,1,0:T(8,128)(2,1)S(1)} %shard_map.86.refs_2_), channel_id=1, source_target_pairs={{0,12},{4,8},{8,4},{12,0},{1,13},{5,9},{9,5},{13,1},{2,14},{6,10},... | collective-permute-start | bytes 98312 | tf_op jit(solution)/shard_map/ppermute | solution.py:238
  9.7 0.2 collective-permute-start.1
  10.0 0.0 copy-start
  10.0 2.3 %shard_map.87 = (f32[1280,256]{1,0:T(8,128)S(1)}, bf16[5,2,256,256]{3,2,1,0:T(8,128)(2,1)S(1)}, f32[5,2,128,128]{3,2,1,0:T(8,128)S(1)}, bf16[1280,256]{1,0:T(8,128)(2,1)S(1)}) custom-call(s32[1]{0:T(128)S(6)} %copy.9.count_ref, bf16[1280,256]{1,0:T(8,128)(2,1)} %cot_hbm.1, bf16[1280,256]{1,0:T(8,128)(2,1)S(1)} %get-tuple-element.39.q_ref, ...), custom_call_target="tpu_custom_call" | custom-call | flops 587202560 | bytes 6553604 | tf_op jit(solution)/shard_map/pallas_call | solution.py:167
  12.3 0.0 collective-permute-done.3.refs_5_
  12.3 1.8 %collective-permute-done.2.refs_4_ = bf16[2,64,128]{2,1,0:T(8,128)(2,1)S(1)} collective-permute-done((bf16[2,64,128]{2,1,0:T(8,128)(2,1)S(1)}, bf16[2,64,128]{2,1,0:T(8,128)(2,1)S(1)}, u32[]{:S(2)}, u32[]{:S(2)}) %collective-permute-start.2) | collective-permute-done | bytes 32800 | tf_op jit(solution)/shard_map/ppermute | solution.py:238
  14.1 0.0 collective-permute-done.1.refs_3_
  14.1 0.1 collective-permute-start.4
  14.2 1.2 %collective-permute-done.4.far_ref = f32[2,64,128]{2,1,0:T(8,128)S(1)} collective-permute-done((f32[2,64,128]{2,1,0:T(8,128)S(1)}, f32[2,64,128]{2,1,0:T(8,128)S(1)}, u32[]{:S(2)}, u32[]{:S(2)}) %collective-permute-start.4) | collective-permute-done | bytes 65568 | tf_op jit(solution)/shard_map/ppermute | solution.py:248
  15.5 0.0 copy-done
  15.5 1.2 %shard_map.89 = (bf16[1280,256]{1,0:T(8,128)(2,1)S(1)}, bf16[5,2,128,128]{3,2,1,0:T(8,128)(2,1)S(1)}, f32[5,2,128,128]{3,2,1,0:T(8,128)S(1)}, f32[2,64,128]{2,1,0:T(8,128)S(1)}, bf16[2,64,128]{2,1,0:T(8,128)(2,1)S(1)}) custom-call(s32[1]{0:T(128)S(6)} %copy.9.count_ref, bf16[1280,256]{1,0:T(8,128)(2,1)S(1)} %get-tuple-element.39.q_ref, ...), custom_call_target="tpu_custom_call" | custom-call | flops 167772160 | bytes 5145604 | tf_op jit(solution)/shard_map/pallas_call | solution.py:167
  16.7 0.2 collective-permute-start.5
  16.9 0.5 %shard_map.90.gv_part_ref = f32[1280,256]{1,0:T(8,128)S(1)} custom-call(bf16[1280,256]{1,0:T(8,128)(2,1)S(1)} %get-tuple-element.58.grad_ref, bf16[5,2,256,256]{3,2,1,0:T(8,128)(2,1)S(1)} %get-tuple-element.59.turned_ref), custom_call_target="tpu_custom_call" | custom-call | flops 167772160 | bytes 3276800 | tf_op jit(solution)/shard_map/pallas_call | solution.py:167
  17.4 0.6 %collective-permute-done.5.came_ref.refs_1_ = bf16[2,64,128]{2,1,0:T(8,128)(2,1)S(1)} collective-permute-done((bf16[2,64,128]{2,1,0:T(8,128)(2,1)S(1)}, bf16[2,64,128]{2,1,0:T(8,128)(2,1)S(1)}, u32[]{:S(2)}, u32[]{:S(2)}) %collective-permute-start.5) | collective-permute-done | bytes 32800 | tf_op jit(solution)/shard_map/ppermute | solution.py:226
  18.0 1.3 %collective-permute-start.8 = (bf16[2,64,128]{2,1,0:T(8,128)(2,1)S(1)}, bf16[2,64,128]{2,1,0:T(8,128)(2,1)S(1)}, u32[]{:S(2)}, u32[]{:S(2)}) collective-permute-start(bf16[2,64,128]{2,1,0:T(8,128)(2,1)S(1)} %shard_map.91.refs_2_), channel_id=1, source_target_pairs={{0,8},{4,12},{8,0},{12,4},{1,9},{5,13},{9,1},{13,5},{2,10},{6,14},... | collective-permute-start | bytes 98312 | tf_op jit(solution)/shard_map/ppermute | solution.py:238
  19.3 1.2 %collective-permute-start.7 = (bf16[2,64,128]{2,1,0:T(8,128)(2,1)S(1)}, bf16[2,64,128]{2,1,0:T(8,128)(2,1)S(1)}, u32[]{:S(2)}, u32[]{:S(2)}) collective-permute-start(bf16[2,64,128]{2,1,0:T(8,128)(2,1)S(1)} %shard_map.91.refs_2_), channel_id=1, source_target_pairs={{0,12},{4,8},{8,4},{12,0},{1,13},{5,9},{9,5},{13,1},{2,14},{6,10},... | collective-permute-start | bytes 98312 | tf_op jit(solution)/shard_map/ppermute | solution.py:238
  20.5 1.1 %collective-permute-start.6 = (bf16[2,64,128]{2,1,0:T(8,128)(2,1)S(1)}, bf16[2,64,128]{2,1,0:T(8,128)(2,1)S(1)}, u32[]{:S(2)}, u32[]{:S(2)}) collective-permute-start(bf16[2,64,128]{2,1,0:T(8,128)(2,1)S(1)} %shard_map.91.refs_2_), channel_id=1, source_target_pairs={{0,4},{4,0},{8,12},{12,8},{1,5},{5,1},{9,13},{13,9},{2,6},{6,2},{1... | collective-permute-start | bytes 98312 | tf_op jit(solution)/shard_map/ppermute | solution.py:238
  21.6 2.1 %shard_map.92 = (bf16[1280,256]{1,0:T(8,128)(2,1)}, f32[1280,256]{1,0:T(8,128)S(1)}) custom-call(bf16[1280,256]{1,0:T(8,128)(2,1)S(1)} %get-tuple-element.39.q_ref, bf16[1280,256]{1,0:T(8,128)(2,1)S(1)} %get-tuple-element.42.k_ref, bf16[1280,256]{1,0:T(8,128)(2,1)S(1)} %get-tuple-element.43.v_ref, bf16[1280,256]{1,0:T(8,128)(2,1)S(1)} %get-tuple-element.58.grad_ref, ...), custom_call_target="tpu_custom_call" | custom-call | flops 754974720 | bytes 4915200 | tf_op jit(solution)/shard_map/pallas_call | solution.py:167
  23.7 0.0 collective-permute-done.8.refs_5_
  23.7 1.3 %collective-permute-done.7.refs_4_ = bf16[2,64,128]{2,1,0:T(8,128)(2,1)S(1)} collective-permute-done((bf16[2,64,128]{2,1,0:T(8,128)(2,1)S(1)}, bf16[2,64,128]{2,1,0:T(8,128)(2,1)S(1)}, u32[]{:S(2)}, u32[]{:S(2)}) %collective-permute-start.7) | collective-permute-done | bytes 32800 | tf_op jit(solution)/shard_map/ppermute | solution.py:238
  25.0 0.0 collective-permute-done.6.refs_3_
  25.1 0.1 collective-permute-start.9
  25.1 1.2 %collective-permute-done.9.far_ref = f32[2,64,128]{2,1,0:T(8,128)S(1)} collective-permute-done((f32[2,64,128]{2,1,0:T(8,128)S(1)}, f32[2,64,128]{2,1,0:T(8,128)S(1)}, u32[]{:S(2)}, u32[]{:S(2)}) %collective-permute-start.9) | collective-permute-done | bytes 65568 | tf_op jit(solution)/shard_map/ppermute | solution.py:248
  26.4 1.3 %shard_map.94 = (bf16[1280,256]{1,0:T(8,128)(2,1)}, bf16[1280,256]{1,0:T(8,128)(2,1)}) custom-call(s32[1]{0:T(128)S(6)} %copy.9.count_ref, bf16[1280,256]{1,0:T(8,128)(2,1)S(1)} %get-tuple-element.42.k_ref, bf16[1280,256]{1,0:T(8,128)(2,1)S(1)} %get-tuple-element.43.v_ref, f32[1280,256]{1,0:T(8,128)S(1)} %get-tuple-element.65.gk_part_ref, ...), custom_call_target="tpu_custom_call" | custom-call | flops 167772160 | bytes 6029316 | tf_op jit(solution)/shard_map/pallas_call | solution.py:167
  (4 shorter events, 0.1 us)
Async XLA Ops:
  3.0 1.4 %collective-permute-start = (bf16[2,64,128]{2,1,0:T(8,128)(2,1)S(1)}, bf16[2,64,128]{2,1,0:T(8,128)(2,1)S(1)}, u32[]{:S(2)}, u32[]{:S(2)}) collective-permute-start(bf16[2,64,128]{2,1,0:T(8,128)(2,1)S(1)} %get-tuple-element.41), channel_id=1, source_target_pairs={{0,1},{1,0},{2,3},{3,2},{4,5},{5,4},{6,7},{7,6},{8,9},{9,8},{10,11... | collective-permute-start | bytes 98312 | tf_op jit(solution)/shard_map/ppermute | solution.py:226
  4.4 7.9 %collective-permute-start.3 = (bf16[2,64,128]{2,1,0:T(8,128)(2,1)S(1)}, bf16[2,64,128]{2,1,0:T(8,128)(2,1)S(1)}, u32[]{:S(2)}, u32[]{:S(2)}) collective-permute-start(bf16[2,64,128]{2,1,0:T(8,128)(2,1)S(1)} %shard_map.86.refs_2_), channel_id=1, source_target_pairs={{0,8},{4,12},{8,0},{12,4},{1,9},{5,13},{9,1},{13,5},{2,10},{6,14},... | collective-permute-start | bytes 98312 | tf_op jit(solution)/shard_map/ppermute | solution.py:238
  8.4 5.7 %collective-permute-start.2 = (bf16[2,64,128]{2,1,0:T(8,128)(2,1)S(1)}, bf16[2,64,128]{2,1,0:T(8,128)(2,1)S(1)}, u32[]{:S(2)}, u32[]{:S(2)}) collective-permute-start(bf16[2,64,128]{2,1,0:T(8,128)(2,1)S(1)} %shard_map.86.refs_2_), channel_id=1, source_target_pairs={{0,12},{4,8},{8,4},{12,0},{1,13},{5,9},{9,5},{13,1},{2,14},{6,10},... | collective-permute-start | bytes 98312 | tf_op jit(solution)/shard_map/ppermute | solution.py:238
  9.7 4.4 %collective-permute-start.1 = (bf16[2,64,128]{2,1,0:T(8,128)(2,1)S(1)}, bf16[2,64,128]{2,1,0:T(8,128)(2,1)S(1)}, u32[]{:S(2)}, u32[]{:S(2)}) collective-permute-start(bf16[2,64,128]{2,1,0:T(8,128)(2,1)S(1)} %shard_map.86.refs_2_), channel_id=1, source_target_pairs={{0,4},{4,0},{8,12},{12,8},{1,5},{5,1},{9,13},{13,9},{2,6},{6,2},{1... | collective-permute-start | bytes 98312 | tf_op jit(solution)/shard_map/ppermute | solution.py:238
  10.0 5.5 %copy-start = (f32[256]{0:T(256)S(1)}, f32[256]{0:T(256)}, u32[]{:S(2)}) copy-start(f32[256]{0:T(256)} %param.10) | copy-start | bytes 3076
  14.1 1.3 %collective-permute-start.4 = (f32[2,64,128]{2,1,0:T(8,128)S(1)}, f32[2,64,128]{2,1,0:T(8,128)S(1)}, u32[]{:S(2)}, u32[]{:S(2)}) collective-permute-start(f32[2,64,128]{2,1,0:T(8,128)S(1)} %get-tuple-element.55), channel_id=1, source_target_pairs={{0,1},{1,0},{2,3},{3,2},{4,5},{5,4},{6,7},{7,6},{8,9},{9,8},{10,11... | collective-permute-start | bytes 196616 | tf_op jit(solution)/shard_map/ppermute | solution.py:248
  16.7 1.3 %collective-permute-start.5 = (bf16[2,64,128]{2,1,0:T(8,128)(2,1)S(1)}, bf16[2,64,128]{2,1,0:T(8,128)(2,1)S(1)}, u32[]{:S(2)}, u32[]{:S(2)}) collective-permute-start(bf16[2,64,128]{2,1,0:T(8,128)(2,1)S(1)} %get-tuple-element.57), channel_id=1, source_target_pairs={{0,1},{1,0},{2,3},{3,2},{4,5},{5,4},{6,7},{7,6},{8,9},{9,8},{10,11... | collective-permute-start | bytes 98312 | tf_op jit(solution)/shard_map/ppermute | solution.py:226
  18.0 5.7 %collective-permute-start.8 = (bf16[2,64,128]{2,1,0:T(8,128)(2,1)S(1)}, bf16[2,64,128]{2,1,0:T(8,128)(2,1)S(1)}, u32[]{:S(2)}, u32[]{:S(2)}) collective-permute-start(bf16[2,64,128]{2,1,0:T(8,128)(2,1)S(1)} %shard_map.91.refs_2_), channel_id=1, source_target_pairs={{0,8},{4,12},{8,0},{12,4},{1,9},{5,13},{9,1},{13,5},{2,10},{6,14},... | collective-permute-start | bytes 98312 | tf_op jit(solution)/shard_map/ppermute | solution.py:238
  19.3 5.7 %collective-permute-start.7 = (bf16[2,64,128]{2,1,0:T(8,128)(2,1)S(1)}, bf16[2,64,128]{2,1,0:T(8,128)(2,1)S(1)}, u32[]{:S(2)}, u32[]{:S(2)}) collective-permute-start(bf16[2,64,128]{2,1,0:T(8,128)(2,1)S(1)} %shard_map.91.refs_2_), channel_id=1, source_target_pairs={{0,12},{4,8},{8,4},{12,0},{1,13},{5,9},{9,5},{13,1},{2,14},{6,10},... | collective-permute-start | bytes 98312 | tf_op jit(solution)/shard_map/ppermute | solution.py:238
  20.5 4.6 %collective-permute-start.6 = (bf16[2,64,128]{2,1,0:T(8,128)(2,1)S(1)}, bf16[2,64,128]{2,1,0:T(8,128)(2,1)S(1)}, u32[]{:S(2)}, u32[]{:S(2)}) collective-permute-start(bf16[2,64,128]{2,1,0:T(8,128)(2,1)S(1)} %shard_map.91.refs_2_), channel_id=1, source_target_pairs={{0,4},{4,0},{8,12},{12,8},{1,5},{5,1},{9,13},{13,9},{2,6},{6,2},{1... | collective-permute-start | bytes 98312 | tf_op jit(solution)/shard_map/ppermute | solution.py:238
  25.1 1.3 %collective-permute-start.9 = (f32[2,64,128]{2,1,0:T(8,128)S(1)}, f32[2,64,128]{2,1,0:T(8,128)S(1)}, u32[]{:S(2)}, u32[]{:S(2)}) collective-permute-start(f32[2,64,128]{2,1,0:T(8,128)S(1)} %get-tuple-element.72), channel_id=1, source_target_pairs={{0,1},{1,0},{2,3},{3,2},{4,5},{5,4},{6,7},{7,6},{8,9},{9,8},{10,11... | collective-permute-start | bytes 196616 | tf_op jit(solution)/shard_map/ppermute | solution.py:248

commit v4 on v2

v4 whole, which is shorter than its diff:
```python
import functools
import math

import jax
import jax.numpy as jnp
from jax import lax
from jax.experimental import pallas as pl
from jax.experimental.pallas import tpu as pltpu
from jax.sharding import PartitionSpec as P

DH = 128
SPAN = 256
LIVE = 6
EPSILON = 1e-06
F32 = jnp.float32
BF16 = jnp.bfloat16
VMEM = pl.BlockSpec(memory_space=pltpu.VMEM)
SMEM = pl.BlockSpec(memory_space=pltpu.SMEM)
HBM = pl.BlockSpec(memory_space=pltpu.HBM)
SWAP = [(0, 1), (1, 0)]


def nn(a, b):
    return lax.dot_general(a, b, (((1,), (0,)), ((), ())), preferred_element_type=F32)


def nt(a, b):
    return lax.dot_general(a, b, (((1,), (1,)), ((), ())), preferred_element_type=F32)


def tn(a, b):
    return lax.dot_general(a, b, (((0,), (0,)), ((), ())), preferred_element_type=F32)


def rows_of(block):
    if isinstance(block, int):
        return slice(block * SPAN, (block + 1) * SPAN)
    return pl.ds(pl.multiple_of(block * SPAN, SPAN), SPAN)


def columns_of(core):
    return pl.ds(pl.multiple_of(core * DH, DH), DH)


def fetch(pairs, sems):
    copies = [pltpu.make_async_copy(source, target, sems.at[at]) for at, (source, target) in enumerate(pairs)]
    for copy in copies:
        copy.start()
    return copies


def wait(copies):
    for copy in copies:
        copy.wait()


def core_and_counts(count_ref):
    core, own = lax.axis_index("loader"), count_ref[0]
    return core, jnp.where(core == 0, own, LIVE - own), own


def live_block(own_ref, other_ref, at, core, count):
    late = (at >= count).astype(jnp.int32)
    r = rows_of(at - late * count)
    c = columns_of(core) if other_ref.shape[1] > DH else slice(None)
    return jnp.where(late == core, own_ref[r, :], other_ref[r, c])


def load_kernel(k_hbm, v_hbm, q_hbm, cot_hbm, gain_hbm,
                k_ref, v_ref, q_ref, cot_ref, give_ref, gain_ref, sems):
    core = lax.axis_index("loader")
    own, other = columns_of(core), columns_of(1 - core)
    wait(fetch(((k_hbm.at[:, own], k_ref), (v_hbm.at[:, own], v_ref), (q_hbm.at[:, own], q_ref),
                (cot_hbm.at[:, own], cot_ref), (q_hbm.at[:, other], give_ref.at[0]),
                (cot_hbm.at[:, other], give_ref.at[1]), (gain_hbm, gain_ref)), sems))


def state_kernel(count_ref, k_own_ref, v_own_ref, k_other_ref, v_other_ref, total_ref, k_ref, v_ref, run_ref):
    core, count, _ = core_and_counts(count_ref)
    running = jnp.zeros((DH, DH), F32)
    for at in range(LIVE):
        r = rows_of(at)
        k = live_block(k_own_ref, k_other_ref, at, core, count)
        v = live_block(v_own_ref, v_other_ref, at, core, count)
        k_ref[r, :], v_ref[r, :] = k, v
        run_ref[at] = running
        running = running + tn(k, v)
    total_ref[...] = running.astype(total_ref.dtype)


def score_kernel(count_ref, q_own_ref, cot_own_ref, other_ref, k_ref, v_ref,
                 q_ref, cot_ref, part_ref, turned_ref):
    core, count, _ = core_and_counts(count_ref)
    t = lax.broadcasted_iota(jnp.int32, (SPAN, SPAN), 0)
    s = lax.broadcasted_iota(jnp.int32, (SPAN, SPAN), 1)
    for at in range(LIVE):
        r = rows_of(at)
        q = live_block(q_own_ref, other_ref.at[0], at, core, count)
        q_ref[r, :] = q
        cot_ref[r, :] = live_block(cot_own_ref, other_ref.at[1], at, core, count)
        k = k_ref[r, :]
        scored = jnp.where(t >= s, nt(q, k), 0.0).astype(BF16)
        part_ref[r, :] = nn(scored, v_ref[r, :])
        turned_ref[at] = jnp.where(t <= s, nt(k, q), 0.0).astype(BF16)


def norm_kernel(q_ref, cot_ref, gain_ref, part_ref, run_ref, outside_ref,
                grad_ref, prefix_ref, back_ref, total_ref):
    outside = outside_ref[...]
    gain = gain_ref[:, columns_of(lax.axis_index("loader"))]
    running = jnp.zeros((DH, DH), F32)
    for at in reversed(range(LIVE)):
        r = rows_of(at)
        prefix = (run_ref[at] + outside).astype(BF16)
        prefix_ref[at] = prefix
        q = q_ref[r, :]
        raw = part_ref[r, :] + nn(q, prefix)
        inverse = lax.rsqrt(jnp.mean(raw * raw, axis=-1, keepdims=True) + EPSILON)
        weighted = gain * cot_ref[r, :].astype(F32)
        pulled = jnp.mean(weighted * raw, axis=-1, keepdims=True)
        grad = (inverse * weighted - raw * (inverse * inverse * inverse * pulled)).astype(BF16)
        grad_ref[r, :] = grad
        back_ref[at] = running
        running = running + tn(q, grad)
    total_ref[...] = running.astype(total_ref.dtype)


def spread(live_ref, own_ref, other_ref, core, count, own):
    for b in range(own_ref.shape[0] // SPAN):
        for target, shift, limit in (
                (own_ref, jnp.where(core == 0, 0, count), own),
                (other_ref, jnp.where(core == 0, count, 0), LIVE - own)):
            block = live_ref[rows_of(jnp.minimum(b + shift, LIVE - 1)), :]
            target[rows_of(b), :] = jnp.where(b < limit, block, jnp.zeros_like(block))


def pull_kernel(count_ref, q_ref, k_ref, v_ref, grad_ref, turned_ref, prefix_ref,
                gq_own_ref, other_ref, gk_ref, gv_ref, gq_ref):
    t = lax.broadcasted_iota(jnp.int32, (SPAN, SPAN), 0)
    s = lax.broadcasted_iota(jnp.int32, (SPAN, SPAN), 1)
    for at in range(LIVE):
        r = rows_of(at)
        v, grad = v_ref[r, :], grad_ref[r, :]
        pull = jnp.where(t >= s, nt(grad, v), 0.0).astype(BF16)
        gq_ref[r, :] = (nn(pull, k_ref[r, :]) + nt(grad, prefix_ref[at])).astype(BF16)
        turned = jnp.where(t <= s, nt(v, grad), 0.0).astype(BF16)
        gk_ref[r, :] = nn(turned, q_ref[r, :])
        gv_ref[r, :] = nn(turned_ref[at], grad)
    spread(gq_ref, gq_own_ref, other_ref.at[0], *core_and_counts(count_ref))


def suffix_kernel(count_ref, k_ref, v_ref, gk_part_ref, gv_part_ref, back_ref, outside_ref, begun_ref,
                  gk_own_ref, gv_own_ref, other_ref, gk_ref, gv_ref):
    del begun_ref
    outside = outside_ref[...]
    for at in range(LIVE):
        r = rows_of(at)
        suffix = (back_ref[at] + outside).astype(BF16)
        gk_ref[r, :] = (gk_part_ref[r, :] + nt(v_ref[r, :], suffix)).astype(BF16)
        gv_ref[r, :] = (gv_part_ref[r, :] + nn(k_ref[r, :], suffix)).astype(BF16)
    where = core_and_counts(count_ref)
    spread(gk_ref, gk_own_ref, other_ref.at[1], *where)
    spread(gv_ref, gv_own_ref, other_ref.at[2], *where)


def own_kernel(gq_own_ref, gk_own_ref, gv_own_ref, gq_hbm, gk_hbm, gv_hbm, sems):
    c = columns_of(lax.axis_index("loader"))
    wait(fetch(((gq_own_ref, gq_hbm.at[:, c]), (gk_own_ref, gk_hbm.at[:, c]), (gv_own_ref, gv_hbm.at[:, c])), sems))


def came_kernel(came_ref, gq_in_hbm, gk_in_hbm, gv_in_hbm, gq_hbm, gk_hbm, gv_hbm, sems):
    del gq_in_hbm, gk_in_hbm, gv_in_hbm
    c = columns_of(1 - lax.axis_index("loader"))
    wait(fetch([(came_ref.at[at], target.at[:, c]) for at, target in enumerate((gq_hbm, gk_hbm, gv_hbm))], sems))


def call(kernel, ins, outs, flops, scratch=(), aliases={}):
    size = sum(a.size * a.dtype.itemsize for a, _ in ins)
    size += sum(math.prod(shape) * jnp.dtype(kind).itemsize for (shape, kind), _ in outs)
    return pl.pallas_call(
        kernel,
        out_shape=[pltpu.VMEM(*a) if space is VMEM else pltpu.HBM(*a) for a, space in outs],
        in_specs=[space for _, space in ins],
        out_specs=[space for _, space in outs],
        scratch_shapes=scratch,
        input_output_aliases=aliases,
        cost_estimate=pl.CostEstimate(flops=flops, bytes_accessed=size, transcendentals=0),
        compiler_params=pltpu.CompilerParams(vmem_limit_bytes=16 * 2**20),
    )(*[a if space is SMEM else pltpu.with_memory_space_constraint(a, space.memory_space) for a, space in ins])


def radices(count):
    found = []
    for radix in (4, 2):
        while count % radix == 0:
            found.append(radix)
            count //= radix
    return found + [count] if count > 1 else found


def partner(digit, step, radix):
    return digit ^ step if radix in (2, 4) else (digit + step) % radix


def combine_kernel(steps, radix, stride, reverse, first, last, *refs):
    group_ref, came, outs = refs[0], refs[1:1 + len(steps)], refs[1 + len(steps) + (not first):]
    digit = lax.rem(lax.div(lax.axis_index("seq"), stride), radix)
    outside = jnp.zeros(outs[0].shape, F32) if first else refs[1 + len(steps)][...]
    whole = group_ref[...].astype(F32)
    for step, piece_ref in zip(steps, came):
        source = partner(digit, step if radix in (2, 4) else radix - step, radix)
        use = source > digit if reverse else source < digit
        piece = piece_ref[...].astype(F32)
        outside = outside + jnp.where(use, piece, 0.0)
        whole = whole + piece
    outs[0][...] = outside
    if not last:
        outs[1][...] = whole.astype(outs[1].dtype)


def order(radix, reverse):
    return [3, 2, 1] if radix == 4 else list(range(radix - 1, 0, -1))


def outside_sum(total, reverse, cover):
    count, stride, group, outside = lax.axis_size("seq"), 1, total, []
    chain = radices(count)
    for at, radix in enumerate(chain):
        steps = order(radix, reverse)
        came = []
        for step in steps:
            pairs = [(s, s + (partner(s // stride % radix, step, radix) - s // stride % radix) * stride)
                     for s in range(count)]
            came.append(lax.ppermute(group, "seq", pairs))
        if at == 0:
            came, cover = lax.optimization_barrier((came, cover))
        last = at + 1 == len(chain)
        kernel = functools.partial(combine_kernel, steps, radix, stride, reverse, at == 0, last)
        sums = [((total.shape, F32), VMEM)] + ([] if last else [((total.shape, total.dtype), VMEM)])
        out = call(kernel, [(a, VMEM) for a in (group, *came, *outside)], sums, total.size)
        outside, group = out[:1], out[-1]
        stride *= radix
    return outside[0], cover


def shards(queries, key_rows, values, cotangent, out_gain, counts):
    rows, width = queries.shape
    unit = 2 * LIVE * SPAN * DH * DH
    buffer = ((rows, DH), BF16), VMEM
    half = ((LIVE * SPAN, DH), BF16), VMEM
    plane = ((LIVE * SPAN, DH), F32), VMEM
    states = ((LIVE, DH, DH), F32), VMEM
    prefixes = ((LIVE, DH, DH), BF16), VMEM
    total = ((DH, DH), BF16), VMEM
    square = ((LIVE, SPAN, SPAN), BF16), VMEM
    result = ((rows, width), BF16), HBM
    staged = pltpu.VMEM((LIVE * SPAN, DH), BF16)
    count = [(counts, SMEM)]

    def vmem(*arrays):
        return [(a, VMEM) for a in arrays]

    def sems(n):
        return pltpu.SemaphoreType.DMA((n,))

    def swap(array):
        return lax.ppermute(array, "loader", SWAP)

    k_other, v_other = swap(key_rows), swap(values)
    pair = ((2, rows, DH), BF16), VMEM
    loaded = call(
        load_kernel, [(a, HBM) for a in (key_rows, values, queries, cotangent, out_gain.reshape(1, width))],
        [buffer] * 4 + [pair, (((1, width), F32), VMEM)], 0, [sems(7)])
    k_other, v_other, loaded = lax.optimization_barrier((k_other, v_other, loaded))
    k_own, v_own, q_own, cot_own, give, gain = loaded
    own, k, v, run = call(
        state_kernel, count + vmem(k_own, v_own, k_other, v_other), [total, half, half, states], unit)
    cover = call(
        score_kernel, count + vmem(q_own, cot_own, swap(give), k, v), [half, half, plane, square], 6 * unit)
    outside, (q, cot, part, turned) = outside_sum(own, False, cover)
    grad, prefix, back, own_back = call(
        norm_kernel, vmem(q, cot, gain, part, run, outside),
        [half, prefixes, states, total], 2 * unit)
    three = ((3, rows, DH), BF16), VMEM
    cover = call(
        pull_kernel, count + vmem(q, k, v, grad, turned, prefix), [buffer, three, plane, plane], 11 * unit, [staged])
    outside, (gq_own, other, gk_part, gv_part) = outside_sum(own_back, True, cover)
    gk_own, gv_own, other = call(
        suffix_kernel, count + vmem(k, v, gk_part, gv_part, back, outside, other),
        [buffer, buffer, three], 2 * unit, [staged, staged], {7: 2})
    came = swap(other)
    grads = call(own_kernel, vmem(gq_own, gk_own, gv_own), [result] * 3, 0, [sems(3)])
    came, grads = lax.optimization_barrier((came, grads))
    return tuple(call(
        came_kernel, vmem(came) + [(grad, HBM) for grad in grads], [result] * 3, 0, [sems(3)], {1: 0, 2: 1, 3: 2}))


def solution(mesh):
    rows = P(("groups", "seq", "loader"), "head")
    return jax.shard_map(
        shards,
        mesh=mesh,
        in_specs=(rows, rows, rows, rows, P("head"), P(("groups", "seq", "loader"))),
        out_specs=(rows, rows, rows),
        check_vma=False,
    )
```

time: 29 us -> 27.1 us (0.934)
  Pallas kernels: 12.4 us -> 8.43 us
  waiting for transfers between devices: 4.74 us -> 6.23 us
  starting transfers between devices: 10.4 us -> 11 us
    pallas_call x7 -> x10, Pallas kernels: 12.4 us -> 8.43 us  [call(): pl.pallas_call(kernel, out_shape=[pltpu.VMEM(*a) if space is VMEM else pl...]
    ppermute x6, waiting for transfers between devices: 2.09 us -> 3.4 us  [outside_sum(): came.append(lax.ppermute(group, 'seq', pairs))]
    ppermute x2 -> x4, starting transfers between devices: 0.17 us -> 1.04 us  [swap(): return lax.ppermute(array, 'loader', SWAP)]
    ppermute x2 -> x4, waiting for transfers between devices: 2.65 us -> 2.83 us  [swap(): return lax.ppermute(array, 'loader', SWAP)]
  transfers between devices with their start and end apart: 8 -> 10, of which waited for: 4 -> 7; matrix products, arithmetic and copies ran while one was open for 0% -> 0% of each run, Pallas kernels for 26% -> 22%
where the time goes in v4:
time: 27.1 us; the launch traced here: 27 us
  starting transfers between devices  11 us (41%)
  Pallas kernels  8.43 us (31%)
  waiting for transfers between devices  6.23 us (23%)
  between operations  1.37 us (5%)
    ppermute x6, starting transfers between devices, outside_sum(): came.append(lax.ppermute(group, 'seq', pairs))  9.92 us
    pallas_call x10, Pallas kernels, call(): pl.pallas_call(kernel, out_shape=[pltpu.VMEM(*a) if space is VMEM else pl...  8.43 us
    ppermute x6, waiting for transfers between devices, outside_sum(): came.append(lax.ppermute(group, 'seq', pairs))  3.4 us
    ppermute x4, waiting for transfers between devices, swap(): return lax.ppermute(array, 'loader', SWAP)  2.83 us
    ppermute x4, starting transfers between devices, swap(): return lax.ppermute(array, 'loader', SWAP)  1.04 us
  transfers between devices with their start and end apart: 10, of which 7 were waited for; matrix products, arithmetic and copies ran while one was open for 0% of the time, Pallas kernels for 22%

profile of v4, /device:TPU:0, one launch (start us, length us, event | category | flops | bytes accessed | tf_op | source)
XLA Modules:
  0.0 27.0 jit_solution(8153061183799706043)
XLA Ops:
  0.6 0.5 %collective-permute-start = (bf16[1280,256]{1,0:T(8,128)(2,1)}, bf16[1280,256]{1,0:T(8,128)(2,1)S(1)}, u32[]{:S(2)}, u32[]{:S(2)}) collective-permute-start(bf16[1280,256]{1,0:T(8,128)(2,1)} %k_hbm.1), channel_id=1, source_target_pairs={{0,1},{1,0},{2,3},{3,2},{4,5},{5,4},{6,7},{7,6},{8,9},{9,8},{10,11... | collective-permute-start | bytes 1966088 | tf_op jit(solution)/shard_map/ppermute | solution.py:267
  1.1 0.1 collective-permute-start.1
  1.2 1.5 %shard_map.85 = (bf16[1280,128]{1,0:T(8,128)(2,1)S(1)}, bf16[1280,128]{1,0:T(8,128)(2,1)S(1)}, bf16[1280,128]{1,0:T(8,128)(2,1)S(1)}, bf16[1280,128]{1,0:T(8,128...) custom-call(bf16[1280,256]{1,0:T(8,128)(2,1)} %k_hbm.1, bf16[1280,256]{1,0:T(8,128)(2,1)} %v_hbm.1, ...), custom_call_target="tpu_custom_call" | custom-call | bytes 4589568 | tf_op jit(solution)/shard_map/pallas_call | solution.py:180
  2.8 0.3 %collective-permute-done.k_other_ref = bf16[1280,256]{1,0:T(8,128)(2,1)S(1)} collective-permute-done((bf16[1280,256]{1,0:T(8,128)(2,1)}, bf16[1280,256]{1,0:T(8,128)(2,1)S(1)}, u32[]{:S(2)}, u32[]{:S(2)}) %collective-permute-start) | collective-permute-done | bytes 655392 | tf_op jit(solution)/shard_map/ppermute | solution.py:267
  3.1 0.9 %collective-permute-done.1.v_other_ref = bf16[1280,256]{1,0:T(8,128)(2,1)S(1)} collective-permute-done((bf16[1280,256]{1,0:T(8,128)(2,1)}, bf16[1280,256]{1,0:T(8,128)(2,1)S(1)}, u32[]{:S(2)}, u32[]{:S(2)}) %collective-permute-start.1) | collective-permute-done | bytes 655392 | tf_op jit(solution)/shard_map/ppermute | solution.py:267
  4.0 0.4 %collective-permute-start.5 = (bf16[2,1280,128]{2,1,0:T(8,128)(2,1)S(1)}, bf16[2,1280,128]{2,1,0:T(8,128)(2,1)S(1)}, u32[]{:S(2)}, u32[]{:S(2)}) collective-permute-start(bf16[2,1280,128]{2,1,0:T(8,128)(2,1)S(1)} %get-tuple-element.72), channel_id=1, source_target_pairs={{0,1},{1,0},{2,3},{3,2},{4,5},{5,4},{6,7},{7,6},{8,9},{9,8},{10,11... | collective-permute-start | bytes 1966088 | tf_op jit(solution)/shard_map/ppermute | solution.py:267
  5.0 0.4 %shard_map.86 = (bf16[128,128]{1,0:T(8,128)(2,1)S(1)}, bf16[1536,128]{1,0:T(8,128)(2,1)S(1)}, bf16[1536,128]{1,0:T(8,128)(2,1)S(1)}, f32[6,128,128]{2,1,0:T(8,128)S(1)}) custom-call(s32[1]{0:T(128)S(6)} %copy.17.count_ref, bf16[1280,128]{1,0:T(8,128)(2,1)S(1)} %get-tuple-element.63.k_own_ref, bf16[1280,128]{1,0:T(8,128)(2,1)S(1)} %get-tuple-element.64.v_own_ref, ...), custom_call_target="tpu_custom_call" | custom-call | flops 50331648 | bytes 3178500 | tf_op jit(solution)/shard_map/pallas_call | solution.py:180
  5.4 4.8 %collective-permute-start.2 = (bf16[128,128]{1,0:T(8,128)(2,1)S(1)}, bf16[128,128]{1,0:T(8,128)(2,1)S(1)}, u32[]{:S(2)}, u32[]{:S(2)}) collective-permute-start(bf16[128,128]{1,0:T(8,128)(2,1)S(1)} %get-tuple-element.69.refs_0_), channel_id=1, source_target_pairs={{0,12},{4,8},{8,4},{12,0},{1,13},{5,9},{9,5},{13,1},{2,14},{6,10},... | collective-permute-start | bytes 98312 | tf_op jit(solution)/shard_map/ppermute | solution.py:234
  10.3 0.0 collective-permute-start.3
  10.3 0.6 %collective-permute-start.4 = (bf16[128,128]{1,0:T(8,128)(2,1)S(1)}, bf16[128,128]{1,0:T(8,128)(2,1)S(1)}, u32[]{:S(2)}, u32[]{:S(2)}) collective-permute-start(bf16[128,128]{1,0:T(8,128)(2,1)S(1)} %get-tuple-element.69.refs_0_), channel_id=1, source_target_pairs={{0,4},{4,0},{8,12},{12,8},{1,5},{5,1},{9,13},{13,9},{2,6},{6,2},{1... | collective-permute-start | bytes 98312 | tf_op jit(solution)/shard_map/ppermute | solution.py:234
  10.9 0.0 collective-permute-done.5.other_ref
  10.9 1.2 %shard_map.87 = (bf16[1536,128]{1,0:T(8,128)(2,1)S(1)}, bf16[1536,128]{1,0:T(8,128)(2,1)S(1)}, f32[1536,128]{1,0:T(8,128)S(1)}, bf16[6,256,256]{2,1,0:T(8,128)(2,1)S(1)}) custom-call(s32[1]{0:T(128)S(6)} %copy.17.count_ref, bf16[1280,128]{1,0:T(8,128)(2,1)S(1)} %get-tuple-element.70.q_own_ref, bf16[1280,128]{1,0:T(8,128)(2,1)S(1)} %get-tuple-element.71.cot_own_ref, ...), custom_call_target="tpu_custom_call" | custom-call | flops 301989888 | bytes 4456452 | tf_op jit(solution)/shard_map/pallas_call | solution.py:180
  12.1 0.1 collective-permute-done.2.refs_1_
  12.3 2.8 %collective-permute-done.3.refs_2_ = bf16[128,128]{1,0:T(8,128)(2,1)S(1)} collective-permute-done((bf16[128,128]{1,0:T(8,128)(2,1)S(1)}, bf16[128,128]{1,0:T(8,128)(2,1)S(1)}, u32[]{:S(2)}, u32[]{:S(2)}) %collective-permute-start.3) | collective-permute-done | bytes 32800 | tf_op jit(solution)/shard_map/ppermute | solution.py:234
  15.1 0.0 collective-permute-done.4.refs_3_
  15.1 0.8 %shard_map.89 = (bf16[1536,128]{1,0:T(8,128)(2,1)S(1)}, bf16[6,128,128]{2,1,0:T(8,128)(2,1)S(1)}, f32[6,128,128]{2,1,0:T(8,128)S(1)}, bf16[128,128]{1,0:T(8,128)(2,1)S(1)}) custom-call(bf16[1536,128]{1,0:T(8,128)(2,1)S(1)} %get-tuple-element.77.q_ref, bf16[1536,128]{1,0:T(8,128)(2,1)S(1)} %get-tuple-element.78.cot_ref, ...), custom_call_target="tpu_custom_call" | custom-call | flops 100663296 | bytes 3048448 | tf_op jit(solution)/shard_map/pallas_call | solution.py:180
  16.0 1.6 %collective-permute-start.6 = (bf16[128,128]{1,0:T(8,128)(2,1)S(1)}, bf16[128,128]{1,0:T(8,128)(2,1)S(1)}, u32[]{:S(2)}, u32[]{:S(2)}) collective-permute-start(bf16[128,128]{1,0:T(8,128)(2,1)S(1)} %get-tuple-element.85.refs_0_), channel_id=1, source_target_pairs={{0,12},{4,8},{8,4},{12,0},{1,13},{5,9},{9,5},{13,1},{2,14},{6,10},... | collective-permute-start | bytes 98312 | tf_op jit(solution)/shard_map/ppermute | solution.py:234
  17.5 0.6 %collective-permute-start.7 = (bf16[128,128]{1,0:T(8,128)(2,1)S(1)}, bf16[128,128]{1,0:T(8,128)(2,1)S(1)}, u32[]{:S(2)}, u32[]{:S(2)}) collective-permute-start(bf16[128,128]{1,0:T(8,128)(2,1)S(1)} %get-tuple-element.85.refs_0_), channel_id=1, source_target_pairs={{0,8},{4,12},{8,0},{12,4},{1,9},{5,13},{9,1},{13,5},{2,10},{6,14},... | collective-permute-start | bytes 98312 | tf_op jit(solution)/shard_map/ppermute | solution.py:234
  18.1 2.3 %collective-permute-start.8 = (bf16[128,128]{1,0:T(8,128)(2,1)S(1)}, bf16[128,128]{1,0:T(8,128)(2,1)S(1)}, u32[]{:S(2)}, u32[]{:S(2)}) collective-permute-start(bf16[128,128]{1,0:T(8,128)(2,1)S(1)} %get-tuple-element.85.refs_0_), channel_id=1, source_target_pairs={{0,4},{4,0},{8,12},{12,8},{1,5},{5,1},{9,13},{13,9},{2,6},{6,2},{1... | collective-permute-start | bytes 98312 | tf_op jit(solution)/shard_map/ppermute | solution.py:234
  20.4 1.8 %shard_map.90 = (bf16[1280,128]{1,0:T(8,128)(2,1)S(1)}, bf16[3,1280,128]{2,1,0:T(8,128)(2,1)S(1)}, f32[1536,128]{1,0:T(8,128)S(1)}, f32[1536,128]{1,0:T(8,128)S(1)}) custom-call(s32[1]{0:T(128)S(6)} %copy.17.count_ref, bf16[1536,128]{1,0:T(8,128)(2,1)S(1)} %get-tuple-element.77.q_ref, bf16[1536,128]{1,0:T(8,128)(2,1)S(1)} %get-tuple-element.67.k_ref, ...), custom_call_target="tpu_custom_call" | custom-call | flops 553648128 | bytes 5439492 | tf_op jit(solution)/shard_map/pallas_call | solution.py:180
  22.2 0.0 collective-permute-done.6.refs_1_
  22.2 0.2 collective-permute-done.7.refs_2_
  22.4 0.3 %collective-permute-done.8.refs_3_ = bf16[128,128]{1,0:T(8,128)(2,1)S(1)} collective-permute-done((bf16[128,128]{1,0:T(8,128)(2,1)S(1)}, bf16[128,128]{1,0:T(8,128)(2,1)S(1)}, u32[]{:S(2)}, u32[]{:S(2)}) %collective-permute-start.8) | collective-permute-done | bytes 32800 | tf_op jit(solution)/shard_map/ppermute | solution.py:234
  22.7 0.6 %shard_map.92 = (bf16[1280,128]{1,0:T(8,128)(2,1)S(1)}, bf16[1280,128]{1,0:T(8,128)(2,1)S(1)}, bf16[3,1280,128]{2,1,0:T(8,128)(2,1)S(1)}) custom-call(s32[1]{0:T(128)S(6)} %copy.17.count_ref, bf16[1536,128]{1,0:T(8,128)(2,1)S(1)} %get-tuple-element.67.k_ref, bf16[1536,128]{1,0:T(8,128)(2,1)S(1)} %get-tuple-element.68.v_ref, ...), custom_call_target="tpu_custom_call", output_to_operand_aliasing={{2}: (7, {})} | custom-call | flops 100663296 | bytes 5439492 | tf_op jit(solution)/shard_map/pallas_call | solution.py:180
  23.4 0.1 collective-permute-start.9
  23.5 1.0 %shard_map.93 = (bf16[1280,256]{1,0:T(8,128)(2,1)}, bf16[1280,256]{1,0:T(8,128)(2,1)}, bf16[1280,256]{1,0:T(8,128)(2,1)}) custom-call(bf16[1280,128]{1,0:T(8,128)(2,1)S(1)} %get-tuple-element.101.gq_own_ref, bf16[1280,128]{1,0:T(8,128)(2,1)S(1)} %get-tuple-element.102.gk_own_ref, bf16[1280,128]{1,0:T(8,128)(2,1)S(1)} %get-tuple-element.103.gv_own_ref), custom_call_target="tpu_custom_call" | custom-call | bytes 2949120 | tf_op jit(solution)/shard_map/pallas_call | solution.py:180
  24.4 1.6 %collective-permute-done.9.came_ref = bf16[3,1280,128]{2,1,0:T(8,128)(2,1)S(1)} collective-permute-done((bf16[3,1280,128]{2,1,0:T(8,128)(2,1)S(1)}, bf16[3,1280,128]{2,1,0:T(8,128)(2,1)S(1)}, u32[]{:S(2)}, u32[]{:S(2)}) %collective-permute-start.9) | collective-permute-done | bytes 983072 | tf_op jit(solution)/shard_map/ppermute | solution.py:267
  26.0 1.0 %shard_map.94 = (bf16[1280,256]{1,0:T(8,128)(2,1)}, bf16[1280,256]{1,0:T(8,128)(2,1)}, bf16[1280,256]{1,0:T(8,128)(2,1)}) custom-call(bf16[3,1280,128]{2,1,0:T(8,128)(2,1)S(1)} %collective-permute-done.9.came_ref, bf16[1280,256]{1,0:T(8,128)(2,1)} %get-tuple-element.108.gq_in_hbm, ...), custom_call_target="tpu_custom_call", output_to_operand_aliasing={{0}: (1, {}), {1}: (2, {}), {2}: (3, {})} | custom-call | bytes 4915200 | tf_op jit(solution)/shard_map/pallas_call | solution.py:180
  (2 shorter events, 0.0 us)
Async XLA Ops:
  0.6 2.5 %collective-permute-start = (bf16[1280,256]{1,0:T(8,128)(2,1)}, bf16[1280,256]{1,0:T(8,128)(2,1)S(1)}, u32[]{:S(2)}, u32[]{:S(2)}) collective-permute-start(bf16[1280,256]{1,0:T(8,128)(2,1)} %k_hbm.1), channel_id=1, source_target_pairs={{0,1},{1,0},{2,3},{3,2},{4,5},{5,4},{6,7},{7,6},{8,9},{9,8},{10,11... | collective-permute-start | bytes 1966088 | tf_op jit(solution)/shard_map/ppermute | solution.py:267
  1.1 2.9 %collective-permute-start.1 = (bf16[1280,256]{1,0:T(8,128)(2,1)}, bf16[1280,256]{1,0:T(8,128)(2,1)S(1)}, u32[]{:S(2)}, u32[]{:S(2)}) collective-permute-start(bf16[1280,256]{1,0:T(8,128)(2,1)} %v_hbm.1), channel_id=1, source_target_pairs={{0,1},{1,0},{2,3},{3,2},{4,5},{5,4},{6,7},{7,6},{8,9},{9,8},{10,11... | collective-permute-start | bytes 1966088 | tf_op jit(solution)/shard_map/ppermute | solution.py:267
  4.0 6.9 %collective-permute-start.5 = (bf16[2,1280,128]{2,1,0:T(8,128)(2,1)S(1)}, bf16[2,1280,128]{2,1,0:T(8,128)(2,1)S(1)}, u32[]{:S(2)}, u32[]{:S(2)}) collective-permute-start(bf16[2,1280,128]{2,1,0:T(8,128)(2,1)S(1)} %get-tuple-element.72), channel_id=1, source_target_pairs={{0,1},{1,0},{2,3},{3,2},{4,5},{5,4},{6,7},{7,6},{8,9},{9,8},{10,11... | collective-permute-start | bytes 1966088 | tf_op jit(solution)/shard_map/ppermute | solution.py:267
  5.4 6.8 %collective-permute-start.2 = (bf16[128,128]{1,0:T(8,128)(2,1)S(1)}, bf16[128,128]{1,0:T(8,128)(2,1)S(1)}, u32[]{:S(2)}, u32[]{:S(2)}) collective-permute-start(bf16[128,128]{1,0:T(8,128)(2,1)S(1)} %get-tuple-element.69.refs_0_), channel_id=1, source_target_pairs={{0,12},{4,8},{8,4},{12,0},{1,13},{5,9},{9,5},{13,1},{2,14},{6,10},... | collective-permute-start | bytes 98312 | tf_op jit(solution)/shard_map/ppermute | solution.py:234
  10.3 4.8 %collective-permute-start.3 = (bf16[128,128]{1,0:T(8,128)(2,1)S(1)}, bf16[128,128]{1,0:T(8,128)(2,1)S(1)}, u32[]{:S(2)}, u32[]{:S(2)}) collective-permute-start(bf16[128,128]{1,0:T(8,128)(2,1)S(1)} %get-tuple-element.69.refs_0_), channel_id=1, source_target_pairs={{0,8},{4,12},{8,0},{12,4},{1,9},{5,13},{9,1},{13,5},{2,10},{6,14},... | collective-permute-start | bytes 98312 | tf_op jit(solution)/shard_map/ppermute | solution.py:234
  10.3 4.8 %collective-permute-start.4 = (bf16[128,128]{1,0:T(8,128)(2,1)S(1)}, bf16[128,128]{1,0:T(8,128)(2,1)S(1)}, u32[]{:S(2)}, u32[]{:S(2)}) collective-permute-start(bf16[128,128]{1,0:T(8,128)(2,1)S(1)} %get-tuple-element.69.refs_0_), channel_id=1, source_target_pairs={{0,4},{4,0},{8,12},{12,8},{1,5},{5,1},{9,13},{13,9},{2,6},{6,2},{1... | collective-permute-start | bytes 98312 | tf_op jit(solution)/shard_map/ppermute | solution.py:234
  16.0 6.3 %collective-permute-start.6 = (bf16[128,128]{1,0:T(8,128)(2,1)S(1)}, bf16[128,128]{1,0:T(8,128)(2,1)S(1)}, u32[]{:S(2)}, u32[]{:S(2)}) collective-permute-start(bf16[128,128]{1,0:T(8,128)(2,1)S(1)} %get-tuple-element.85.refs_0_), channel_id=1, source_target_pairs={{0,12},{4,8},{8,4},{12,0},{1,13},{5,9},{9,5},{13,1},{2,14},{6,10},... | collective-permute-start | bytes 98312 | tf_op jit(solution)/shard_map/ppermute | solution.py:234
  17.5 4.9 %collective-permute-start.7 = (bf16[128,128]{1,0:T(8,128)(2,1)S(1)}, bf16[128,128]{1,0:T(8,128)(2,1)S(1)}, u32[]{:S(2)}, u32[]{:S(2)}) collective-permute-start(bf16[128,128]{1,0:T(8,128)(2,1)S(1)} %get-tuple-element.85.refs_0_), channel_id=1, source_target_pairs={{0,8},{4,12},{8,0},{12,4},{1,9},{5,13},{9,1},{13,5},{2,10},{6,14},... | collective-permute-start | bytes 98312 | tf_op jit(solution)/shard_map/ppermute | solution.py:234
  18.1 4.6 %collective-permute-start.8 = (bf16[128,128]{1,0:T(8,128)(2,1)S(1)}, bf16[128,128]{1,0:T(8,128)(2,1)S(1)}, u32[]{:S(2)}, u32[]{:S(2)}) collective-permute-start(bf16[128,128]{1,0:T(8,128)(2,1)S(1)} %get-tuple-element.85.refs_0_), channel_id=1, source_target_pairs={{0,4},{4,0},{8,12},{12,8},{1,5},{5,1},{9,13},{13,9},{2,6},{6,2},{1... | collective-permute-start | bytes 98312 | tf_op jit(solution)/shard_map/ppermute | solution.py:234
  23.4 2.6 %collective-permute-start.9 = (bf16[3,1280,128]{2,1,0:T(8,128)(2,1)S(1)}, bf16[3,1280,128]{2,1,0:T(8,128)(2,1)S(1)}, u32[]{:S(2)}, u32[]{:S(2)}) collective-permute-start(bf16[3,1280,128]{2,1,0:T(8,128)(2,1)S(1)} %get-tuple-element.100), channel_id=1, source_target_pairs={{0,1},{1,0},{2,3},{3,2},{4,5},{5,4},{6,7},{7,6},{8,9},{9,8},{10,11... | collective-permute-start | bytes 2949128 | tf_op jit(solution)/shard_map/ppermute | solution.py:267

commit v5 on v4

--- a/solution.py
+++ b/solution.py
@@ -62,12 +62,17 @@
 def live_block(own_ref, other_ref, at, core, count):
     late = (at >= count).astype(jnp.int32)
     r = rows_of(at - late * count)
-    c = columns_of(core) if other_ref.shape[1] > DH else slice(None)
-    return jnp.where(late == core, own_ref[r, :], other_ref[r, c])
-
-
-def load_kernel(k_hbm, v_hbm, q_hbm, cot_hbm, gain_hbm,
+    return jnp.where(late == core, own_ref[r, :], other_ref[r, :])
+
+
+def give_kernel(k_hbm, v_hbm, give_ref, sems):
+    other = columns_of(1 - lax.axis_index("loader"))
+    wait(fetch([(source.at[:, other], give_ref.at[at]) for at, source in enumerate((k_hbm, v_hbm))], sems))
+
+
+def load_kernel(count_ref, k_hbm, v_hbm, q_hbm, cot_hbm, gain_hbm,
                 k_ref, v_ref, q_ref, cot_ref, give_ref, gain_ref, sems):
+    del count_ref
     core = lax.axis_index("loader")
     own, other = columns_of(core), columns_of(1 - core)
     wait(fetch(((k_hbm.at[:, own], k_ref), (v_hbm.at[:, own], v_ref), (q_hbm.at[:, own], q_ref),
@@ -75,13 +80,13 @@
                 (cot_hbm.at[:, other], give_ref.at[1]), (gain_hbm, gain_ref)), sems))
 
 
-def state_kernel(count_ref, k_own_ref, v_own_ref, k_other_ref, v_other_ref, total_ref, k_ref, v_ref, run_ref):
+def state_kernel(count_ref, k_own_ref, v_own_ref, other_ref, total_ref, k_ref, v_ref, run_ref):
     core, count, _ = core_and_counts(count_ref)
     running = jnp.zeros((DH, DH), F32)
     for at in range(LIVE):
         r = rows_of(at)
-        k = live_block(k_own_ref, k_other_ref, at, core, count)
-        v = live_block(v_own_ref, v_other_ref, at, core, count)
+        k = live_block(k_own_ref, other_ref.at[0], at, core, count)
+        v = live_block(v_own_ref, other_ref.at[1], at, core, count)
         k_ref[r, :], v_ref[r, :] = k, v
         run_ref[at] = running
         running = running + tn(k, v)
@@ -266,15 +271,15 @@
     def swap(array):
         return lax.ppermute(array, "loader", SWAP)
 
-    k_other, v_other = swap(key_rows), swap(values)
     pair = ((2, rows, DH), BF16), VMEM
+    give, = call(give_kernel, [(key_rows, HBM), (values, HBM)], [pair], 0, [sems(2)])
+    other = swap(give)
     loaded = call(
-        load_kernel, [(a, HBM) for a in (key_rows, values, queries, cotangent, out_gain.reshape(1, width))],
+        load_kernel, count + [(a, HBM) for a in (key_rows, values, queries, cotangent, out_gain.reshape(1, width))],
         [buffer] * 4 + [pair, (((1, width), F32), VMEM)], 0, [sems(7)])
-    k_other, v_other, loaded = lax.optimization_barrier((k_other, v_other, loaded))
-    k_own, v_own, q_own, cot_own, give, gain = loaded
+    other, (k_own, v_own, q_own, cot_own, give, gain) = lax.optimization_barrier((other, loaded))
     own, k, v, run = call(
-        state_kernel, count + vmem(k_own, v_own, k_other, v_other), [total, half, half, states], unit)
+        state_kernel, count + vmem(k_own, v_own, other), [total, half, half, states], unit)
     cover = call(
         score_kernel, count + vmem(q_own, cot_own, swap(give), k, v), [half, half, plane, square], 6 * unit)
     outside, (q, cot, part, turned) = outside_sum(own, False, cover)

time: 27.1 us -> 26.9 us (level)
  waiting for transfers between devices: 6.23 us -> 4.9 us
  Pallas kernels: 8.43 us -> 9.52 us
    ppermute x4 -> x3, waiting for transfers between devices: 2.83 us -> 1.58 us  [swap(): return lax.ppermute(array, 'loader', SWAP)]
    pallas_call x10 -> x11, Pallas kernels: 8.43 us -> 9.52 us  [call(): pl.pallas_call(kernel, out_shape=[pltpu.VMEM(*a) if space is VMEM else pl...]
    ppermute x4 -> x3, starting transfers between devices: 1.04 us -> 0.71 us  [swap(): return lax.ppermute(array, 'loader', SWAP)]
    ppermute x6, starting transfers between devices: 9.92 us -> 10.2 us  [outside_sum(): came.append(lax.ppermute(group, 'seq', pairs))]
  transfers between devices with their start and end apart: 10 -> 9, of which waited for: 7 -> 4; matrix products, arithmetic and copies ran while one was open for 0% -> 0% of each run, Pallas kernels for 22% -> 22%
where the time goes in v5:
time: 26.9 us; the launch traced here: 26.7 us
  starting transfers between devices  10.9 us (41%)
  Pallas kernels  9.52 us (35%)
  waiting for transfers between devices  4.9 us (18%)
  between operations  1.38 us (5%)
    ppermute x6, starting transfers between devices, outside_sum(): came.append(lax.ppermute(group, 'seq', pairs))  10.2 us
    pallas_call x11, Pallas kernels, call(): pl.pallas_call(kernel, out_shape=[pltpu.VMEM(*a) if space is VMEM else pl...  9.52 us
    ppermute x6, waiting for transfers between devices, outside_sum(): came.append(lax.ppermute(group, 'seq', pairs))  3.33 us
    ppermute x3, waiting for transfers between devices, swap(): return lax.ppermute(array, 'loader', SWAP)  1.58 us
    ppermute x3, starting transfers between devices, swap(): return lax.ppermute(array, 'loader', SWAP)  0.71 us
  transfers between devices with their start and end apart: 9, of which 4 were waited for; matrix products, arithmetic and copies ran while one was open for 0% of the time, Pallas kernels for 22%

profile of v5, /device:TPU:0, one launch (start us, length us, event | category | flops | bytes accessed | tf_op | source)
XLA Modules:
  0.0 26.7 jit_solution(10762757973033365773)
XLA Ops:
  0.6 1.1 %shard_map.85 = bf16[2,1280,128]{2,1,0:T(8,128)(2,1)S(1)} custom-call(bf16[1280,256]{1,0:T(8,128)(2,1)} %k_hbm.3, bf16[1280,256]{1,0:T(8,128)(2,1)} %v_hbm.3), custom_call_target="tpu_custom_call" | custom-call | bytes 1966080 | tf_op jit(solution)/shard_map/pallas_call | solution.py:185
  1.7 0.5 %collective-permute-start = (bf16[2,1280,128]{2,1,0:T(8,128)(2,1)S(1)}, bf16[2,1280,128]{2,1,0:T(8,128)(2,1)S(1)}, u32[]{:S(2)}, u32[]{:S(2)}) collective-permute-start(bf16[2,1280,128]{2,1,0:T(8,128)(2,1)S(1)} %shard_map.85), channel_id=1, source_target_pairs={{0,1},{1,0},{2,3},{3,2},{4,5},{5,4},{6,7},{7,6},{8,9},{9,8},{10,11... | collective-permute-start | bytes 1966088 | tf_op jit(solution)/shard_map/ppermute | solution.py:272
  2.9 1.5 %shard_map.86 = (bf16[1280,128]{1,0:T(8,128)(2,1)S(1)}, bf16[1280,128]{1,0:T(8,128)(2,1)S(1)}, bf16[1280,128]{1,0:T(8,128)(2,1)S(1)}, bf16[1280,128]{1,0:T(8,128...) custom-call(s32[1]{0:T(128)S(6)} %copy.17.count_ref, bf16[1280,256]{1,0:T(8,128)(2,1)} %k_hbm.3, ...), custom_call_target="tpu_custom_call" | custom-call | bytes 4589572 | tf_op jit(solution)/shard_map/pallas_call | solution.py:185
  4.5 0.0 collective-permute-done.other_ref
  4.5 0.1 collective-permute-start.4
  4.6 0.4 %shard_map.87 = (bf16[128,128]{1,0:T(8,128)(2,1)S(1)}, bf16[1536,128]{1,0:T(8,128)(2,1)S(1)}, bf16[1536,128]{1,0:T(8,128)(2,1)S(1)}, f32[6,128,128]{2,1,0:T(8,128)S(1)}) custom-call(s32[1]{0:T(128)S(6)} %copy.17.count_ref, bf16[1280,128]{1,0:T(8,128)(2,1)S(1)} %get-tuple-element.62.k_own_ref, bf16[1280,128]{1,0:T(8,128)(2,1)S(1)} %get-tuple-element.63.v_own_ref, ...), custom_call_target="tpu_custom_call" | custom-call | flops 50331648 | bytes 2523140 | tf_op jit(solution)/shard_map/pallas_call | solution.py:185
  5.0 5.1 %collective-permute-start.1 = (bf16[128,128]{1,0:T(8,128)(2,1)S(1)}, bf16[128,128]{1,0:T(8,128)(2,1)S(1)}, u32[]{:S(2)}, u32[]{:S(2)}) collective-permute-start(bf16[128,128]{1,0:T(8,128)(2,1)S(1)} %get-tuple-element.67.refs_0_), channel_id=1, source_target_pairs={{0,12},{4,8},{8,4},{12,0},{1,13},{5,9},{9,5},{13,1},{2,14},{6,10},... | collective-permute-start | bytes 98312 | tf_op jit(solution)/shard_map/ppermute | solution.py:239
  10.1 0.0 collective-permute-start.2
  10.1 0.6 %collective-permute-start.3 = (bf16[128,128]{1,0:T(8,128)(2,1)S(1)}, bf16[128,128]{1,0:T(8,128)(2,1)S(1)}, u32[]{:S(2)}, u32[]{:S(2)}) collective-permute-start(bf16[128,128]{1,0:T(8,128)(2,1)S(1)} %get-tuple-element.67.refs_0_), channel_id=1, source_target_pairs={{0,4},{4,0},{8,12},{12,8},{1,5},{5,1},{9,13},{13,9},{2,6},{6,2},{1... | collective-permute-start | bytes 98312 | tf_op jit(solution)/shard_map/ppermute | solution.py:239
  10.7 0.0 collective-permute-done.4.other_ref
  10.7 1.2 %shard_map.88 = (bf16[1536,128]{1,0:T(8,128)(2,1)S(1)}, bf16[1536,128]{1,0:T(8,128)(2,1)S(1)}, f32[1536,128]{1,0:T(8,128)S(1)}, bf16[6,256,256]{2,1,0:T(8,128)(2,1)S(1)}) custom-call(s32[1]{0:T(128)S(6)} %copy.17.count_ref, bf16[1280,128]{1,0:T(8,128)(2,1)S(1)} %get-tuple-element.68.q_own_ref, bf16[1280,128]{1,0:T(8,128)(2,1)S(1)} %get-tuple-element.69.cot_own_ref, ...), custom_call_target="tpu_custom_call" | custom-call | flops 301989888 | bytes 4456452 | tf_op jit(solution)/shard_map/pallas_call | solution.py:185
  12.0 0.0 collective-permute-done.1.refs_1_
  12.0 2.9 %collective-permute-done.2.refs_2_ = bf16[128,128]{1,0:T(8,128)(2,1)S(1)} collective-permute-done((bf16[128,128]{1,0:T(8,128)(2,1)S(1)}, bf16[128,128]{1,0:T(8,128)(2,1)S(1)}, u32[]{:S(2)}, u32[]{:S(2)}) %collective-permute-start.2) | collective-permute-done | bytes 32800 | tf_op jit(solution)/shard_map/ppermute | solution.py:239
  14.9 0.0 collective-permute-done.3.refs_3_
  14.9 0.8 %shard_map.90 = (bf16[1536,128]{1,0:T(8,128)(2,1)S(1)}, bf16[6,128,128]{2,1,0:T(8,128)(2,1)S(1)}, f32[6,128,128]{2,1,0:T(8,128)S(1)}, bf16[128,128]{1,0:T(8,128)(2,1)S(1)}) custom-call(bf16[1536,128]{1,0:T(8,128)(2,1)S(1)} %get-tuple-element.75.q_ref, bf16[1536,128]{1,0:T(8,128)(2,1)S(1)} %get-tuple-element.76.cot_ref, ...), custom_call_target="tpu_custom_call" | custom-call | flops 100663296 | bytes 3048448 | tf_op jit(solution)/shard_map/pallas_call | solution.py:185
  15.8 1.5 %collective-permute-start.5 = (bf16[128,128]{1,0:T(8,128)(2,1)S(1)}, bf16[128,128]{1,0:T(8,128)(2,1)S(1)}, u32[]{:S(2)}, u32[]{:S(2)}) collective-permute-start(bf16[128,128]{1,0:T(8,128)(2,1)S(1)} %get-tuple-element.83.refs_0_), channel_id=1, source_target_pairs={{0,12},{4,8},{8,4},{12,0},{1,13},{5,9},{9,5},{13,1},{2,14},{6,10},... | collective-permute-start | bytes 98312 | tf_op jit(solution)/shard_map/ppermute | solution.py:239
  17.3 0.6 %collective-permute-start.6 = (bf16[128,128]{1,0:T(8,128)(2,1)S(1)}, bf16[128,128]{1,0:T(8,128)(2,1)S(1)}, u32[]{:S(2)}, u32[]{:S(2)}) collective-permute-start(bf16[128,128]{1,0:T(8,128)(2,1)S(1)} %get-tuple-element.83.refs_0_), channel_id=1, source_target_pairs={{0,8},{4,12},{8,0},{12,4},{1,9},{5,13},{9,1},{13,5},{2,10},{6,14},... | collective-permute-start | bytes 98312 | tf_op jit(solution)/shard_map/ppermute | solution.py:239
  17.9 2.3 %collective-permute-start.7 = (bf16[128,128]{1,0:T(8,128)(2,1)S(1)}, bf16[128,128]{1,0:T(8,128)(2,1)S(1)}, u32[]{:S(2)}, u32[]{:S(2)}) collective-permute-start(bf16[128,128]{1,0:T(8,128)(2,1)S(1)} %get-tuple-element.83.refs_0_), channel_id=1, source_target_pairs={{0,4},{4,0},{8,12},{12,8},{1,5},{5,1},{9,13},{13,9},{2,6},{6,2},{1... | collective-permute-start | bytes 98312 | tf_op jit(solution)/shard_map/ppermute | solution.py:239
  20.2 1.8 %shard_map.91 = (bf16[1280,128]{1,0:T(8,128)(2,1)S(1)}, bf16[3,1280,128]{2,1,0:T(8,128)(2,1)S(1)}, f32[1536,128]{1,0:T(8,128)S(1)}, f32[1536,128]{1,0:T(8,128)S(1)}) custom-call(s32[1]{0:T(128)S(6)} %copy.17.count_ref, bf16[1536,128]{1,0:T(8,128)(2,1)S(1)} %get-tuple-element.75.q_ref, bf16[1536,128]{1,0:T(8,128)(2,1)S(1)} %get-tuple-element.65.k_ref, ...), custom_call_target="tpu_custom_call" | custom-call | flops 553648128 | bytes 5439492 | tf_op jit(solution)/shard_map/pallas_call | solution.py:185
  22.0 0.0 collective-permute-done.5.refs_1_
  22.1 0.1 collective-permute-done.6.refs_2_
  22.1 0.3 %collective-permute-done.7.refs_3_ = bf16[128,128]{1,0:T(8,128)(2,1)S(1)} collective-permute-done((bf16[128,128]{1,0:T(8,128)(2,1)S(1)}, bf16[128,128]{1,0:T(8,128)(2,1)S(1)}, u32[]{:S(2)}, u32[]{:S(2)}) %collective-permute-start.7) | collective-permute-done | bytes 32800 | tf_op jit(solution)/shard_map/ppermute | solution.py:239
  22.5 0.6 %shard_map.93 = (bf16[1280,128]{1,0:T(8,128)(2,1)S(1)}, bf16[1280,128]{1,0:T(8,128)(2,1)S(1)}, bf16[3,1280,128]{2,1,0:T(8,128)(2,1)S(1)}) custom-call(s32[1]{0:T(128)S(6)} %copy.17.count_ref, bf16[1536,128]{1,0:T(8,128)(2,1)S(1)} %get-tuple-element.65.k_ref, bf16[1536,128]{1,0:T(8,128)(2,1)S(1)} %get-tuple-element.66.v_ref, ...), custom_call_target="tpu_custom_call", output_to_operand_aliasing={{2}: (7, {})} | custom-call | flops 100663296 | bytes 5439492 | tf_op jit(solution)/shard_map/pallas_call | solution.py:185
  23.1 0.1 collective-permute-start.8
  23.2 1.0 %shard_map.94 = (bf16[1280,256]{1,0:T(8,128)(2,1)}, bf16[1280,256]{1,0:T(8,128)(2,1)}, bf16[1280,256]{1,0:T(8,128)(2,1)}) custom-call(bf16[1280,128]{1,0:T(8,128)(2,1)S(1)} %get-tuple-element.99.gq_own_ref, bf16[1280,128]{1,0:T(8,128)(2,1)S(1)} %get-tuple-element.100.gk_own_ref, bf16[1280,128]{1,0:T(8,128)(2,1)S(1)} %get-tuple-element.101.gv_own_ref), custom_call_target="tpu_custom_call" | custom-call | bytes 2949120 | tf_op jit(solution)/shard_map/pallas_call | solution.py:185
  24.2 1.6 %collective-permute-done.8.came_ref = bf16[3,1280,128]{2,1,0:T(8,128)(2,1)S(1)} collective-permute-done((bf16[3,1280,128]{2,1,0:T(8,128)(2,1)S(1)}, bf16[3,1280,128]{2,1,0:T(8,128)(2,1)S(1)}, u32[]{:S(2)}, u32[]{:S(2)}) %collective-permute-start.8) | collective-permute-done | bytes 983072 | tf_op jit(solution)/shard_map/ppermute | solution.py:272
  25.8 1.0 %shard_map.95 = (bf16[1280,256]{1,0:T(8,128)(2,1)}, bf16[1280,256]{1,0:T(8,128)(2,1)}, bf16[1280,256]{1,0:T(8,128)(2,1)}) custom-call(bf16[3,1280,128]{2,1,0:T(8,128)(2,1)S(1)} %collective-permute-done.8.came_ref, bf16[1280,256]{1,0:T(8,128)(2,1)} %get-tuple-element.106.gq_in_hbm, ...), custom_call_target="tpu_custom_call", output_to_operand_aliasing={{0}: (1, {}), {1}: (2, {}), {2}: (3, {})} | custom-call | bytes 4915200 | tf_op jit(solution)/shard_map/pallas_call | solution.py:185
  (2 shorter events, 0.0 us)
Async XLA Ops:
  1.7 2.7 %collective-permute-start = (bf16[2,1280,128]{2,1,0:T(8,128)(2,1)S(1)}, bf16[2,1280,128]{2,1,0:T(8,128)(2,1)S(1)}, u32[]{:S(2)}, u32[]{:S(2)}) collective-permute-start(bf16[2,1280,128]{2,1,0:T(8,128)(2,1)S(1)} %shard_map.85), channel_id=1, source_target_pairs={{0,1},{1,0},{2,3},{3,2},{4,5},{5,4},{6,7},{7,6},{8,9},{9,8},{10,11... | collective-permute-start | bytes 1966088 | tf_op jit(solution)/shard_map/ppermute | solution.py:272
  4.5 6.3 %collective-permute-start.4 = (bf16[2,1280,128]{2,1,0:T(8,128)(2,1)S(1)}, bf16[2,1280,128]{2,1,0:T(8,128)(2,1)S(1)}, u32[]{:S(2)}, u32[]{:S(2)}) collective-permute-start(bf16[2,1280,128]{2,1,0:T(8,128)(2,1)S(1)} %get-tuple-element.70), channel_id=1, source_target_pairs={{0,1},{1,0},{2,3},{3,2},{4,5},{5,4},{6,7},{7,6},{8,9},{9,8},{10,11... | collective-permute-start | bytes 1966088 | tf_op jit(solution)/shard_map/ppermute | solution.py:272
  5.0 7.1 %collective-permute-start.1 = (bf16[128,128]{1,0:T(8,128)(2,1)S(1)}, bf16[128,128]{1,0:T(8,128)(2,1)S(1)}, u32[]{:S(2)}, u32[]{:S(2)}) collective-permute-start(bf16[128,128]{1,0:T(8,128)(2,1)S(1)} %get-tuple-element.67.refs_0_), channel_id=1, source_target_pairs={{0,12},{4,8},{8,4},{12,0},{1,13},{5,9},{9,5},{13,1},{2,14},{6,10},... | collective-permute-start | bytes 98312 | tf_op jit(solution)/shard_map/ppermute | solution.py:239
  10.1 4.8 %collective-permute-start.2 = (bf16[128,128]{1,0:T(8,128)(2,1)S(1)}, bf16[128,128]{1,0:T(8,128)(2,1)S(1)}, u32[]{:S(2)}, u32[]{:S(2)}) collective-permute-start(bf16[128,128]{1,0:T(8,128)(2,1)S(1)} %get-tuple-element.67.refs_0_), channel_id=1, source_target_pairs={{0,8},{4,12},{8,0},{12,4},{1,9},{5,13},{9,1},{13,5},{2,10},{6,14},... | collective-permute-start | bytes 98312 | tf_op jit(solution)/shard_map/ppermute | solution.py:239
  10.1 4.8 %collective-permute-start.3 = (bf16[128,128]{1,0:T(8,128)(2,1)S(1)}, bf16[128,128]{1,0:T(8,128)(2,1)S(1)}, u32[]{:S(2)}, u32[]{:S(2)}) collective-permute-start(bf16[128,128]{1,0:T(8,128)(2,1)S(1)} %get-tuple-element.67.refs_0_), channel_id=1, source_target_pairs={{0,4},{4,0},{8,12},{12,8},{1,5},{5,1},{9,13},{13,9},{2,6},{6,2},{1... | collective-permute-start | bytes 98312 | tf_op jit(solution)/shard_map/ppermute | solution.py:239
  15.8 6.3 %collective-permute-start.5 = (bf16[128,128]{1,0:T(8,128)(2,1)S(1)}, bf16[128,128]{1,0:T(8,128)(2,1)S(1)}, u32[]{:S(2)}, u32[]{:S(2)}) collective-permute-start(bf16[128,128]{1,0:T(8,128)(2,1)S(1)} %get-tuple-element.83.refs_0_), channel_id=1, source_target_pairs={{0,12},{4,8},{8,4},{12,0},{1,13},{5,9},{9,5},{13,1},{2,14},{6,10},... | collective-permute-start | bytes 98312 | tf_op jit(solution)/shard_map/ppermute | solution.py:239
  17.3 4.8 %collective-permute-start.6 = (bf16[128,128]{1,0:T(8,128)(2,1)S(1)}, bf16[128,128]{1,0:T(8,128)(2,1)S(1)}, u32[]{:S(2)}, u32[]{:S(2)}) collective-permute-start(bf16[128,128]{1,0:T(8,128)(2,1)S(1)} %get-tuple-element.83.refs_0_), channel_id=1, source_target_pairs={{0,8},{4,12},{8,0},{12,4},{1,9},{5,13},{9,1},{13,5},{2,10},{6,14},... | collective-permute-start | bytes 98312 | tf_op jit(solution)/shard_map/ppermute | solution.py:239
  17.9 4.5 %collective-permute-start.7 = (bf16[128,128]{1,0:T(8,128)(2,1)S(1)}, bf16[128,128]{1,0:T(8,128)(2,1)S(1)}, u32[]{:S(2)}, u32[]{:S(2)}) collective-permute-start(bf16[128,128]{1,0:T(8,128)(2,1)S(1)} %get-tuple-element.83.refs_0_), channel_id=1, source_target_pairs={{0,4},{4,0},{8,12},{12,8},{1,5},{5,1},{9,13},{13,9},{2,6},{6,2},{1... | collective-permute-start | bytes 98312 | tf_op jit(solution)/shard_map/ppermute | solution.py:239
  23.1 2.6 %collective-permute-start.8 = (bf16[3,1280,128]{2,1,0:T(8,128)(2,1)S(1)}, bf16[3,1280,128]{2,1,0:T(8,128)(2,1)S(1)}, u32[]{:S(2)}, u32[]{:S(2)}) collective-permute-start(bf16[3,1280,128]{2,1,0:T(8,128)(2,1)S(1)} %get-tuple-element.98), channel_id=1, source_target_pairs={{0,1},{1,0},{2,3},{3,2},{4,5},{5,4},{6,7},{7,6},{8,9},{9,8},{10,11... | collective-permute-start | bytes 2949128 | tf_op jit(solution)/shard_map/ppermute | solution.py:272

commit v6 on v5

--- a/solution.py
+++ b/solution.py
@@ -12,6 +12,7 @@
 SPAN = 256
 LIVE = 6
 EPSILON = 1e-06
+COVER = 10**10
 F32 = jnp.float32
 BF16 = jnp.bfloat16
 VMEM = pl.BlockSpec(memory_space=pltpu.VMEM)
@@ -136,47 +137,44 @@
                 (own_ref, jnp.where(core == 0, 0, count), own),
                 (other_ref, jnp.where(core == 0, count, 0), LIVE - own)):
             block = live_ref[rows_of(jnp.minimum(b + shift, LIVE - 1)), :]
-            target[rows_of(b), :] = jnp.where(b < limit, block, jnp.zeros_like(block))
-
-
-def pull_kernel(count_ref, q_ref, k_ref, v_ref, grad_ref, turned_ref, prefix_ref,
-                gq_own_ref, other_ref, gk_ref, gv_ref, gq_ref):
+            target[rows_of(b), :] = jnp.where(b < limit, block, jnp.zeros_like(block)).astype(target.dtype)
+
+
+def pull_kernel(count_ref, q_ref, k_ref, v_ref, grad_ref, turned_ref, prefix_ref, back_ref,
+                gq_own_ref, own_ref, other_ref, gq_ref, gk_ref, gv_ref):
     t = lax.broadcasted_iota(jnp.int32, (SPAN, SPAN), 0)
     s = lax.broadcasted_iota(jnp.int32, (SPAN, SPAN), 1)
     for at in range(LIVE):
         r = rows_of(at)
-        v, grad = v_ref[r, :], grad_ref[r, :]
+        k, v, grad, back = k_ref[r, :], v_ref[r, :], grad_ref[r, :], back_ref[at].astype(BF16)
         pull = jnp.where(t >= s, nt(grad, v), 0.0).astype(BF16)
-        gq_ref[r, :] = (nn(pull, k_ref[r, :]) + nt(grad, prefix_ref[at])).astype(BF16)
+        gq_ref[r, :] = (nn(pull, k) + nt(grad, prefix_ref[at])).astype(BF16)
         turned = jnp.where(t <= s, nt(v, grad), 0.0).astype(BF16)
-        gk_ref[r, :] = nn(turned, q_ref[r, :])
-        gv_ref[r, :] = nn(turned_ref[at], grad)
-    spread(gq_ref, gq_own_ref, other_ref.at[0], *core_and_counts(count_ref))
-
-
-def suffix_kernel(count_ref, k_ref, v_ref, gk_part_ref, gv_part_ref, back_ref, outside_ref, begun_ref,
-                  gk_own_ref, gv_own_ref, other_ref, gk_ref, gv_ref):
-    del begun_ref
-    outside = outside_ref[...]
-    for at in range(LIVE):
-        r = rows_of(at)
-        suffix = (back_ref[at] + outside).astype(BF16)
-        gk_ref[r, :] = (gk_part_ref[r, :] + nt(v_ref[r, :], suffix)).astype(BF16)
-        gv_ref[r, :] = (gv_part_ref[r, :] + nn(k_ref[r, :], suffix)).astype(BF16)
+        gk_ref[r, :] = nn(turned, q_ref[r, :]) + nt(v, back)
+        gv_ref[r, :] = nn(turned_ref[at], grad) + nn(k, back)
     where = core_and_counts(count_ref)
-    spread(gk_ref, gk_own_ref, other_ref.at[1], *where)
-    spread(gv_ref, gv_own_ref, other_ref.at[2], *where)
-
-
-def own_kernel(gq_own_ref, gk_own_ref, gv_own_ref, gq_hbm, gk_hbm, gv_hbm, sems):
-    c = columns_of(lax.axis_index("loader"))
-    wait(fetch(((gq_own_ref, gq_hbm.at[:, c]), (gk_own_ref, gk_hbm.at[:, c]), (gv_own_ref, gv_hbm.at[:, c])), sems))
-
-
-def came_kernel(came_ref, gq_in_hbm, gk_in_hbm, gv_in_hbm, gq_hbm, gk_hbm, gv_hbm, sems):
-    del gq_in_hbm, gk_in_hbm, gv_in_hbm
-    c = columns_of(1 - lax.axis_index("loader"))
-    wait(fetch([(came_ref.at[at], target.at[:, c]) for at, target in enumerate((gq_hbm, gk_hbm, gv_hbm))], sems))
+    spread(gq_ref, gq_own_ref, other_ref.at[0], *where)
+    spread(gk_ref, own_ref.at[0], other_ref.at[1], *where)
+    spread(gv_ref, own_ref.at[1], other_ref.at[2], *where)
+
+
+def final_kernel(count_ref, gq_own_ref, own_ref, k_own_ref, v_own_ref, outside_ref,
+                 came_ref, give_ref, outside_came_ref, gq_hbm, gk_hbm, gv_hbm, gk_ref, gv_ref, sems):
+    core, _, own = core_and_counts(count_ref)
+    columns = columns_of(core), columns_of(1 - core)
+    copies = fetch(((gq_own_ref, gq_hbm.at[:, columns[0]]), (came_ref.at[0], gq_hbm.at[:, columns[1]])), sems.at[0])
+    heads = ((k_own_ref, v_own_ref, own_ref.at[0], own_ref.at[1], outside_ref),
+             (give_ref.at[0], give_ref.at[1], came_ref.at[1], came_ref.at[2], outside_came_ref))
+    for h, (k_ref, v_ref, gk_part_ref, gv_part_ref, sum_ref) in enumerate(heads):
+        outside = sum_ref[...].astype(BF16)
+        for b in range(k_ref.shape[0] // SPAN):
+            r = rows_of(b)
+            suffix = jnp.where(b < own, outside, jnp.zeros_like(outside))
+            gk_ref[h, r, :] = (gk_part_ref[r, :].astype(F32) + nt(v_ref[r, :], suffix)).astype(BF16)
+            gv_ref[h, r, :] = (gv_part_ref[r, :].astype(F32) + nn(k_ref[r, :], suffix)).astype(BF16)
+        copies += fetch(((gk_ref.at[h], gk_hbm.at[:, columns[h]]), (gv_ref.at[h], gv_hbm.at[:, columns[h]])),
+                        sems.at[1 + h])
+    wait(copies)
 
 
 def call(kernel, ins, outs, flops, scratch=(), aliases={}):
@@ -224,7 +222,7 @@
 
 
 def order(radix, reverse):
-    return [3, 2, 1] if radix == 4 else list(range(radix - 1, 0, -1))
+    return [1, 2, 3] if radix == 4 else list(range(radix - 1, 0, -1))
 
 
 def outside_sum(total, reverse, cover):
@@ -242,7 +240,7 @@
         last = at + 1 == len(chain)
         kernel = functools.partial(combine_kernel, steps, radix, stride, reverse, at == 0, last)
         sums = [((total.shape, F32), VMEM)] + ([] if last else [((total.shape, total.dtype), VMEM)])
-        out = call(kernel, [(a, VMEM) for a in (group, *came, *outside)], sums, total.size)
+        out = call(kernel, [(a, VMEM) for a in (group, *came, *outside)], sums, COVER)
         outside, group = out[:1], out[-1]
         stride *= radix
     return outside[0], cover
@@ -259,7 +257,6 @@
     total = ((DH, DH), BF16), VMEM
     square = ((LIVE, SPAN, SPAN), BF16), VMEM
     result = ((rows, width), BF16), HBM
-    staged = pltpu.VMEM((LIVE * SPAN, DH), BF16)
     count = [(counts, SMEM)]
 
     def vmem(*arrays):
@@ -272,8 +269,8 @@
         return lax.ppermute(array, "loader", SWAP)
 
     pair = ((2, rows, DH), BF16), VMEM
-    give, = call(give_kernel, [(key_rows, HBM), (values, HBM)], [pair], 0, [sems(2)])
-    other = swap(give)
+    beside, = call(give_kernel, [(key_rows, HBM), (values, HBM)], [pair], 0, [sems(2)])
+    other = swap(beside)
     loaded = call(
         load_kernel, count + [(a, HBM) for a in (key_rows, values, queries, cotangent, out_gain.reshape(1, width))],
         [buffer] * 4 + [pair, (((1, width), F32), VMEM)], 0, [sems(7)])
@@ -286,18 +283,15 @@
     grad, prefix, back, own_back = call(
         norm_kernel, vmem(q, cot, gain, part, run, outside),
         [half, prefixes, states, total], 2 * unit)
-    three = ((3, rows, DH), BF16), VMEM
-    cover = call(
-        pull_kernel, count + vmem(q, k, v, grad, turned, prefix), [buffer, three, plane, plane], 11 * unit, [staged])
-    outside, (gq_own, other, gk_part, gv_part) = outside_sum(own_back, True, cover)
-    gk_own, gv_own, other = call(
-        suffix_kernel, count + vmem(k, v, gk_part, gv_part, back, outside, other),
-        [buffer, buffer, three], 2 * unit, [staged, staged], {7: 2})
+    staged = [pltpu.VMEM((LIVE * SPAN, DH), kind) for kind in (BF16, F32, F32)]
+    gq_own, parts, other = call(
+        pull_kernel, count + vmem(q, k, v, grad, turned, prefix, back),
+        [buffer, (((2, rows, DH), F32), VMEM), (((3, rows, DH), BF16), VMEM)], 13 * unit, staged)
     came = swap(other)
-    grads = call(own_kernel, vmem(gq_own, gk_own, gv_own), [result] * 3, 0, [sems(3)])
-    came, grads = lax.optimization_barrier((came, grads))
+    outside, (gq_own, parts) = outside_sum(own_back, True, (gq_own, parts))
     return tuple(call(
-        came_kernel, vmem(came) + [(grad, HBM) for grad in grads], [result] * 3, 0, [sems(3)], {1: 0, 2: 1, 3: 2}))
+        final_kernel, count + vmem(gq_own, parts, k_own, v_own, outside, came, beside, swap(outside)),
+        [result] * 3, 4 * unit, [pltpu.VMEM((2, rows, DH), BF16)] * 2 + [pltpu.SemaphoreType.DMA((3, 2))]))
 
 
 def solution(mesh):

time: 26.9 us -> 26.9 us (level)
  Pallas kernels: 9.52 us -> 8.89 us
  starting transfers between devices: 10.9 us -> 11.5 us
    pallas_call x11 -> x9, Pallas kernels: 9.52 us -> 8.89 us  [call(): pl.pallas_call(kernel, out_shape=[pltpu.VMEM(*a) if space is VMEM else pl...]
    ppermute x3 -> x4, starting transfers between devices: 0.71 us -> 1.25 us  [swap(): return lax.ppermute(array, 'loader', SWAP)]
    ppermute x3 -> x4, waiting for transfers between devices: 1.58 us -> 2.04 us  [swap(): return lax.ppermute(array, 'loader', SWAP)]
    ppermute x6, waiting for transfers between devices: 3.33 us -> 2.92 us  [outside_sum(): came.append(lax.ppermute(group, 'seq', pairs))]
  transfers between devices with their start and end apart: 9 -> 10, of which waited for: 4 -> 2; matrix products, arithmetic and copies ran while one was open for 0% -> 0% of each run, Pallas kernels for 22% -> 20%
where the time goes in v6:
time: 26.9 us; the launch traced here: 26.7 us
  starting transfers between devices  11.5 us (43%)
  Pallas kernels  8.89 us (33%)
  waiting for transfers between devices  4.96 us (18%)
  between operations  1.39 us (5%)
    ppermute x6, starting transfers between devices, outside_sum(): came.append(lax.ppermute(group, 'seq', pairs))  10.2 us
    pallas_call x9, Pallas kernels, call(): pl.pallas_call(kernel, out_shape=[pltpu.VMEM(*a) if space is VMEM else pl...  8.89 us
    ppermute x6, waiting for transfers between devices, outside_sum(): came.append(lax.ppermute(group, 'seq', pairs))  2.92 us
    ppermute x4, waiting for transfers between devices, swap(): return lax.ppermute(array, 'loader', SWAP)  2.04 us
    ppermute x4, starting transfers between devices, swap(): return lax.ppermute(array, 'loader', SWAP)  1.25 us
  transfers between devices with their start and end apart: 10, of which 2 were waited for; matrix products, arithmetic and copies ran while one was open for 0% of the time, Pallas kernels for 20%

profile of v6, /device:TPU:0, one launch (start us, length us, event | category | flops | bytes accessed | tf_op | source)
XLA Modules:
  0.0 26.7 jit_solution(2427909918308228966)
XLA Ops:
  0.6 1.1 %shard_map.85.give_ref = bf16[2,1280,128]{2,1,0:T(8,128)(2,1)S(1)} custom-call(bf16[1280,256]{1,0:T(8,128)(2,1)} %k_hbm.3, bf16[1280,256]{1,0:T(8,128)(2,1)} %v_hbm.3), custom_call_target="tpu_custom_call" | custom-call | bytes 1966080 | tf_op jit(solution)/shard_map/pallas_call | solution.py:183
  1.7 0.5 %collective-permute-start = (bf16[2,1280,128]{2,1,0:T(8,128)(2,1)S(1)}, bf16[2,1280,128]{2,1,0:T(8,128)(2,1)S(1)}, u32[]{:S(2)}, u32[]{:S(2)}) collective-permute-start(bf16[2,1280,128]{2,1,0:T(8,128)(2,1)S(1)} %shard_map.85.give_ref), channel_id=1, source_target_pairs={{0,1},{1,0},{2,3},{3,2},{4,5},{5,4},{6,7},{7,6},{8,9},{9,8},{10,11... | collective-permute-start | bytes 1966088 | tf_op jit(solution)/shard_map/ppermute | solution.py:269
  2.9 1.5 %shard_map.86 = (bf16[1280,128]{1,0:T(8,128)(2,1)S(1)}, bf16[1280,128]{1,0:T(8,128)(2,1)S(1)}, bf16[1280,128]{1,0:T(8,128)(2,1)S(1)}, bf16[1280,128]{1,0:T(8,128...) custom-call(s32[1]{0:T(128)S(6)} %copy.9.count_ref, bf16[1280,256]{1,0:T(8,128)(2,1)} %k_hbm.3, ...), custom_call_target="tpu_custom_call" | custom-call | bytes 4589572 | tf_op jit(solution)/shard_map/pallas_call | solution.py:183
  4.5 0.0 collective-permute-done.other_ref
  4.5 0.1 collective-permute-start.4
  4.6 0.4 %shard_map.87 = (bf16[128,128]{1,0:T(8,128)(2,1)S(1)}, bf16[1536,128]{1,0:T(8,128)(2,1)S(1)}, bf16[1536,128]{1,0:T(8,128)(2,1)S(1)}, f32[6,128,128]{2,1,0:T(8,128)S(1)}) custom-call(s32[1]{0:T(128)S(6)} %copy.9.count_ref, bf16[1280,128]{1,0:T(8,128)(2,1)S(1)} %get-tuple-element.49.k_own_ref, bf16[1280,128]{1,0:T(8,128)(2,1)S(1)} %get-tuple-element.50.v_own_ref, ...), custom_call_target="tpu_custom_call" | custom-call | flops 50331648 | bytes 2523140 | tf_op jit(solution)/shard_map/pallas_call | solution.py:183
  5.0 5.1 %collective-permute-start.3 = (bf16[128,128]{1,0:T(8,128)(2,1)S(1)}, bf16[128,128]{1,0:T(8,128)(2,1)S(1)}, u32[]{:S(2)}, u32[]{:S(2)}) collective-permute-start(bf16[128,128]{1,0:T(8,128)(2,1)S(1)} %get-tuple-element.52.refs_0_), channel_id=1, source_target_pairs={{0,12},{4,8},{8,4},{12,0},{1,13},{5,9},{9,5},{13,1},{2,14},{6,10},... | collective-permute-start | bytes 98312 | tf_op jit(solution)/shard_map/ppermute | solution.py:237
  10.1 0.0 collective-permute-start.2
  10.1 0.6 %collective-permute-start.1 = (bf16[128,128]{1,0:T(8,128)(2,1)S(1)}, bf16[128,128]{1,0:T(8,128)(2,1)S(1)}, u32[]{:S(2)}, u32[]{:S(2)}) collective-permute-start(bf16[128,128]{1,0:T(8,128)(2,1)S(1)} %get-tuple-element.52.refs_0_), channel_id=1, source_target_pairs={{0,4},{4,0},{8,12},{12,8},{1,5},{5,1},{9,13},{13,9},{2,6},{6,2},{1... | collective-permute-start | bytes 98312 | tf_op jit(solution)/shard_map/ppermute | solution.py:237
  10.7 0.0 collective-permute-done.4.other_ref
  10.7 1.2 %shard_map.88 = (bf16[1536,128]{1,0:T(8,128)(2,1)S(1)}, bf16[1536,128]{1,0:T(8,128)(2,1)S(1)}, f32[1536,128]{1,0:T(8,128)S(1)}, bf16[6,256,256]{2,1,0:T(8,128)(2,1)S(1)}) custom-call(s32[1]{0:T(128)S(6)} %copy.9.count_ref, bf16[1280,128]{1,0:T(8,128)(2,1)S(1)} %get-tuple-element.53.q_own_ref, bf16[1280,128]{1,0:T(8,128)(2,1)S(1)} %get-tuple-element.54.cot_own_ref, ...), custom_call_target="tpu_custom_call" | custom-call | flops 301989888 | bytes 4456452 | tf_op jit(solution)/shard_map/pallas_call | solution.py:183
  12.0 0.0 collective-permute-done.3.refs_3_
  12.0 2.9 %collective-permute-done.2.refs_2_ = bf16[128,128]{1,0:T(8,128)(2,1)S(1)} collective-permute-done((bf16[128,128]{1,0:T(8,128)(2,1)S(1)}, bf16[128,128]{1,0:T(8,128)(2,1)S(1)}, u32[]{:S(2)}, u32[]{:S(2)}) %collective-permute-start.2) | collective-permute-done | bytes 32800 | tf_op jit(solution)/shard_map/ppermute | solution.py:237
  14.9 0.0 collective-permute-done.1.refs_1_
  14.9 0.8 %shard_map.90 = (bf16[1536,128]{1,0:T(8,128)(2,1)S(1)}, bf16[6,128,128]{2,1,0:T(8,128)(2,1)S(1)}, f32[6,128,128]{2,1,0:T(8,128)S(1)}, bf16[128,128]{1,0:T(8,128)(2,1)S(1)}) custom-call(bf16[1536,128]{1,0:T(8,128)(2,1)S(1)} %get-tuple-element.62.q_ref, bf16[1536,128]{1,0:T(8,128)(2,1)S(1)} %get-tuple-element.63.cot_ref, ...), custom_call_target="tpu_custom_call" | custom-call | flops 100663296 | bytes 3048448 | tf_op jit(solution)/shard_map/pallas_call | solution.py:183
  15.8 1.5 %collective-permute-start.7 = (bf16[128,128]{1,0:T(8,128)(2,1)S(1)}, bf16[128,128]{1,0:T(8,128)(2,1)S(1)}, u32[]{:S(2)}, u32[]{:S(2)}) collective-permute-start(bf16[128,128]{1,0:T(8,128)(2,1)S(1)} %get-tuple-element.70.refs_0_), channel_id=1, source_target_pairs={{0,12},{4,8},{8,4},{12,0},{1,13},{5,9},{9,5},{13,1},{2,14},{6,10},... | collective-permute-start | bytes 98312 | tf_op jit(solution)/shard_map/ppermute | solution.py:237
  17.3 0.6 %collective-permute-start.6 = (bf16[128,128]{1,0:T(8,128)(2,1)S(1)}, bf16[128,128]{1,0:T(8,128)(2,1)S(1)}, u32[]{:S(2)}, u32[]{:S(2)}) collective-permute-start(bf16[128,128]{1,0:T(8,128)(2,1)S(1)} %get-tuple-element.70.refs_0_), channel_id=1, source_target_pairs={{0,8},{4,12},{8,0},{12,4},{1,9},{5,13},{9,1},{13,5},{2,10},{6,14},... | collective-permute-start | bytes 98312 | tf_op jit(solution)/shard_map/ppermute | solution.py:237
  17.9 2.3 %collective-permute-start.5 = (bf16[128,128]{1,0:T(8,128)(2,1)S(1)}, bf16[128,128]{1,0:T(8,128)(2,1)S(1)}, u32[]{:S(2)}, u32[]{:S(2)}) collective-permute-start(bf16[128,128]{1,0:T(8,128)(2,1)S(1)} %get-tuple-element.70.refs_0_), channel_id=1, source_target_pairs={{0,4},{4,0},{8,12},{12,8},{1,5},{5,1},{9,13},{13,9},{2,6},{6,2},{1... | collective-permute-start | bytes 98312 | tf_op jit(solution)/shard_map/ppermute | solution.py:237
  20.2 2.2 %shard_map.91 = (bf16[1280,128]{1,0:T(8,128)(2,1)S(1)}, f32[2,1280,128]{2,1,0:T(8,128)S(1)}, bf16[3,1280,128]{2,1,0:T(8,128)(2,1)S(1)}) custom-call(s32[1]{0:T(128)S(6)} %copy.9.count_ref, bf16[1536,128]{1,0:T(8,128)(2,1)S(1)} %get-tuple-element.62.q_ref, bf16[1536,128]{1,0:T(8,128)(2,1)S(1)} %get-tuple-element.56.k_ref, ...), custom_call_target="tpu_custom_call" | custom-call | flops 654311424 | bytes 5570564 | tf_op jit(solution)/shard_map/pallas_call | solution.py:183
  22.5 0.1 collective-permute-start.8
  22.5 0.0 collective-permute-done.7.refs_3_
  22.5 0.0 collective-permute-done.6.refs_2_
  22.6 0.0 collective-permute-done.5.refs_1_
  22.6 0.5 %collective-permute-start.9 = (f32[128,128]{1,0:T(8,128)S(1)}, f32[128,128]{1,0:T(8,128)S(1)}, u32[]{:S(2)}, u32[]{:S(2)}) collective-permute-start(f32[128,128]{1,0:T(8,128)S(1)} %shard_map.92.outside_ref), channel_id=1, source_target_pairs={{0,1},{1,0},{2,3},{3,2},{4,5},{5,4},{6,7},{7,6},{8,9},{9,8},{10,11... | collective-permute-start | bytes 196616 | tf_op jit(solution)/shard_map/ppermute | solution.py:269
  23.2 2.0 %collective-permute-done.9.outside_came_ref = f32[128,128]{1,0:T(8,128)S(1)} collective-permute-done((f32[128,128]{1,0:T(8,128)S(1)}, f32[128,128]{1,0:T(8,128)S(1)}, u32[]{:S(2)}, u32[]{:S(2)}) %collective-permute-start.9) | collective-permute-done | bytes 65568 | tf_op jit(solution)/shard_map/ppermute | solution.py:269
  25.2 0.0 collective-permute-done.8.came_ref
  25.2 1.5 %shard_map.93 = (bf16[1280,256]{1,0:T(8,128)(2,1)}, bf16[1280,256]{1,0:T(8,128)(2,1)}, bf16[1280,256]{1,0:T(8,128)(2,1)}) custom-call(s32[1]{0:T(128)S(6)} %copy.9.count_ref, bf16[1280,128]{1,0:T(8,128)(2,1)S(1)} %get-tuple-element.77.gq_own_ref, f32[2,1280,128]{2,1,0:T(8,128)S(1)} %get-tuple-element.78.own_ref, ...), custom_call_target="tpu_custom_call" | custom-call | flops 201326592 | bytes 6029316 | tf_op jit(solution)/shard_map/pallas_call | solution.py:183
  (2 shorter events, 0.1 us)
Async XLA Ops:
  1.7 2.7 %collective-permute-start = (bf16[2,1280,128]{2,1,0:T(8,128)(2,1)S(1)}, bf16[2,1280,128]{2,1,0:T(8,128)(2,1)S(1)}, u32[]{:S(2)}, u32[]{:S(2)}) collective-permute-start(bf16[2,1280,128]{2,1,0:T(8,128)(2,1)S(1)} %shard_map.85.give_ref), channel_id=1, source_target_pairs={{0,1},{1,0},{2,3},{3,2},{4,5},{5,4},{6,7},{7,6},{8,9},{9,8},{10,11... | collective-permute-start | bytes 1966088 | tf_op jit(solution)/shard_map/ppermute | solution.py:269
  4.5 6.3 %collective-permute-start.4 = (bf16[2,1280,128]{2,1,0:T(8,128)(2,1)S(1)}, bf16[2,1280,128]{2,1,0:T(8,128)(2,1)S(1)}, u32[]{:S(2)}, u32[]{:S(2)}) collective-permute-start(bf16[2,1280,128]{2,1,0:T(8,128)(2,1)S(1)} %get-tuple-element.55), channel_id=1, source_target_pairs={{0,1},{1,0},{2,3},{3,2},{4,5},{5,4},{6,7},{7,6},{8,9},{9,8},{10,11... | collective-permute-start | bytes 1966088 | tf_op jit(solution)/shard_map/ppermute | solution.py:269
  5.0 7.1 %collective-permute-start.3 = (bf16[128,128]{1,0:T(8,128)(2,1)S(1)}, bf16[128,128]{1,0:T(8,128)(2,1)S(1)}, u32[]{:S(2)}, u32[]{:S(2)}) collective-permute-start(bf16[128,128]{1,0:T(8,128)(2,1)S(1)} %get-tuple-element.52.refs_0_), channel_id=1, source_target_pairs={{0,12},{4,8},{8,4},{12,0},{1,13},{5,9},{9,5},{13,1},{2,14},{6,10},... | collective-permute-start | bytes 98312 | tf_op jit(solution)/shard_map/ppermute | solution.py:237
  10.1 4.8 %collective-permute-start.2 = (bf16[128,128]{1,0:T(8,128)(2,1)S(1)}, bf16[128,128]{1,0:T(8,128)(2,1)S(1)}, u32[]{:S(2)}, u32[]{:S(2)}) collective-permute-start(bf16[128,128]{1,0:T(8,128)(2,1)S(1)} %get-tuple-element.52.refs_0_), channel_id=1, source_target_pairs={{0,8},{4,12},{8,0},{12,4},{1,9},{5,13},{9,1},{13,5},{2,10},{6,14},... | collective-permute-start | bytes 98312 | tf_op jit(solution)/shard_map/ppermute | solution.py:237
  10.1 4.8 %collective-permute-start.1 = (bf16[128,128]{1,0:T(8,128)(2,1)S(1)}, bf16[128,128]{1,0:T(8,128)(2,1)S(1)}, u32[]{:S(2)}, u32[]{:S(2)}) collective-permute-start(bf16[128,128]{1,0:T(8,128)(2,1)S(1)} %get-tuple-element.52.refs_0_), channel_id=1, source_target_pairs={{0,4},{4,0},{8,12},{12,8},{1,5},{5,1},{9,13},{13,9},{2,6},{6,2},{1... | collective-permute-start | bytes 98312 | tf_op jit(solution)/shard_map/ppermute | solution.py:237
  15.8 6.8 %collective-permute-start.7 = (bf16[128,128]{1,0:T(8,128)(2,1)S(1)}, bf16[128,128]{1,0:T(8,128)(2,1)S(1)}, u32[]{:S(2)}, u32[]{:S(2)}) collective-permute-start(bf16[128,128]{1,0:T(8,128)(2,1)S(1)} %get-tuple-element.70.refs_0_), channel_id=1, source_target_pairs={{0,12},{4,8},{8,4},{12,0},{1,13},{5,9},{9,5},{13,1},{2,14},{6,10},... | collective-permute-start | bytes 98312 | tf_op jit(solution)/shard_map/ppermute | solution.py:237
  17.3 5.3 %collective-permute-start.6 = (bf16[128,128]{1,0:T(8,128)(2,1)S(1)}, bf16[128,128]{1,0:T(8,128)(2,1)S(1)}, u32[]{:S(2)}, u32[]{:S(2)}) collective-permute-start(bf16[128,128]{1,0:T(8,128)(2,1)S(1)} %get-tuple-element.70.refs_0_), channel_id=1, source_target_pairs={{0,8},{4,12},{8,0},{12,4},{1,9},{5,13},{9,1},{13,5},{2,10},{6,14},... | collective-permute-start | bytes 98312 | tf_op jit(solution)/shard_map/ppermute | solution.py:237
  17.9 4.6 %collective-permute-start.5 = (bf16[128,128]{1,0:T(8,128)(2,1)S(1)}, bf16[128,128]{1,0:T(8,128)(2,1)S(1)}, u32[]{:S(2)}, u32[]{:S(2)}) collective-permute-start(bf16[128,128]{1,0:T(8,128)(2,1)S(1)} %get-tuple-element.70.refs_0_), channel_id=1, source_target_pairs={{0,4},{4,0},{8,12},{12,8},{1,5},{5,1},{9,13},{13,9},{2,6},{6,2},{1... | collective-permute-start | bytes 98312 | tf_op jit(solution)/shard_map/ppermute | solution.py:237
  22.5 2.7 %collective-permute-start.8 = (bf16[3,1280,128]{2,1,0:T(8,128)(2,1)S(1)}, bf16[3,1280,128]{2,1,0:T(8,128)(2,1)S(1)}, u32[]{:S(2)}, u32[]{:S(2)}) collective-permute-start(bf16[3,1280,128]{2,1,0:T(8,128)(2,1)S(1)} %get-tuple-element.82), channel_id=1, source_target_pairs={{0,1},{1,0},{2,3},{3,2},{4,5},{5,4},{6,7},{7,6},{8,9},{9,8},{10,11... | collective-permute-start | bytes 2949128 | tf_op jit(solution)/shard_map/ppermute | solution.py:269
  22.6 2.6 %collective-permute-start.9 = (f32[128,128]{1,0:T(8,128)S(1)}, f32[128,128]{1,0:T(8,128)S(1)}, u32[]{:S(2)}, u32[]{:S(2)}) collective-permute-start(f32[128,128]{1,0:T(8,128)S(1)} %shard_map.92.outside_ref), channel_id=1, source_target_pairs={{0,1},{1,0},{2,3},{3,2},{4,5},{5,4},{6,7},{7,6},{8,9},{9,8},{10,11... | collective-permute-start | bytes 196616 | tf_op jit(solution)/shard_map/ppermute | solution.py:269

commit v7 on v5

--- a/solution.py
+++ b/solution.py
@@ -12,6 +12,7 @@
 SPAN = 256
 LIVE = 6
 EPSILON = 1e-06
+COVER = 10**10
 F32 = jnp.float32
 BF16 = jnp.bfloat16
 VMEM = pl.BlockSpec(memory_space=pltpu.VMEM)
@@ -140,7 +141,7 @@
 
 
 def pull_kernel(count_ref, q_ref, k_ref, v_ref, grad_ref, turned_ref, prefix_ref,
-                gq_own_ref, other_ref, gk_ref, gv_ref, gq_ref):
+                gq_own_ref, gq_other_ref, gk_ref, gv_ref, gq_ref):
     t = lax.broadcasted_iota(jnp.int32, (SPAN, SPAN), 0)
     s = lax.broadcasted_iota(jnp.int32, (SPAN, SPAN), 1)
     for at in range(LIVE):
@@ -151,12 +152,11 @@
         turned = jnp.where(t <= s, nt(v, grad), 0.0).astype(BF16)
         gk_ref[r, :] = nn(turned, q_ref[r, :])
         gv_ref[r, :] = nn(turned_ref[at], grad)
-    spread(gq_ref, gq_own_ref, other_ref.at[0], *core_and_counts(count_ref))
-
-
-def suffix_kernel(count_ref, k_ref, v_ref, gk_part_ref, gv_part_ref, back_ref, outside_ref, begun_ref,
+    spread(gq_ref, gq_own_ref, gq_other_ref, *core_and_counts(count_ref))
+
+
+def suffix_kernel(count_ref, k_ref, v_ref, gk_part_ref, gv_part_ref, back_ref, outside_ref,
                   gk_own_ref, gv_own_ref, other_ref, gk_ref, gv_ref):
-    del begun_ref
     outside = outside_ref[...]
     for at in range(LIVE):
         r = rows_of(at)
@@ -164,8 +164,8 @@
         gk_ref[r, :] = (gk_part_ref[r, :] + nt(v_ref[r, :], suffix)).astype(BF16)
         gv_ref[r, :] = (gv_part_ref[r, :] + nn(k_ref[r, :], suffix)).astype(BF16)
     where = core_and_counts(count_ref)
-    spread(gk_ref, gk_own_ref, other_ref.at[1], *where)
-    spread(gv_ref, gv_own_ref, other_ref.at[2], *where)
+    spread(gk_ref, gk_own_ref, other_ref.at[0], *where)
+    spread(gv_ref, gv_own_ref, other_ref.at[1], *where)
 
 
 def own_kernel(gq_own_ref, gk_own_ref, gv_own_ref, gq_hbm, gk_hbm, gv_hbm, sems):
@@ -173,10 +173,10 @@
     wait(fetch(((gq_own_ref, gq_hbm.at[:, c]), (gk_own_ref, gk_hbm.at[:, c]), (gv_own_ref, gv_hbm.at[:, c])), sems))
 
 
-def came_kernel(came_ref, gq_in_hbm, gk_in_hbm, gv_in_hbm, gq_hbm, gk_hbm, gv_hbm, sems):
+def came_kernel(gq_ref, came_ref, gq_in_hbm, gk_in_hbm, gv_in_hbm, gq_hbm, gk_hbm, gv_hbm, sems):
     del gq_in_hbm, gk_in_hbm, gv_in_hbm
     c = columns_of(1 - lax.axis_index("loader"))
-    wait(fetch([(came_ref.at[at], target.at[:, c]) for at, target in enumerate((gq_hbm, gk_hbm, gv_hbm))], sems))
+    wait(fetch(((gq_ref, gq_hbm.at[:, c]), (came_ref.at[0], gk_hbm.at[:, c]), (came_ref.at[1], gv_hbm.at[:, c])), sems))
 
 
 def call(kernel, ins, outs, flops, scratch=(), aliases={}):
@@ -242,7 +242,7 @@
         last = at + 1 == len(chain)
         kernel = functools.partial(combine_kernel, steps, radix, stride, reverse, at == 0, last)
         sums = [((total.shape, F32), VMEM)] + ([] if last else [((total.shape, total.dtype), VMEM)])
-        out = call(kernel, [(a, VMEM) for a in (group, *came, *outside)], sums, total.size)
+        out = call(kernel, [(a, VMEM) for a in (group, *came, *outside)], sums, COVER)
         outside, group = out[:1], out[-1]
         stride *= radix
     return outside[0], cover
@@ -286,18 +286,19 @@
     grad, prefix, back, own_back = call(
         norm_kernel, vmem(q, cot, gain, part, run, outside),
         [half, prefixes, states, total], 2 * unit)
-    three = ((3, rows, DH), BF16), VMEM
-    cover = call(
-        pull_kernel, count + vmem(q, k, v, grad, turned, prefix), [buffer, three, plane, plane], 11 * unit, [staged])
-    outside, (gq_own, other, gk_part, gv_part) = outside_sum(own_back, True, cover)
+    gq_own, gq_other, gk_part, gv_part = call(
+        pull_kernel, count + vmem(q, k, v, grad, turned, prefix), [buffer, buffer, plane, plane], 11 * unit, [staged])
+    gq_came = swap(gq_other)
+    outside, (gq_own, gk_part, gv_part) = outside_sum(own_back, True, (gq_own, gk_part, gv_part))
     gk_own, gv_own, other = call(
-        suffix_kernel, count + vmem(k, v, gk_part, gv_part, back, outside, other),
-        [buffer, buffer, three], 2 * unit, [staged, staged], {7: 2})
+        suffix_kernel, count + vmem(k, v, gk_part, gv_part, back, outside),
+        [buffer, buffer, pair], 2 * unit, [staged, staged])
     came = swap(other)
     grads = call(own_kernel, vmem(gq_own, gk_own, gv_own), [result] * 3, 0, [sems(3)])
     came, grads = lax.optimization_barrier((came, grads))
     return tuple(call(
-        came_kernel, vmem(came) + [(grad, HBM) for grad in grads], [result] * 3, 0, [sems(3)], {1: 0, 2: 1, 3: 2}))
+        came_kernel, vmem(gq_came, came) + [(grad, HBM) for grad in grads], [result] * 3, 0, [sems(3)],
+        {2: 0, 3: 1, 4: 2}))
 
 
 def solution(mesh):

time: 26.9 us -> 26.9 us (level)
  starting transfers between devices: 10.9 us -> 11.4 us
  waiting for transfers between devices: 4.9 us -> 4.42 us
    ppermute x3 -> x4, starting transfers between devices: 0.71 us -> 1.21 us  [swap(): return lax.ppermute(array, 'loader', SWAP)]
    ppermute x3 -> x4, waiting for transfers between devices: 1.58 us -> 1.09 us  [swap(): return lax.ppermute(array, 'loader', SWAP)]
  transfers between devices with their start and end apart: 9 -> 10, of which waited for: 4 -> 5; matrix products, arithmetic and copies ran while one was open for 0% -> 0% of each run, Pallas kernels for 22% -> 22%
where the time goes in v7:
time: 26.9 us; the launch traced here: 26.7 us
  starting transfers between devices  11.4 us (42%)
  Pallas kernels  9.49 us (35%)
  waiting for transfers between devices  4.42 us (16%)
  between operations  1.38 us (5%)
    ppermute x6, starting transfers between devices, outside_sum(): came.append(lax.ppermute(group, 'seq', pairs))  10.2 us
    pallas_call x11, Pallas kernels, call(): pl.pallas_call(kernel, out_shape=[pltpu.VMEM(*a) if space is VMEM else pl...  9.49 us
    ppermute x6, waiting for transfers between devices, outside_sum(): came.append(lax.ppermute(group, 'seq', pairs))  3.33 us
    ppermute x4, starting transfers between devices, swap(): return lax.ppermute(array, 'loader', SWAP)  1.21 us
    ppermute x4, waiting for transfers between devices, swap(): return lax.ppermute(array, 'loader', SWAP)  1.09 us
  transfers between devices with their start and end apart: 10, of which 5 were waited for; matrix products, arithmetic and copies ran while one was open for 0% of the time, Pallas kernels for 22%

profile of v7, /device:TPU:0, one launch (start us, length us, event | category | flops | bytes accessed | tf_op | source)
XLA Modules:
  0.0 26.7 jit_solution(13956070598942123535)
XLA Ops:
  0.6 1.1 %shard_map.85 = bf16[2,1280,128]{2,1,0:T(8,128)(2,1)S(1)} custom-call(bf16[1280,256]{1,0:T(8,128)(2,1)} %k_hbm.3, bf16[1280,256]{1,0:T(8,128)(2,1)} %v_hbm.3), custom_call_target="tpu_custom_call" | custom-call | bytes 1966080 | tf_op jit(solution)/shard_map/pallas_call | solution.py:185
  1.7 0.5 %collective-permute-start = (bf16[2,1280,128]{2,1,0:T(8,128)(2,1)S(1)}, bf16[2,1280,128]{2,1,0:T(8,128)(2,1)S(1)}, u32[]{:S(2)}, u32[]{:S(2)}) collective-permute-start(bf16[2,1280,128]{2,1,0:T(8,128)(2,1)S(1)} %shard_map.85), channel_id=1, source_target_pairs={{0,1},{1,0},{2,3},{3,2},{4,5},{5,4},{6,7},{7,6},{8,9},{9,8},{10,11... | collective-permute-start | bytes 1966088 | tf_op jit(solution)/shard_map/ppermute | solution.py:272
  2.9 1.5 %shard_map.86 = (bf16[1280,128]{1,0:T(8,128)(2,1)S(1)}, bf16[1280,128]{1,0:T(8,128)(2,1)S(1)}, bf16[1280,128]{1,0:T(8,128)(2,1)S(1)}, bf16[1280,128]{1,0:T(8,128...) custom-call(s32[1]{0:T(128)S(6)} %copy.15.count_ref, bf16[1280,256]{1,0:T(8,128)(2,1)} %k_hbm.3, ...), custom_call_target="tpu_custom_call" | custom-call | bytes 4589572 | tf_op jit(solution)/shard_map/pallas_call | solution.py:185
  4.5 0.0 collective-permute-done.other_ref
  4.5 0.1 collective-permute-start.4
  4.6 0.4 %shard_map.87 = (bf16[128,128]{1,0:T(8,128)(2,1)S(1)}, bf16[1536,128]{1,0:T(8,128)(2,1)S(1)}, bf16[1536,128]{1,0:T(8,128)(2,1)S(1)}, f32[6,128,128]{2,1,0:T(8,128)S(1)}) custom-call(s32[1]{0:T(128)S(6)} %copy.15.count_ref, bf16[1280,128]{1,0:T(8,128)(2,1)S(1)} %get-tuple-element.61.k_own_ref, bf16[1280,128]{1,0:T(8,128)(2,1)S(1)} %get-tuple-element.62.v_own_ref, ...), custom_call_target="tpu_custom_call" | custom-call | flops 50331648 | bytes 2523140 | tf_op jit(solution)/shard_map/pallas_call | solution.py:185
  5.0 5.1 %collective-permute-start.1 = (bf16[128,128]{1,0:T(8,128)(2,1)S(1)}, bf16[128,128]{1,0:T(8,128)(2,1)S(1)}, u32[]{:S(2)}, u32[]{:S(2)}) collective-permute-start(bf16[128,128]{1,0:T(8,128)(2,1)S(1)} %get-tuple-element.64.refs_0_), channel_id=1, source_target_pairs={{0,12},{4,8},{8,4},{12,0},{1,13},{5,9},{9,5},{13,1},{2,14},{6,10},... | collective-permute-start | bytes 98312 | tf_op jit(solution)/shard_map/ppermute | solution.py:239
  10.1 0.0 collective-permute-start.2
  10.1 0.6 %collective-permute-start.3 = (bf16[128,128]{1,0:T(8,128)(2,1)S(1)}, bf16[128,128]{1,0:T(8,128)(2,1)S(1)}, u32[]{:S(2)}, u32[]{:S(2)}) collective-permute-start(bf16[128,128]{1,0:T(8,128)(2,1)S(1)} %get-tuple-element.64.refs_0_), channel_id=1, source_target_pairs={{0,4},{4,0},{8,12},{12,8},{1,5},{5,1},{9,13},{13,9},{2,6},{6,2},{1... | collective-permute-start | bytes 98312 | tf_op jit(solution)/shard_map/ppermute | solution.py:239
  10.7 0.0 collective-permute-done.4.other_ref
  10.7 1.2 %shard_map.88 = (bf16[1536,128]{1,0:T(8,128)(2,1)S(1)}, bf16[1536,128]{1,0:T(8,128)(2,1)S(1)}, f32[1536,128]{1,0:T(8,128)S(1)}, bf16[6,256,256]{2,1,0:T(8,128)(2,1)S(1)}) custom-call(s32[1]{0:T(128)S(6)} %copy.15.count_ref, bf16[1280,128]{1,0:T(8,128)(2,1)S(1)} %get-tuple-element.65.q_own_ref, bf16[1280,128]{1,0:T(8,128)(2,1)S(1)} %get-tuple-element.66.cot_own_ref, ...), custom_call_target="tpu_custom_call" | custom-call | flops 301989888 | bytes 4456452 | tf_op jit(solution)/shard_map/pallas_call | solution.py:185
  12.0 0.0 collective-permute-done.1.refs_1_
  12.0 2.9 %collective-permute-done.2.refs_2_ = bf16[128,128]{1,0:T(8,128)(2,1)S(1)} collective-permute-done((bf16[128,128]{1,0:T(8,128)(2,1)S(1)}, bf16[128,128]{1,0:T(8,128)(2,1)S(1)}, u32[]{:S(2)}, u32[]{:S(2)}) %collective-permute-start.2) | collective-permute-done | bytes 32800 | tf_op jit(solution)/shard_map/ppermute | solution.py:239
  14.9 0.0 collective-permute-done.3.refs_3_
  14.9 0.8 %shard_map.90 = (bf16[1536,128]{1,0:T(8,128)(2,1)S(1)}, bf16[6,128,128]{2,1,0:T(8,128)(2,1)S(1)}, f32[6,128,128]{2,1,0:T(8,128)S(1)}, bf16[128,128]{1,0:T(8,128)(2,1)S(1)}) custom-call(bf16[1536,128]{1,0:T(8,128)(2,1)S(1)} %get-tuple-element.74.q_ref, bf16[1536,128]{1,0:T(8,128)(2,1)S(1)} %get-tuple-element.75.cot_ref, ...), custom_call_target="tpu_custom_call" | custom-call | flops 100663296 | bytes 3048448 | tf_op jit(solution)/shard_map/pallas_call | solution.py:185
  15.8 1.5 %collective-permute-start.6 = (bf16[128,128]{1,0:T(8,128)(2,1)S(1)}, bf16[128,128]{1,0:T(8,128)(2,1)S(1)}, u32[]{:S(2)}, u32[]{:S(2)}) collective-permute-start(bf16[128,128]{1,0:T(8,128)(2,1)S(1)} %get-tuple-element.86.refs_0_), channel_id=1, source_target_pairs={{0,12},{4,8},{8,4},{12,0},{1,13},{5,9},{9,5},{13,1},{2,14},{6,10},... | collective-permute-start | bytes 98312 | tf_op jit(solution)/shard_map/ppermute | solution.py:239
  17.3 0.6 %collective-permute-start.7 = (bf16[128,128]{1,0:T(8,128)(2,1)S(1)}, bf16[128,128]{1,0:T(8,128)(2,1)S(1)}, u32[]{:S(2)}, u32[]{:S(2)}) collective-permute-start(bf16[128,128]{1,0:T(8,128)(2,1)S(1)} %get-tuple-element.86.refs_0_), channel_id=1, source_target_pairs={{0,8},{4,12},{8,0},{12,4},{1,9},{5,13},{9,1},{13,5},{2,10},{6,14},... | collective-permute-start | bytes 98312 | tf_op jit(solution)/shard_map/ppermute | solution.py:239
  17.9 2.3 %collective-permute-start.8 = (bf16[128,128]{1,0:T(8,128)(2,1)S(1)}, bf16[128,128]{1,0:T(8,128)(2,1)S(1)}, u32[]{:S(2)}, u32[]{:S(2)}) collective-permute-start(bf16[128,128]{1,0:T(8,128)(2,1)S(1)} %get-tuple-element.86.refs_0_), channel_id=1, source_target_pairs={{0,4},{4,0},{8,12},{12,8},{1,5},{5,1},{9,13},{13,9},{2,6},{6,2},{1... | collective-permute-start | bytes 98312 | tf_op jit(solution)/shard_map/ppermute | solution.py:239
  20.2 1.8 %shard_map.91 = (bf16[1280,128]{1,0:T(8,128)(2,1)S(1)}, bf16[1280,128]{1,0:T(8,128)(2,1)S(1)}, f32[1536,128]{1,0:T(8,128)S(1)}, f32[1536,128]{1,0:T(8,128)S(1)}) custom-call(s32[1]{0:T(128)S(6)} %copy.15.count_ref, bf16[1536,128]{1,0:T(8,128)(2,1)S(1)} %get-tuple-element.74.q_ref, bf16[1536,128]{1,0:T(8,128)(2,1)S(1)} %get-tuple-element.68.k_ref, ...), custom_call_target="tpu_custom_call" | custom-call | flops 553648128 | bytes 4784132 | tf_op jit(solution)/shard_map/pallas_call | solution.py:185
  22.0 0.0 collective-permute-done.6.refs_1_
  22.0 0.1 collective-permute-done.7.refs_2_
  22.1 0.3 %collective-permute-done.8.refs_3_ = bf16[128,128]{1,0:T(8,128)(2,1)S(1)} collective-permute-done((bf16[128,128]{1,0:T(8,128)(2,1)S(1)}, bf16[128,128]{1,0:T(8,128)(2,1)S(1)}, u32[]{:S(2)}, u32[]{:S(2)}) %collective-permute-start.8) | collective-permute-done | bytes 32800 | tf_op jit(solution)/shard_map/ppermute | solution.py:239
  22.5 0.6 %shard_map.93 = (bf16[1280,128]{1,0:T(8,128)(2,1)S(1)}, bf16[1280,128]{1,0:T(8,128)(2,1)S(1)}, bf16[2,1280,128]{2,1,0:T(8,128)(2,1)S(1)}) custom-call(s32[1]{0:T(128)S(6)} %copy.15.count_ref, bf16[1536,128]{1,0:T(8,128)(2,1)S(1)} %get-tuple-element.68.k_ref, bf16[1536,128]{1,0:T(8,128)(2,1)S(1)} %get-tuple-element.69.v_ref, ...), custom_call_target="tpu_custom_call" | custom-call | flops 100663296 | bytes 4128772 | tf_op jit(solution)/shard_map/pallas_call | solution.py:185
  23.1 0.1 collective-permute-start.9
  23.2 0.5 %collective-permute-start.5 = (bf16[1280,128]{1,0:T(8,128)(2,1)S(1)}, bf16[1280,128]{1,0:T(8,128)(2,1)S(1)}, u32[]{:S(2)}, u32[]{:S(2)}) collective-permute-start(bf16[1280,128]{1,0:T(8,128)(2,1)S(1)} %get-tuple-element.85), channel_id=1, source_target_pairs={{0,1},{1,0},{2,3},{3,2},{4,5},{5,4},{6,7},{7,6},{8,9},{9,8},{10,11... | collective-permute-start | bytes 983048 | tf_op jit(solution)/shard_map/ppermute | solution.py:272
  23.7 1.0 %shard_map.94 = (bf16[1280,256]{1,0:T(8,128)(2,1)}, bf16[1280,256]{1,0:T(8,128)(2,1)}, bf16[1280,256]{1,0:T(8,128)(2,1)}) custom-call(bf16[1280,128]{1,0:T(8,128)(2,1)S(1)} %get-tuple-element.97.gq_own_ref, bf16[1280,128]{1,0:T(8,128)(2,1)S(1)} %get-tuple-element.98.gk_own_ref, bf16[1280,128]{1,0:T(8,128)(2,1)S(1)} %get-tuple-element.99.gv_own_ref), custom_call_target="tpu_custom_call" | custom-call | bytes 2949120 | tf_op jit(solution)/shard_map/pallas_call | solution.py:185
  24.7 0.6 %collective-permute-done.9.came_ref = bf16[2,1280,128]{2,1,0:T(8,128)(2,1)S(1)} collective-permute-done((bf16[2,1280,128]{2,1,0:T(8,128)(2,1)S(1)}, bf16[2,1280,128]{2,1,0:T(8,128)(2,1)S(1)}, u32[]{:S(2)}, u32[]{:S(2)}) %collective-permute-start.9) | collective-permute-done | bytes 655392 | tf_op jit(solution)/shard_map/ppermute | solution.py:272
  25.3 0.5 %collective-permute-done.5.gq_ref = bf16[1280,128]{1,0:T(8,128)(2,1)S(1)} collective-permute-done((bf16[1280,128]{1,0:T(8,128)(2,1)S(1)}, bf16[1280,128]{1,0:T(8,128)(2,1)S(1)}, u32[]{:S(2)}, u32[]{:S(2)}) %collective-permute-start.5) | collective-permute-done | bytes 327712 | tf_op jit(solution)/shard_map/ppermute | solution.py:272
  25.7 1.0 %shard_map.95 = (bf16[1280,256]{1,0:T(8,128)(2,1)}, bf16[1280,256]{1,0:T(8,128)(2,1)}, bf16[1280,256]{1,0:T(8,128)(2,1)}) custom-call(bf16[1280,128]{1,0:T(8,128)(2,1)S(1)} %collective-permute-done.5.gq_ref, bf16[2,1280,128]{2,1,0:T(8,128)(2,1)S(1)} %collective-permute-done.9.came_ref, ...), custom_call_target="tpu_custom_call", output_to_operand_aliasing={{0}: (2, {}), {1}: (3, {}), {2}: (4, {})} | custom-call | bytes 4915200 | tf_op jit(solution)/shard_map/pallas_call | solution.py:185
  (2 shorter events, 0.0 us)
Async XLA Ops:
  1.7 2.7 %collective-permute-start = (bf16[2,1280,128]{2,1,0:T(8,128)(2,1)S(1)}, bf16[2,1280,128]{2,1,0:T(8,128)(2,1)S(1)}, u32[]{:S(2)}, u32[]{:S(2)}) collective-permute-start(bf16[2,1280,128]{2,1,0:T(8,128)(2,1)S(1)} %shard_map.85), channel_id=1, source_target_pairs={{0,1},{1,0},{2,3},{3,2},{4,5},{5,4},{6,7},{7,6},{8,9},{9,8},{10,11... | collective-permute-start | bytes 1966088 | tf_op jit(solution)/shard_map/ppermute | solution.py:272
  4.5 6.3 %collective-permute-start.4 = (bf16[2,1280,128]{2,1,0:T(8,128)(2,1)S(1)}, bf16[2,1280,128]{2,1,0:T(8,128)(2,1)S(1)}, u32[]{:S(2)}, u32[]{:S(2)}) collective-permute-start(bf16[2,1280,128]{2,1,0:T(8,128)(2,1)S(1)} %get-tuple-element.67), channel_id=1, source_target_pairs={{0,1},{1,0},{2,3},{3,2},{4,5},{5,4},{6,7},{7,6},{8,9},{9,8},{10,11... | collective-permute-start | bytes 1966088 | tf_op jit(solution)/shard_map/ppermute | solution.py:272
  5.0 7.1 %collective-permute-start.1 = (bf16[128,128]{1,0:T(8,128)(2,1)S(1)}, bf16[128,128]{1,0:T(8,128)(2,1)S(1)}, u32[]{:S(2)}, u32[]{:S(2)}) collective-permute-start(bf16[128,128]{1,0:T(8,128)(2,1)S(1)} %get-tuple-element.64.refs_0_), channel_id=1, source_target_pairs={{0,12},{4,8},{8,4},{12,0},{1,13},{5,9},{9,5},{13,1},{2,14},{6,10},... | collective-permute-start | bytes 98312 | tf_op jit(solution)/shard_map/ppermute | solution.py:239
  10.1 4.8 %collective-permute-start.2 = (bf16[128,128]{1,0:T(8,128)(2,1)S(1)}, bf16[128,128]{1,0:T(8,128)(2,1)S(1)}, u32[]{:S(2)}, u32[]{:S(2)}) collective-permute-start(bf16[128,128]{1,0:T(8,128)(2,1)S(1)} %get-tuple-element.64.refs_0_), channel_id=1, source_target_pairs={{0,8},{4,12},{8,0},{12,4},{1,9},{5,13},{9,1},{13,5},{2,10},{6,14},... | collective-permute-start | bytes 98312 | tf_op jit(solution)/shard_map/ppermute | solution.py:239
  10.1 4.8 %collective-permute-start.3 = (bf16[128,128]{1,0:T(8,128)(2,1)S(1)}, bf16[128,128]{1,0:T(8,128)(2,1)S(1)}, u32[]{:S(2)}, u32[]{:S(2)}) collective-permute-start(bf16[128,128]{1,0:T(8,128)(2,1)S(1)} %get-tuple-element.64.refs_0_), channel_id=1, source_target_pairs={{0,4},{4,0},{8,12},{12,8},{1,5},{5,1},{9,13},{13,9},{2,6},{6,2},{1... | collective-permute-start | bytes 98312 | tf_op jit(solution)/shard_map/ppermute | solution.py:239
  15.8 6.3 %collective-permute-start.6 = (bf16[128,128]{1,0:T(8,128)(2,1)S(1)}, bf16[128,128]{1,0:T(8,128)(2,1)S(1)}, u32[]{:S(2)}, u32[]{:S(2)}) collective-permute-start(bf16[128,128]{1,0:T(8,128)(2,1)S(1)} %get-tuple-element.86.refs_0_), channel_id=1, source_target_pairs={{0,12},{4,8},{8,4},{12,0},{1,13},{5,9},{9,5},{13,1},{2,14},{6,10},... | collective-permute-start | bytes 98312 | tf_op jit(solution)/shard_map/ppermute | solution.py:239
  17.3 4.8 %collective-permute-start.7 = (bf16[128,128]{1,0:T(8,128)(2,1)S(1)}, bf16[128,128]{1,0:T(8,128)(2,1)S(1)}, u32[]{:S(2)}, u32[]{:S(2)}) collective-permute-start(bf16[128,128]{1,0:T(8,128)(2,1)S(1)} %get-tuple-element.86.refs_0_), channel_id=1, source_target_pairs={{0,8},{4,12},{8,0},{12,4},{1,9},{5,13},{9,1},{13,5},{2,10},{6,14},... | collective-permute-start | bytes 98312 | tf_op jit(solution)/shard_map/ppermute | solution.py:239
  17.9 4.5 %collective-permute-start.8 = (bf16[128,128]{1,0:T(8,128)(2,1)S(1)}, bf16[128,128]{1,0:T(8,128)(2,1)S(1)}, u32[]{:S(2)}, u32[]{:S(2)}) collective-permute-start(bf16[128,128]{1,0:T(8,128)(2,1)S(1)} %get-tuple-element.86.refs_0_), channel_id=1, source_target_pairs={{0,4},{4,0},{8,12},{12,8},{1,5},{5,1},{9,13},{13,9},{2,6},{6,2},{1... | collective-permute-start | bytes 98312 | tf_op jit(solution)/shard_map/ppermute | solution.py:239
  23.1 2.2 %collective-permute-start.9 = (bf16[2,1280,128]{2,1,0:T(8,128)(2,1)S(1)}, bf16[2,1280,128]{2,1,0:T(8,128)(2,1)S(1)}, u32[]{:S(2)}, u32[]{:S(2)}) collective-permute-start(bf16[2,1280,128]{2,1,0:T(8,128)(2,1)S(1)} %get-tuple-element.96), channel_id=1, source_target_pairs={{0,1},{1,0},{2,3},{3,2},{4,5},{5,4},{6,7},{7,6},{8,9},{9,8},{10,11... | collective-permute-start | bytes 1966088 | tf_op jit(solution)/shard_map/ppermute | solution.py:272
  23.2 2.6 %collective-permute-start.5 = (bf16[1280,128]{1,0:T(8,128)(2,1)S(1)}, bf16[1280,128]{1,0:T(8,128)(2,1)S(1)}, u32[]{:S(2)}, u32[]{:S(2)}) collective-permute-start(bf16[1280,128]{1,0:T(8,128)(2,1)S(1)} %get-tuple-element.85), channel_id=1, source_target_pairs={{0,1},{1,0},{2,3},{3,2},{4,5},{5,4},{6,7},{7,6},{8,9},{9,8},{10,11... | collective-permute-start | bytes 983048 | tf_op jit(solution)/shard_map/ppermute | solution.py:272

commit v8 on v5

--- a/solution.py
+++ b/solution.py
@@ -123,7 +123,7 @@
         inverse = lax.rsqrt(jnp.mean(raw * raw, axis=-1, keepdims=True) + EPSILON)
         weighted = gain * cot_ref[r, :].astype(F32)
         pulled = jnp.mean(weighted * raw, axis=-1, keepdims=True)
-        grad = (inverse * weighted - raw * (inverse * inverse * inverse * pulled)).astype(BF16)
+        grad = (inverse * (weighted - raw * (inverse * inverse * pulled))).astype(BF16)
         grad_ref[r, :] = grad
         back_ref[at] = running
         running = running + tn(q, grad)

time: 26.9 us -> 26.9 us (level)
  no operation moved by 1% of the time
where the time goes in v8:
time: 26.9 us; the launch traced here: 26.7 us
  starting transfers between devices  10.9 us (41%)
  Pallas kernels  9.51 us (35%)
  waiting for transfers between devices  4.9 us (18%)
  between operations  1.38 us (5%)
    ppermute x6, starting transfers between devices, outside_sum(): came.append(lax.ppermute(group, 'seq', pairs))  10.2 us
    pallas_call x11, Pallas kernels, call(): pl.pallas_call(kernel, out_shape=[pltpu.VMEM(*a) if space is VMEM else pl...  9.51 us
    ppermute x6, waiting for transfers between devices, outside_sum(): came.append(lax.ppermute(group, 'seq', pairs))  3.33 us
    ppermute x3, waiting for transfers between devices, swap(): return lax.ppermute(array, 'loader', SWAP)  1.58 us
    ppermute x3, starting transfers between devices, swap(): return lax.ppermute(array, 'loader', SWAP)  0.71 us
  transfers between devices with their start and end apart: 9, of which 4 were waited for; matrix products, arithmetic and copies ran while one was open for 0% of the time, Pallas kernels for 22%

profile of v8, /device:TPU:0, one launch (start us, length us, event | category | flops | bytes accessed | tf_op | source)
XLA Modules:
  0.0 26.7 jit_solution(11872302475625167026)
XLA Ops:
  0.6 1.1 %shard_map.85 = bf16[2,1280,128]{2,1,0:T(8,128)(2,1)S(1)} custom-call(bf16[1280,256]{1,0:T(8,128)(2,1)} %k_hbm.3, bf16[1280,256]{1,0:T(8,128)(2,1)} %v_hbm.3), custom_call_target="tpu_custom_call" | custom-call | bytes 1966080 | tf_op jit(solution)/shard_map/pallas_call | solution.py:185
  1.7 0.5 %collective-permute-start = (bf16[2,1280,128]{2,1,0:T(8,128)(2,1)S(1)}, bf16[2,1280,128]{2,1,0:T(8,128)(2,1)S(1)}, u32[]{:S(2)}, u32[]{:S(2)}) collective-permute-start(bf16[2,1280,128]{2,1,0:T(8,128)(2,1)S(1)} %shard_map.85), channel_id=1, source_target_pairs={{0,1},{1,0},{2,3},{3,2},{4,5},{5,4},{6,7},{7,6},{8,9},{9,8},{10,11... | collective-permute-start | bytes 1966088 | tf_op jit(solution)/shard_map/ppermute | solution.py:272
  2.9 1.5 %shard_map.86 = (bf16[1280,128]{1,0:T(8,128)(2,1)S(1)}, bf16[1280,128]{1,0:T(8,128)(2,1)S(1)}, bf16[1280,128]{1,0:T(8,128)(2,1)S(1)}, bf16[1280,128]{1,0:T(8,128...) custom-call(s32[1]{0:T(128)S(6)} %copy.17.count_ref, bf16[1280,256]{1,0:T(8,128)(2,1)} %k_hbm.3, ...), custom_call_target="tpu_custom_call" | custom-call | bytes 4589572 | tf_op jit(solution)/shard_map/pallas_call | solution.py:185
  4.5 0.0 collective-permute-done.other_ref
  4.5 0.1 collective-permute-start.4
  4.6 0.4 %shard_map.87 = (bf16[128,128]{1,0:T(8,128)(2,1)S(1)}, bf16[1536,128]{1,0:T(8,128)(2,1)S(1)}, bf16[1536,128]{1,0:T(8,128)(2,1)S(1)}, f32[6,128,128]{2,1,0:T(8,128)S(1)}) custom-call(s32[1]{0:T(128)S(6)} %copy.17.count_ref, bf16[1280,128]{1,0:T(8,128)(2,1)S(1)} %get-tuple-element.62.k_own_ref, bf16[1280,128]{1,0:T(8,128)(2,1)S(1)} %get-tuple-element.63.v_own_ref, ...), custom_call_target="tpu_custom_call" | custom-call | flops 50331648 | bytes 2523140 | tf_op jit(solution)/shard_map/pallas_call | solution.py:185
  5.0 5.1 %collective-permute-start.1 = (bf16[128,128]{1,0:T(8,128)(2,1)S(1)}, bf16[128,128]{1,0:T(8,128)(2,1)S(1)}, u32[]{:S(2)}, u32[]{:S(2)}) collective-permute-start(bf16[128,128]{1,0:T(8,128)(2,1)S(1)} %get-tuple-element.67.refs_0_), channel_id=1, source_target_pairs={{0,12},{4,8},{8,4},{12,0},{1,13},{5,9},{9,5},{13,1},{2,14},{6,10},... | collective-permute-start | bytes 98312 | tf_op jit(solution)/shard_map/ppermute | solution.py:239
  10.1 0.0 collective-permute-start.2
  10.1 0.6 %collective-permute-start.3 = (bf16[128,128]{1,0:T(8,128)(2,1)S(1)}, bf16[128,128]{1,0:T(8,128)(2,1)S(1)}, u32[]{:S(2)}, u32[]{:S(2)}) collective-permute-start(bf16[128,128]{1,0:T(8,128)(2,1)S(1)} %get-tuple-element.67.refs_0_), channel_id=1, source_target_pairs={{0,4},{4,0},{8,12},{12,8},{1,5},{5,1},{9,13},{13,9},{2,6},{6,2},{1... | collective-permute-start | bytes 98312 | tf_op jit(solution)/shard_map/ppermute | solution.py:239
  10.7 0.0 collective-permute-done.4.other_ref
  10.7 1.2 %shard_map.88 = (bf16[1536,128]{1,0:T(8,128)(2,1)S(1)}, bf16[1536,128]{1,0:T(8,128)(2,1)S(1)}, f32[1536,128]{1,0:T(8,128)S(1)}, bf16[6,256,256]{2,1,0:T(8,128)(2,1)S(1)}) custom-call(s32[1]{0:T(128)S(6)} %copy.17.count_ref, bf16[1280,128]{1,0:T(8,128)(2,1)S(1)} %get-tuple-element.68.q_own_ref, bf16[1280,128]{1,0:T(8,128)(2,1)S(1)} %get-tuple-element.69.cot_own_ref, ...), custom_call_target="tpu_custom_call" | custom-call | flops 301989888 | bytes 4456452 | tf_op jit(solution)/shard_map/pallas_call | solution.py:185
  12.0 0.0 collective-permute-done.1.refs_1_
  12.0 2.9 %collective-permute-done.2.refs_2_ = bf16[128,128]{1,0:T(8,128)(2,1)S(1)} collective-permute-done((bf16[128,128]{1,0:T(8,128)(2,1)S(1)}, bf16[128,128]{1,0:T(8,128)(2,1)S(1)}, u32[]{:S(2)}, u32[]{:S(2)}) %collective-permute-start.2) | collective-permute-done | bytes 32800 | tf_op jit(solution)/shard_map/ppermute | solution.py:239
  14.9 0.0 collective-permute-done.3.refs_3_
  14.9 0.8 %shard_map.90 = (bf16[1536,128]{1,0:T(8,128)(2,1)S(1)}, bf16[6,128,128]{2,1,0:T(8,128)(2,1)S(1)}, f32[6,128,128]{2,1,0:T(8,128)S(1)}, bf16[128,128]{1,0:T(8,128)(2,1)S(1)}) custom-call(bf16[1536,128]{1,0:T(8,128)(2,1)S(1)} %get-tuple-element.75.q_ref, bf16[1536,128]{1,0:T(8,128)(2,1)S(1)} %get-tuple-element.76.cot_ref, ...), custom_call_target="tpu_custom_call" | custom-call | flops 100663296 | bytes 3048448 | tf_op jit(solution)/shard_map/pallas_call | solution.py:185
  15.8 1.5 %collective-permute-start.5 = (bf16[128,128]{1,0:T(8,128)(2,1)S(1)}, bf16[128,128]{1,0:T(8,128)(2,1)S(1)}, u32[]{:S(2)}, u32[]{:S(2)}) collective-permute-start(bf16[128,128]{1,0:T(8,128)(2,1)S(1)} %get-tuple-element.83.refs_0_), channel_id=1, source_target_pairs={{0,12},{4,8},{8,4},{12,0},{1,13},{5,9},{9,5},{13,1},{2,14},{6,10},... | collective-permute-start | bytes 98312 | tf_op jit(solution)/shard_map/ppermute | solution.py:239
  17.3 0.6 %collective-permute-start.6 = (bf16[128,128]{1,0:T(8,128)(2,1)S(1)}, bf16[128,128]{1,0:T(8,128)(2,1)S(1)}, u32[]{:S(2)}, u32[]{:S(2)}) collective-permute-start(bf16[128,128]{1,0:T(8,128)(2,1)S(1)} %get-tuple-element.83.refs_0_), channel_id=1, source_target_pairs={{0,8},{4,12},{8,0},{12,4},{1,9},{5,13},{9,1},{13,5},{2,10},{6,14},... | collective-permute-start | bytes 98312 | tf_op jit(solution)/shard_map/ppermute | solution.py:239
  17.9 2.3 %collective-permute-start.7 = (bf16[128,128]{1,0:T(8,128)(2,1)S(1)}, bf16[128,128]{1,0:T(8,128)(2,1)S(1)}, u32[]{:S(2)}, u32[]{:S(2)}) collective-permute-start(bf16[128,128]{1,0:T(8,128)(2,1)S(1)} %get-tuple-element.83.refs_0_), channel_id=1, source_target_pairs={{0,4},{4,0},{8,12},{12,8},{1,5},{5,1},{9,13},{13,9},{2,6},{6,2},{1... | collective-permute-start | bytes 98312 | tf_op jit(solution)/shard_map/ppermute | solution.py:239
  20.2 1.8 %shard_map.91 = (bf16[1280,128]{1,0:T(8,128)(2,1)S(1)}, bf16[3,1280,128]{2,1,0:T(8,128)(2,1)S(1)}, f32[1536,128]{1,0:T(8,128)S(1)}, f32[1536,128]{1,0:T(8,128)S(1)}) custom-call(s32[1]{0:T(128)S(6)} %copy.17.count_ref, bf16[1536,128]{1,0:T(8,128)(2,1)S(1)} %get-tuple-element.75.q_ref, bf16[1536,128]{1,0:T(8,128)(2,1)S(1)} %get-tuple-element.65.k_ref, ...), custom_call_target="tpu_custom_call" | custom-call | flops 553648128 | bytes 5439492 | tf_op jit(solution)/shard_map/pallas_call | solution.py:185
  22.0 0.0 collective-permute-done.5.refs_1_
  22.0 0.1 collective-permute-done.6.refs_2_
  22.1 0.3 %collective-permute-done.7.refs_3_ = bf16[128,128]{1,0:T(8,128)(2,1)S(1)} collective-permute-done((bf16[128,128]{1,0:T(8,128)(2,1)S(1)}, bf16[128,128]{1,0:T(8,128)(2,1)S(1)}, u32[]{:S(2)}, u32[]{:S(2)}) %collective-permute-start.7) | collective-permute-done | bytes 32800 | tf_op jit(solution)/shard_map/ppermute | solution.py:239
  22.5 0.6 %shard_map.93 = (bf16[1280,128]{1,0:T(8,128)(2,1)S(1)}, bf16[1280,128]{1,0:T(8,128)(2,1)S(1)}, bf16[3,1280,128]{2,1,0:T(8,128)(2,1)S(1)}) custom-call(s32[1]{0:T(128)S(6)} %copy.17.count_ref, bf16[1536,128]{1,0:T(8,128)(2,1)S(1)} %get-tuple-element.65.k_ref, bf16[1536,128]{1,0:T(8,128)(2,1)S(1)} %get-tuple-element.66.v_ref, ...), custom_call_target="tpu_custom_call", output_to_operand_aliasing={{2}: (7, {})} | custom-call | flops 100663296 | bytes 5439492 | tf_op jit(solution)/shard_map/pallas_call | solution.py:185
  23.1 0.1 collective-permute-start.8
  23.2 1.0 %shard_map.94 = (bf16[1280,256]{1,0:T(8,128)(2,1)}, bf16[1280,256]{1,0:T(8,128)(2,1)}, bf16[1280,256]{1,0:T(8,128)(2,1)}) custom-call(bf16[1280,128]{1,0:T(8,128)(2,1)S(1)} %get-tuple-element.99.gq_own_ref, bf16[1280,128]{1,0:T(8,128)(2,1)S(1)} %get-tuple-element.100.gk_own_ref, bf16[1280,128]{1,0:T(8,128)(2,1)S(1)} %get-tuple-element.101.gv_own_ref), custom_call_target="tpu_custom_call" | custom-call | bytes 2949120 | tf_op jit(solution)/shard_map/pallas_call | solution.py:185
  24.2 1.6 %collective-permute-done.8.came_ref = bf16[3,1280,128]{2,1,0:T(8,128)(2,1)S(1)} collective-permute-done((bf16[3,1280,128]{2,1,0:T(8,128)(2,1)S(1)}, bf16[3,1280,128]{2,1,0:T(8,128)(2,1)S(1)}, u32[]{:S(2)}, u32[]{:S(2)}) %collective-permute-start.8) | collective-permute-done | bytes 983072 | tf_op jit(solution)/shard_map/ppermute | solution.py:272
  25.7 1.0 %shard_map.95 = (bf16[1280,256]{1,0:T(8,128)(2,1)}, bf16[1280,256]{1,0:T(8,128)(2,1)}, bf16[1280,256]{1,0:T(8,128)(2,1)}) custom-call(bf16[3,1280,128]{2,1,0:T(8,128)(2,1)S(1)} %collective-permute-done.8.came_ref, bf16[1280,256]{1,0:T(8,128)(2,1)} %get-tuple-element.106.gq_in_hbm, ...), custom_call_target="tpu_custom_call", output_to_operand_aliasing={{0}: (1, {}), {1}: (2, {}), {2}: (3, {})} | custom-call | bytes 4915200 | tf_op jit(solution)/shard_map/pallas_call | solution.py:185
  (2 shorter events, 0.0 us)
Async XLA Ops:
  1.7 2.7 %collective-permute-start = (bf16[2,1280,128]{2,1,0:T(8,128)(2,1)S(1)}, bf16[2,1280,128]{2,1,0:T(8,128)(2,1)S(1)}, u32[]{:S(2)}, u32[]{:S(2)}) collective-permute-start(bf16[2,1280,128]{2,1,0:T(8,128)(2,1)S(1)} %shard_map.85), channel_id=1, source_target_pairs={{0,1},{1,0},{2,3},{3,2},{4,5},{5,4},{6,7},{7,6},{8,9},{9,8},{10,11... | collective-permute-start | bytes 1966088 | tf_op jit(solution)/shard_map/ppermute | solution.py:272
  4.5 6.3 %collective-permute-start.4 = (bf16[2,1280,128]{2,1,0:T(8,128)(2,1)S(1)}, bf16[2,1280,128]{2,1,0:T(8,128)(2,1)S(1)}, u32[]{:S(2)}, u32[]{:S(2)}) collective-permute-start(bf16[2,1280,128]{2,1,0:T(8,128)(2,1)S(1)} %get-tuple-element.70), channel_id=1, source_target_pairs={{0,1},{1,0},{2,3},{3,2},{4,5},{5,4},{6,7},{7,6},{8,9},{9,8},{10,11... | collective-permute-start | bytes 1966088 | tf_op jit(solution)/shard_map/ppermute | solution.py:272
  5.0 7.1 %collective-permute-start.1 = (bf16[128,128]{1,0:T(8,128)(2,1)S(1)}, bf16[128,128]{1,0:T(8,128)(2,1)S(1)}, u32[]{:S(2)}, u32[]{:S(2)}) collective-permute-start(bf16[128,128]{1,0:T(8,128)(2,1)S(1)} %get-tuple-element.67.refs_0_), channel_id=1, source_target_pairs={{0,12},{4,8},{8,4},{12,0},{1,13},{5,9},{9,5},{13,1},{2,14},{6,10},... | collective-permute-start | bytes 98312 | tf_op jit(solution)/shard_map/ppermute | solution.py:239
  10.1 4.8 %collective-permute-start.2 = (bf16[128,128]{1,0:T(8,128)(2,1)S(1)}, bf16[128,128]{1,0:T(8,128)(2,1)S(1)}, u32[]{:S(2)}, u32[]{:S(2)}) collective-permute-start(bf16[128,128]{1,0:T(8,128)(2,1)S(1)} %get-tuple-element.67.refs_0_), channel_id=1, source_target_pairs={{0,8},{4,12},{8,0},{12,4},{1,9},{5,13},{9,1},{13,5},{2,10},{6,14},... | collective-permute-start | bytes 98312 | tf_op jit(solution)/shard_map/ppermute | solution.py:239
  10.1 4.8 %collective-permute-start.3 = (bf16[128,128]{1,0:T(8,128)(2,1)S(1)}, bf16[128,128]{1,0:T(8,128)(2,1)S(1)}, u32[]{:S(2)}, u32[]{:S(2)}) collective-permute-start(bf16[128,128]{1,0:T(8,128)(2,1)S(1)} %get-tuple-element.67.refs_0_), channel_id=1, source_target_pairs={{0,4},{4,0},{8,12},{12,8},{1,5},{5,1},{9,13},{13,9},{2,6},{6,2},{1... | collective-permute-start | bytes 98312 | tf_op jit(solution)/shard_map/ppermute | solution.py:239
  15.8 6.3 %collective-permute-start.5 = (bf16[128,128]{1,0:T(8,128)(2,1)S(1)}, bf16[128,128]{1,0:T(8,128)(2,1)S(1)}, u32[]{:S(2)}, u32[]{:S(2)}) collective-permute-start(bf16[128,128]{1,0:T(8,128)(2,1)S(1)} %get-tuple-element.83.refs_0_), channel_id=1, source_target_pairs={{0,12},{4,8},{8,4},{12,0},{1,13},{5,9},{9,5},{13,1},{2,14},{6,10},... | collective-permute-start | bytes 98312 | tf_op jit(solution)/shard_map/ppermute | solution.py:239
  17.3 4.8 %collective-permute-start.6 = (bf16[128,128]{1,0:T(8,128)(2,1)S(1)}, bf16[128,128]{1,0:T(8,128)(2,1)S(1)}, u32[]{:S(2)}, u32[]{:S(2)}) collective-permute-start(bf16[128,128]{1,0:T(8,128)(2,1)S(1)} %get-tuple-element.83.refs_0_), channel_id=1, source_target_pairs={{0,8},{4,12},{8,0},{12,4},{1,9},{5,13},{9,1},{13,5},{2,10},{6,14},... | collective-permute-start | bytes 98312 | tf_op jit(solution)/shard_map/ppermute | solution.py:239
  17.9 4.5 %collective-permute-start.7 = (bf16[128,128]{1,0:T(8,128)(2,1)S(1)}, bf16[128,128]{1,0:T(8,128)(2,1)S(1)}, u32[]{:S(2)}, u32[]{:S(2)}) collective-permute-start(bf16[128,128]{1,0:T(8,128)(2,1)S(1)} %get-tuple-element.83.refs_0_), channel_id=1, source_target_pairs={{0,4},{4,0},{8,12},{12,8},{1,5},{5,1},{9,13},{13,9},{2,6},{6,2},{1... | collective-permute-start | bytes 98312 | tf_op jit(solution)/shard_map/ppermute | solution.py:239
  23.1 2.6 %collective-permute-start.8 = (bf16[3,1280,128]{2,1,0:T(8,128)(2,1)S(1)}, bf16[3,1280,128]{2,1,0:T(8,128)(2,1)S(1)}, u32[]{:S(2)}, u32[]{:S(2)}) collective-permute-start(bf16[3,1280,128]{2,1,0:T(8,128)(2,1)S(1)} %get-tuple-element.98), channel_id=1, source_target_pairs={{0,1},{1,0},{2,3},{3,2},{4,5},{5,4},{6,7},{7,6},{8,9},{9,8},{10,11... | collective-permute-start | bytes 2949128 | tf_op jit(solution)/shard_map/ppermute | solution.py:272
